TPU v7x, 256 devices: a whole 4x4x8 slice. The times are simulated.
256 devices in a mesh: section: 8 (over z_hi, x), rep: 32 (over z_lo, y, core).
Axes of the slice: x: 4, y: 4, z: 8 (z_hi: 2, z_lo: 4; z = z_hi * 4 + z_lo), core: 2. Of those that a mesh axis runs over, the one named last changes fastest.
Arguments:
- layer_in: bfloat16 [8, 128, 4096], P('section', 'rep'), may hold values from -6 to 6
- next_in: bfloat16 [8, 128, 4096], P('section', 'rep'), may hold values from -6 to 6
- returned: bfloat16 [8, 256, 4096], P('section', 'rep'), may hold values from -6 to 6
- norm_gain: float32 [8, 4096], P('section'), may hold values from 0.25 to 1.75
- gate_weight: bfloat16 [8, 4096, 14336], P('section', None, 'rep'), may hold values from -0.09375 to 0.09375
- up_weight: bfloat16 [8, 4096, 14336], P('section', None, 'rep'), may hold values from -0.09375 to 0.09375
- down_weight: bfloat16 [8, 14336, 4096], P('section', 'rep'), may hold values from -0.046875 to 0.046875
- wiring: int32 [8, 32, 32], P('section'), may hold values from 0 to 2, as said below
Outputs:
- forwarded: bfloat16 [8, 256, 4096], P('section', 'rep')
- input_grad: bfloat16 [8, 128, 4096], P('section', 'rep')
- next_out: bfloat16 [8, 128, 4096], P('section', 'rep')
Inputs may be any that keep to these rules, and one draw needn't show every extreme that they name: For every position p and row group r the entries wiring[p, r, :] sum to 2. For every position p and receiver j the column wiring[p, :, j] sums to at most 4, and in every position some column sums to exactly 4. In every position some row group sends all its 2 blocks to one receiver, and some receiver gets none.
All inputs are finite; a program needn't handle non-finite values.
Results may differ from a plain program's by a relative error of at most 0.035.
Values may be sent and summed in bfloat16 or wider, within the bound.
No kernel may reach another device: no remote copies, remote signals or barrier semaphores. Data moves between devices by JAX's collectives and lax.ppermute only.
A program may use at most 128 MiB of HBM per device.

v0:
```python
import functools

import jax
import jax.numpy as jnp
from jax import lax
from jax.experimental import pallas as pl
from jax.experimental.pallas import tpu as pltpu
from jax.sharding import PartitionSpec as P

BLK = 2
NZ = 4
NY = 4
NC = 2

epsilon = 1e-05
step_rate = 0.5

F32 = jnp.float32
BF16 = jnp.bfloat16
WIDTH = 1024
VMEM_LIMIT = 18 << 20


def send(value, ds=0, dz=0, dy=0, dc=0):
    sections = lax.axis_size("section")
    replicas = lax.axis_size("rep")
    pairs = []
    for s in range(sections):
        for z in range(NZ):
            for y in range(NY):
                for c in range(NC):
                    source = s * replicas + (z * NY + y) * NC + c
                    target = (
                        ((s + ds) % sections) * replicas
                        + (((z + dz) % NZ) * NY + (y + dy) % NY) * NC
                        + (c + dc) % NC
                    )
                    pairs.append((source, target))
    return lax.ppermute(value, ("section", "rep"), pairs)


def group_at(index):
    me = lax.axis_index("rep")
    z, y, c = me // (NY * NC), (me // NC) % NY, me % NC
    dz, dy, dc = index % NZ, (index // NZ) % NY, index // (NZ * NY)
    return (((z + dz) % NZ) * NY + (y + dy) % NY) * NC + (c + dc) % NC


def selection(wiring, blocks_dev, capacity):
    groups = wiring.shape[0]
    per_group = blocks_dev * BLK
    per_slots = capacity * BLK
    per_unit = per_slots + per_group
    rows, columns = groups * per_group, groups * per_unit
    counts = wiring.astype(BF16)
    row_id = lax.broadcasted_iota(jnp.int32, (rows, groups), 0)
    row_member = lax.broadcasted_iota(jnp.int32, (rows, groups), 1)
    row_group = group_at(row_id // per_group)
    left = jnp.concatenate(
        [(row_member == row_group).astype(BF16), (row_member < row_group).astype(BF16)], axis=0
    )
    column_id = lax.broadcasted_iota(jnp.int32, (groups, columns), 1)
    column_member = lax.broadcasted_iota(jnp.int32, (groups, columns), 0)
    column_group = group_at(column_id // per_unit)
    right = jnp.concatenate(
        [(column_member == column_group).astype(BF16), (column_member < column_group).astype(BF16)],
        axis=1,
    )
    half = jnp.dot(left, counts, preferred_element_type=F32).astype(BF16)
    table = jnp.dot(half, right, preferred_element_type=F32).astype(jnp.int32)
    count = table[:rows, :columns]
    row_start = table[:rows, columns:]
    column_start = table[rows:, :columns]
    r = lax.broadcasted_iota(jnp.int32, (rows, columns), 0)
    q = lax.broadcasted_iota(jnp.int32, (rows, columns), 1)
    inner = q % per_unit
    block = (r % per_group) // BLK
    offset = block - row_start
    hit = (offset >= 0) & (offset < count) & (inner // BLK == column_start + offset)
    hit = hit & (inner < per_slots) & (r % BLK == inner % BLK)
    plain = (q // per_unit == r // per_group) & (inner == per_slots + r % per_group)
    chosen = jnp.concatenate([hit.astype(BF16), plain.astype(BF16)], axis=0)
    return lax.optimization_barrier(chosen)


def normalize(layer_rows, gain_row):
    values = layer_rows.astype(F32)
    row_scale = lax.rsqrt(jnp.mean(values * values, axis=1, keepdims=True) + epsilon)
    return values, row_scale, (values * row_scale * gain_row[None, :]).astype(BF16)


def dot(a, b, ca=1, cb=0):
    return lax.dot_general(a, b, (((ca,), (cb,)), ((), ())), preferred_element_type=F32)


def after(value, *others):
    return lax.optimization_barrier((value, *others))[0]


def add_up(parts):
    total = parts[0].astype(F32)
    for part in parts[1:]:
        total = total + part.astype(F32)
    return total


def cut(value, count):
    size = value.shape[0] // count
    return [value[i * size : (i + 1) * size] for i in range(count)]


def core_sum(terms):
    mine, other = cut(terms, NC)
    return add_up([mine, send(other, dc=1)]).astype(BF16)


def y_sum(terms):
    parts = cut(terms, NY)
    return add_up(
        [parts[0]] + [send(parts[k], dy=k) for k in range(1, NY)]
    ).astype(BF16)


def dot_t(a, b):
    return dot(a, b, 1, 1)


def first_kernel(count, factor, *refs):
    select = refs[0]
    blocks, nexts = refs[1 : 1 + count], refs[1 + count : 1 + 2 * count]
    gate_w, up_w, down_w = refs[1 + 2 * count : 4 + 2 * count]
    cot_out, hidden_out, dgate_out, dup_out, gate_out, up_out, gate_sent, up_sent = refs[
        4 + 2 * count : 12 + 2 * count
    ]
    gate_sum, up_sum, dhidden_sum, inner_sum = refs[12 + 2 * count :]
    step = pl.program_id(0)
    tokens = dhidden_sum.shape[0]
    chosen = dot(select[...], jnp.concatenate([r[...] for r in blocks], axis=0)).astype(BF16)
    cotangent, normed = chosen[:tokens], chosen[tokens:]
    cot_out[...] = cotangent
    ahead = jnp.concatenate([r[...] for r in nexts], axis=0)
    rows = jnp.concatenate([normed, ahead], axis=0)
    gate = dot_t(rows, gate_w[...])
    up = dot_t(rows, up_w[...])
    dhidden = dot_t(cotangent, down_w[...])
    inner = dot_t(ahead, normed)

    @pl.when(step == 0)
    def _():
        gate_sum[...] = gate
        up_sum[...] = up
        dhidden_sum[...] = dhidden
        inner_sum[...] = inner

    @pl.when(step > 0)
    def _():
        gate_sum[...] += gate
        up_sum[...] += up
        dhidden_sum[...] += dhidden
        inner_sum[...] += inner

    @pl.when(step == pl.num_programs(0) - 1)
    def _():
        gate_act, up_act = gate_sum[:tokens], up_sum[:tokens]
        sigmoid_gate = jax.nn.sigmoid(gate_act)
        silu_gate = gate_act * sigmoid_gate
        grad = dhidden_sum[...]
        hidden_out[...] = (silu_gate * up_act).astype(BF16)
        dgate = (
            grad * up_act * sigmoid_gate * (1.0 + gate_act * (1.0 - sigmoid_gate))
        ).astype(BF16)
        dup = (grad * silu_gate).astype(BF16)
        dgate_out[...] = dgate
        dup_out[...] = dup
        overlap = (-factor * inner_sum[...]).astype(BF16)
        gate_next = gate_sum[tokens:] + dot(overlap, dgate)
        up_next = up_sum[tokens:] + dot(overlap, dup)
        gate_out[...] = gate_next
        up_out[...] = up_next
        gate_sent[...] = gate_next.astype(BF16)
        up_sent[...] = up_next.astype(BF16)


def second_kernel(
    spread, hidden, dgate, dup, own_rows, gate_w, up_w, down_w, out
):
    top = own_rows.shape[0]
    term = dot(hidden[...], down_w[...])
    term = jnp.concatenate([term[:top] + own_rows[...], term[top:]], axis=0)
    dterm = dot(dgate[...], gate_w[...]) + dot(dup[...], up_w[...])
    both = jnp.concatenate([term.astype(BF16), dterm.astype(BF16)], axis=0)
    out[...] = dot(spread[...], both).astype(BF16)


def third_kernel(
    factor, row_count, gate, up, mate_gate, mate_up, hidden, cotangent, down_w, out, hidden_next, overlap
):
    @pl.when(pl.program_id(0) == 0)
    def _():
        gate_next = 0.5 * (gate[...] + mate_gate[...].astype(F32))
        up_next = 0.5 * (up[...] + mate_up[...].astype(F32))
        units = (gate_next * jax.nn.sigmoid(gate_next) * up_next).astype(BF16)
        rows = units.shape[0]
        to = lax.broadcasted_iota(jnp.int32, (rows, rows), 0)
        at = lax.broadcasted_iota(jnp.int32, (rows, rows), 1)
        i, j = to & (row_count - 1), to // row_count
        z, replica, y, core = j & (NZ - 1), (j // NZ) & 1, (j // (2 * NZ)) & (NY - 1), j // (2 * NZ * NY)
        source = (((core * NZ + z) * NY + y) * 2 + replica) * row_count + i
        order = jnp.where(at == source, 1.0, 0.0).astype(BF16)
        units = dot(order, units).astype(BF16)
        hidden_next[...] = units
        overlap[...] = (-factor * dot_t(units, hidden[...])).astype(BF16)

    term = dot(hidden_next[...], down_w[...]) + dot(overlap[...], cotangent[...])
    out[...] = (0.5 * term).astype(BF16)


def whole(shape):
    return pl.BlockSpec(shape, lambda i: (0,) * len(shape))


def columns(rows, width):
    return pl.BlockSpec((rows, width), lambda i: (0, i))


def run(kernel, steps, in_specs, outs, out_specs, scratch, flops, name, args):
    moved = sum(a.size * a.dtype.itemsize for a in args)
    return pl.pallas_call(
        kernel,
        grid=(steps,),
        in_specs=in_specs,
        out_shape=outs,
        out_specs=out_specs,
        scratch_shapes=scratch,
        cost_estimate=pl.CostEstimate(flops=flops, bytes_accessed=moved, transcendentals=0),
        compiler_params=pltpu.CompilerParams(vmem_limit_bytes=VMEM_LIMIT),
        name=name,
    )(*args)


def per_device(layer_in, next_in, returned, norm_gain, gate_weight, up_weight, down_weight, wiring):
    half_ring = lax.axis_size("section") // 2
    first_half = lax.axis_index("section") < half_ring
    row_count = layer_in.shape[1]
    blocks_dev = row_count // BLK
    capacity = returned.shape[1] // BLK
    token_count = row_count * lax.axis_size("rep")
    gain_row = norm_gain[0]
    gate_local, up_local, down_local = gate_weight[0].T, up_weight[0].T, down_weight[0]
    slot_rows = returned[0]

    update_factor = step_rate / token_count
    width = layer_in.shape[2]
    units = gate_local.shape[0]
    chunk = min(WIDTH, width)
    steps = width // chunk

    shifted = send(slot_rows, ds=-1)
    next_values, _, next_normed = normalize(next_in[0], gain_row)
    mate_normed = send(next_normed, ds=half_ring)
    values, row_scale, normed = normalize(layer_in[0], gain_row)
    select = selection(wiring[0], blocks_dev, capacity)
    spread = lax.optimization_barrier(select.T)

    block_z = jnp.concatenate([shifted, normed], axis=0)
    block_y = jnp.concatenate(
        [block_z] + [send(block_z, dz=-k) for k in range(1, NZ)], axis=0
    )
    blocks = [block_y] + [send(block_y, dy=-k) for k in range(1, NY)]
    blocks = blocks + [send(block, dc=1) for block in blocks]
    next_y = jnp.concatenate(
        [
            jnp.where(first_half, next_normed, mate_normed),
            jnp.where(first_half, mate_normed, next_normed),
        ],
        axis=0,
    )
    next_z = jnp.concatenate([next_y] + [send(next_y, dy=-k) for k in range(1, NY)], axis=0)
    nexts = [next_z] + [send(next_z, dz=-k) for k in range(1, NZ)]
    nexts = nexts + [send(block, dc=1) for block in nexts]

    pair_tokens = 2 * token_count
    part = jax.ShapeDtypeStruct((token_count, units), BF16)
    product = jax.ShapeDtypeStruct((pair_tokens, units), F32)
    product_sent = jax.ShapeDtypeStruct((pair_tokens, units), BF16)
    per_row = 2 * width * units
    cotangent, hidden, grad_gate_act, grad_up_act, gate_part, up_part, gate_sent, up_sent = run(
        functools.partial(first_kernel, len(blocks), update_factor),
        steps,
        [whole(select.shape)]
        + [columns(block.shape[0], chunk) for block in blocks + nexts]
        + [columns(units, chunk)] * 3,
        [jax.ShapeDtypeStruct((token_count, width), BF16), part, part, part]
        + [product, product, product_sent, product_sent],
        [columns(token_count, chunk)]
        + [whole(part.shape)] * 3
        + [whole(product.shape)] * 4,
        [
            pltpu.VMEM((token_count + pair_tokens, units), F32),
            pltpu.VMEM((token_count + pair_tokens, units), F32),
            pltpu.VMEM((token_count, units), F32),
            pltpu.VMEM((pair_tokens, token_count), F32),
        ],
        per_row * token_count * 9,
        "first",
        [select] + blocks + nexts + [gate_local, up_local, down_local],
    )
    mate_gate = send(gate_sent, ds=half_ring)
    mate_up = send(up_sent, ds=half_ring)

    own_rows = jnp.concatenate([values, jnp.zeros_like(values)], axis=0)
    terms = run(
        second_kernel,
        steps,
        [whole(spread.shape)]
        + [whole(part.shape)] * 3
        + [columns(own_rows.shape[0], chunk)]
        + [columns(units, chunk)] * 3,
        jax.ShapeDtypeStruct((spread.shape[0], width), BF16),
        columns(spread.shape[0], chunk),
        [],
        per_row * token_count * 5,
        "second",
        [spread, hidden, grad_gate_act, grad_up_act, own_rows, gate_local, up_local, down_local],
    )
    both = y_sum(core_sum(terms))
    gate_part, up_part, both = lax.optimization_barrier((gate_part, up_part, both))

    term_next = run(
        functools.partial(third_kernel, update_factor, row_count),
        steps,
        [whole(product.shape)] * 4
        + [whole(part.shape), columns(token_count, chunk), columns(units, chunk)],
        jax.ShapeDtypeStruct((pair_tokens, width), BF16),
        columns(pair_tokens, chunk),
        [pltpu.VMEM((pair_tokens, units), BF16), pltpu.VMEM((pair_tokens, token_count), BF16)],
        per_row * token_count * 3,
        "third",
        [gate_part, up_part, mate_gate, mate_up, hidden, cotangent, down_local],
    )
    pair = core_sum(term_next)
    both = cut(after(both, pair), NZ)
    both = add_up([both[0]] + [send(both[k], dz=k) for k in range(1, NZ)])
    forwarded = send(both[: slot_rows.shape[0]].astype(BF16), ds=1)
    dnormed = both[slot_rows.shape[0] :]
    first, second = cut(after(y_sum(pair), both), 2)
    own_part = jnp.where(first_half, first, second)
    mate_part = jnp.where(first_half, second, first)
    pair_sum = add_up([own_part, send(mate_part, ds=half_ring)]).astype(BF16)
    nparts = cut(pair_sum, NZ)
    next_out = add_up(
        [next_values, nparts[0]] + [send(nparts[k], dz=k) for k in range(1, NZ)]
    ).astype(BF16)
    scaled_grad = gain_row[None, :] * dnormed
    input_grad = (
        cotangent[:row_count].astype(F32)
        + row_scale * scaled_grad
        - values * row_scale**3 * jnp.mean(values * scaled_grad, axis=1, keepdims=True)
    ).astype(BF16)
    return (forwarded[None], input_grad[None], next_out[None])


def solution(mesh):
    in_specs = (
        P("section", "rep", None),
        P("section", "rep", None),
        P("section", "rep", None),
        P("section", None),
        P("section", None, "rep"),
        P("section", None, "rep"),
        P("section", "rep", None),
        P("section", None, None),
    )
    out_specs = (P("section", "rep", None), P("section", "rep", None), P("section", "rep", None))
    return jax.shard_map(
        per_device, mesh=mesh, in_specs=in_specs, out_specs=out_specs, check_vma=False
    )
```

profile of v0, /device:TPU:8, one launch (start us, length us, event | category | flops | bytes accessed | tf_op | source)
XLA Modules:
  0.0 177.2 jit_solution(3532297493175113141)
XLA Ops:
  3.4 7.3 %collective-permute-start.11 = (bf16[4,4096]{1,0:T(4,128)(2,1)S(1)}, bf16[4,4096]{1,0:T(4,128)(2,1)S(1)}, u32[]{:S(2)}, u32[]{:S(2)}) collective-permute-start(bf16[4,4096]{1,0:T(4,128)(2,1)S(1)} %get-tuple-element.43), channel_id=1, source_target_pairs={{0,128},{1,129},{2,130},{3,131},{4,132},{5,133},{6,134},{7,135},{8... | collective-permute-start | bytes 98312 | tf_op jit(solution)/shard_map/ppermute | solution.py:39
  10.7 2.3 %collective-permute-start = (bf16[8,4096]{1,0:T(8,128)(2,1)}, bf16[8,4096]{1,0:T(8,128)(2,1)S(1)}, u32[]{:S(2)}, u32[]{:S(2)}) collective-permute-start(bf16[8,4096]{1,0:T(8,128)(2,1)} %bitcast.45), channel_id=1, source_target_pairs={{0,224},{1,225},{2,226},{3,227},{4,228},{5,229},{6,230},{7,231},{8... | collective-permute-start | bytes 196616 | tf_op jit(solution)/shard_map/ppermute | solution.py:39
  16.5 2.4 %collective-permute-start.12 = (bf16[8,4096]{1,0:T(8,128)(2,1)S(1)}, bf16[8,4096]{1,0:T(8,128)(2,1)S(1)}, u32[]{:S(2)}, u32[]{:S(2)}) collective-permute-start(bf16[8,4096]{1,0:T(8,128)(2,1)S(1)} %pad_maximum_fusion.1), channel_id=1, source_target_pairs={{0,6},{1,7},{2,0},{3,1},{4,2},{5,3},{6,4},{7,5},{8,14},{9,15},{10,... | collective-permute-start | bytes 196616 | tf_op jit(solution)/shard_map/ppermute | solution.py:39
  22.8 2.8 %collective-permute-start.2 = (bf16[12,4096]{1,0:T(8,128)(2,1)S(1)}, bf16[12,4096]{1,0:T(8,128)(2,1)S(1)}, u32[]{:S(2)}, u32[]{:S(2)}) collective-permute-start(bf16[12,4096]{1,0:T(8,128)(2,1)S(1)} %pad_maximum_fusion), channel_id=1, source_target_pairs={{0,16},{1,17},{2,18},{3,19},{4,20},{5,21},{6,22},{7,23},{8,24},{9,... | collective-permute-start | bytes 294920 | tf_op jit(solution)/shard_map/ppermute | solution.py:39
  27.7 10.7 %collective-permute-done.2 = bf16[12,4096]{1,0:T(8,128)(2,1)S(1)} collective-permute-done((bf16[12,4096]{1,0:T(8,128)(2,1)S(1)}, bf16[12,4096]{1,0:T(8,128)(2,1)S(1)}, u32[]{:S(2)}, u32[]{:S(2)}) %collective-permute-start.2) | collective-permute-done | bytes 98336 | tf_op jit(solution)/shard_map/ppermute | solution.py:39
  38.4 9.3 %collective-permute-start.15 = (bf16[32,4096]{1,0:T(8,128)(2,1)S(1)}, bf16[32,4096]{1,0:T(8,128)(2,1)}, u32[]{:S(2)}, u32[]{:S(2)}) collective-permute-start(bf16[32,4096]{1,0:T(8,128)(2,1)S(1)} %concatenate.44.refs_9_), channel_id=1, source_target_pairs={{0,24},{1,25},{2,26},{3,27},{4,28},{5,29},{6,30},{7,31},{8,0},{9,1... | collective-permute-start | bytes 786440 | tf_op jit(solution)/shard_map/ppermute | solution.py:39
  50.3 2.6 %collective-permute-start.5 = (bf16[48,4096]{1,0:T(8,128)(2,1)S(1)}, bf16[48,4096]{1,0:T(8,128)(2,1)S(1)}, u32[]{:S(2)}, u32[]{:S(2)}) collective-permute-start(bf16[48,4096]{1,0:T(8,128)(2,1)S(1)} %concatenate.42.refs_1_), channel_id=1, source_target_pairs={{0,4},{1,5},{2,6},{3,7},{4,0},{5,1},{6,2},{7,3},{8,12},{9,13},{10,... | collective-permute-start | bytes 1179656 | tf_op jit(solution)/shard_map/ppermute | solution.py:39
  53.0 2.0 %collective-permute-start.4 = (bf16[48,4096]{1,0:T(8,128)(2,1)S(1)}, bf16[48,4096]{1,0:T(8,128)(2,1)S(1)}, u32[]{:S(2)}, u32[]{:S(2)}) collective-permute-start(bf16[48,4096]{1,0:T(8,128)(2,1)S(1)} %concatenate.42.refs_1_), channel_id=1, source_target_pairs={{0,6},{1,7},{2,0},{3,1},{4,2},{5,3},{6,4},{7,5},{8,14},{9,15},{10,... | collective-permute-start | bytes 1179656 | tf_op jit(solution)/shard_map/ppermute | solution.py:39
  56.9 3.7 %collective-permute-done.6.refs_4_ = bf16[48,4096]{1,0:T(8,128)(2,1)S(1)} collective-permute-done((bf16[48,4096]{1,0:T(8,128)(2,1)S(1)}, bf16[48,4096]{1,0:T(8,128)(2,1)S(1)}, u32[]{:S(2)}, u32[]{:S(2)}) %collective-permute-start.6) | collective-permute-done | bytes 393248 | tf_op jit(solution)/shard_map/ppermute | solution.py:39
  60.6 3.4 %collective-permute-done.5.refs_3_ = bf16[48,4096]{1,0:T(8,128)(2,1)S(1)} collective-permute-done((bf16[48,4096]{1,0:T(8,128)(2,1)S(1)}, bf16[48,4096]{1,0:T(8,128)(2,1)S(1)}, u32[]{:S(2)}, u32[]{:S(2)}) %collective-permute-start.5) | collective-permute-done | bytes 393248 | tf_op jit(solution)/shard_map/ppermute | solution.py:39
  63.9 6.0 %collective-permute-done.4.refs_2_ = bf16[48,4096]{1,0:T(8,128)(2,1)S(1)} collective-permute-done((bf16[48,4096]{1,0:T(8,128)(2,1)S(1)}, bf16[48,4096]{1,0:T(8,128)(2,1)S(1)}, u32[]{:S(2)}, u32[]{:S(2)}) %collective-permute-start.4) | collective-permute-done | bytes 393248 | tf_op jit(solution)/shard_map/ppermute | solution.py:39
  72.7 2.0 %copy-done = bf16[1,448,4096]{2,1,0:T(8,128)(2,1)S(1)} copy-done((bf16[1,448,4096]{2,1,0:T(8,128)(2,1)S(1)}, bf16[1,448,4096]{2,1,0:T(8,128)(2,1)}, u32[]{:S(2)}) %copy-start) | copy-done | bytes 3670040
  74.8 2.0 %copy-done.2 = bf16[1,4096,448]{1,2,0:T(8,128)(2,1)S(1)} copy-done((bf16[1,4096,448]{1,2,0:T(8,128)(2,1)S(1)}, bf16[1,4096,448]{1,2,0:T(8,128)(2,1)}, u32[]{:S(2)}) %copy-start.2) | copy-done | bytes 3670040
  76.8 2.0 %copy-done.4 = bf16[1,4096,448]{1,2,0:T(8,128)(2,1)S(1)} copy-done((bf16[1,4096,448]{1,2,0:T(8,128)(2,1)S(1)}, bf16[1,4096,448]{1,2,0:T(8,128)(2,1)}, u32[]{:S(2)}) %copy-start.4) | copy-done | bytes 3670040
  80.8 9.6 %first.1 = (bf16[128,4096]{1,0:T(8,128)(2,1)S(1)}, bf16[128,448]{1,0:T(8,128)(2,1)S(1)}, bf16[128,448]{1,0:T(8,128)(2,1)S(1)}, bf16[128,448]{1,0:T(8,128)(2,1)S(...) custom-call(bf16[256,384]{1,0:T(8,128)(2,1)S(1)} %copy.14.refs_0_, ...), custom_call_target="tpu_custom_call" | custom-call | flops 4227858432 | bytes 16449536 | tf_op jit(solution)/shard_map/first/pallas_call | solution.py:228
  90.4 4.4 %second.1 = bf16[384,4096]{1,0:T(8,128)(2,1)S(1)} custom-call(bf16[384,256]{1,0:T(8,128)(2,1)S(1)} %bitcast.40, bf16[128,448]{1,0:T(8,128)(2,1)S(1)} %get-tuple-element.18.hidden, bf16[128,448]{1,0:T(8,128)(2,1)S(1)} %get-tuple-element.19.dgate, bf16[128,448]{1,0:T(8,128)(2,1)S(1)} %get-tuple-element.20.dup, f32[8,4096]{1,0:T(8,128)S(1)} %concatenate.45.own_rows, ...), custom_call_target="tpu_custom_call" | custom-call | flops 2348810240 | bytes 11681792 | tf_op jit(solution)/shard_map/second/pallas_call | solution.py:228
  95.2 3.3 %collective-permute-done.22 = bf16[192,4096]{1,0:T(8,128)(2,1)S(1)} collective-permute-done((bf16[192,4096]{1,0:T(8,128)(2,1)S(1)}, bf16[192,4096]{1,0:T(8,128)(2,1)S(1)}, u32[]{:S(2)}, u32[]{:S(2)}) %collective-permute-start.22) | collective-permute-done | bytes 1572896 | tf_op jit(solution)/shard_map/ppermute | solution.py:39
  101.2 2.6 %collective-permute-start.24 = (bf16[48,4096]{1,0:T(8,128)(2,1)S(1)}, bf16[48,4096]{1,0:T(8,128)(2,1)S(1)}, u32[]{:S(2)}, u32[]{:S(2)}) collective-permute-start(bf16[48,4096]{1,0:T(8,128)(2,1)S(1)} %get-tuple-element.31), channel_id=1, source_target_pairs={{0,4},{1,5},{2,6},{3,7},{4,0},{5,1},{6,2},{7,3},{8,12},{9,13},{10,... | collective-permute-start | bytes 1179656 | tf_op jit(solution)/shard_map/ppermute | solution.py:39
  103.8 5.4 %collective-permute-start.26 = (bf16[256,448]{1,0:T(8,128)(2,1)S(1)}, bf16[256,448]{1,0:T(8,128)(2,1)S(1)}, u32[]{:S(2)}, u32[]{:S(2)}) collective-permute-start(bf16[256,448]{1,0:T(8,128)(2,1)S(1)} %get-tuple-element.24), channel_id=1, source_target_pairs={{0,128},{1,129},{2,130},{3,131},{4,132},{5,133},{6,134},{7,135},{8... | collective-permute-start | bytes 688136 | tf_op jit(solution)/shard_map/ppermute | solution.py:39
  111.5 9.6 %collective-permute-done.24 = bf16[48,4096]{1,0:T(8,128)(2,1)S(1)} collective-permute-done((bf16[48,4096]{1,0:T(8,128)(2,1)S(1)}, bf16[48,4096]{1,0:T(8,128)(2,1)S(1)}, u32[]{:S(2)}, u32[]{:S(2)}) %collective-permute-start.24) | collective-permute-done | bytes 393248 | tf_op jit(solution)/shard_map/ppermute | solution.py:39
  121.3 5.5 %collective-permute-done.26.mate_gate = bf16[256,448]{1,0:T(8,128)(2,1)S(1)} collective-permute-done((bf16[256,448]{1,0:T(8,128)(2,1)S(1)}, bf16[256,448]{1,0:T(8,128)(2,1)S(1)}, u32[]{:S(2)}, u32[]{:S(2)}) %collective-permute-start.26) | collective-permute-done | bytes 229408 | tf_op jit(solution)/shard_map/ppermute | solution.py:39
  126.8 5.4 %collective-permute-done.27.mate_up = bf16[256,448]{1,0:T(8,128)(2,1)S(1)} collective-permute-done((bf16[256,448]{1,0:T(8,128)(2,1)S(1)}, bf16[256,448]{1,0:T(8,128)(2,1)S(1)}, u32[]{:S(2)}, u32[]{:S(2)}) %collective-permute-start.27) | collective-permute-done | bytes 229408 | tf_op jit(solution)/shard_map/ppermute | solution.py:39
  132.2 3.3 %third.1 = bf16[256,4096]{1,0:T(8,128)(2,1)S(1)} custom-call(f32[256,448]{1,0:T(8,128)S(1)} %get-tuple-element.22.gate, f32[256,448]{1,0:T(8,128)S(1)} %get-tuple-element.23.up, bf16[256,448]{1,0:T(8,128)(2,1)S(1)} %collective-permute-done.26.mate_gate, bf16[256,448]{1,0:T(8,128)(2,1)S(1)} %collective-permute-done.27.mate_up, ...), custom_call_target="tpu_custom_call" | custom-call | flops 1409286144 | bytes 6209536 | tf_op jit(solution)/shard_map/third/pallas_call | solution.py:228
  135.8 2.6 %collective-permute-done.28 = bf16[128,4096]{1,0:T(8,128)(2,1)S(1)} collective-permute-done((bf16[128,4096]{1,0:T(8,128)(2,1)S(1)}, bf16[128,4096]{1,0:T(8,128)(2,1)S(1)}, u32[]{:S(2)}, u32[]{:S(2)}) %collective-permute-start.28) | collective-permute-done | bytes 1048608 | tf_op jit(solution)/shard_map/ppermute | solution.py:39
  139.0 3.6 %collective-permute-start.31 = (bf16[12,4096]{1,0:T(8,128)(2,1)S(1)}, bf16[12,4096]{1,0:T(8,128)(2,1)S(1)}, u32[]{:S(2)}, u32[]{:S(2)}) collective-permute-start(bf16[12,4096]{1,0:T(8,128)(2,1)S(1)} %get-tuple-element.36), channel_id=1, source_target_pairs={{0,24},{1,25},{2,26},{3,27},{4,28},{5,29},{6,30},{7,31},{8,0},{9,1... | collective-permute-start | bytes 294920 | tf_op jit(solution)/shard_map/ppermute | solution.py:39
  144.8 2.2 %collective-permute-done.29 = bf16[12,4096]{1,0:T(8,128)(2,1)S(1)} collective-permute-done((bf16[12,4096]{1,0:T(8,128)(2,1)S(1)}, bf16[12,4096]{1,0:T(8,128)(2,1)S(1)}, u32[]{:S(2)}, u32[]{:S(2)}) %collective-permute-start.29) | collective-permute-done | bytes 98336 | tf_op jit(solution)/shard_map/ppermute | solution.py:39
  149.0 3.5 %collective-permute-done.30 = bf16[12,4096]{1,0:T(8,128)(2,1)S(1)} collective-permute-done((bf16[12,4096]{1,0:T(8,128)(2,1)S(1)}, bf16[12,4096]{1,0:T(8,128)(2,1)S(1)}, u32[]{:S(2)}, u32[]{:S(2)}) %collective-permute-start.30) | collective-permute-done | bytes 98336 | tf_op jit(solution)/shard_map/ppermute | solution.py:39
  153.2 4.0 %collective-permute-done.34 = bf16[32,4096]{1,0:T(8,128)(2,1)S(1)} collective-permute-done((bf16[32,4096]{1,0:T(8,128)(2,1)S(1)}, bf16[32,4096]{1,0:T(8,128)(2,1)S(1)}, u32[]{:S(2)}, u32[]{:S(2)}) %collective-permute-start.34) | collective-permute-done | bytes 262176 | tf_op jit(solution)/shard_map/ppermute | solution.py:39
  157.3 3.4 %collective-permute-start.36 = (bf16[16,4096]{1,0:T(8,128)(2,1)S(1)}, bf16[16,4096]{1,0:T(8,128)(2,1)S(1)}, u32[]{:S(2)}, u32[]{:S(2)}) collective-permute-start(bf16[16,4096]{1,0:T(8,128)(2,1)S(1)} %broadcast_select_fusion), channel_id=1, source_target_pairs={{0,128},{1,129},{2,130},{3,131},{4,132},{5,133},{6,134},{7,135},{8... | collective-permute-start | bytes 393224 | tf_op jit(solution)/shard_map/ppermute | solution.py:39
  160.8 6.2 %collective-permute-done.36 = bf16[16,4096]{1,0:T(8,128)(2,1)S(1)} collective-permute-done((bf16[16,4096]{1,0:T(8,128)(2,1)S(1)}, bf16[16,4096]{1,0:T(8,128)(2,1)S(1)}, u32[]{:S(2)}, u32[]{:S(2)}) %collective-permute-start.36) | collective-permute-done | bytes 131104 | tf_op jit(solution)/shard_map/ppermute | solution.py:39
  168.9 2.1 %collective-permute-start.39 = (bf16[4,4096]{1,0:T(4,128)(2,1)S(1)}, bf16[4,4096]{1,0:T(4,128)(2,1)S(1)}, u32[]{:S(2)}, u32[]{:S(2)}) collective-permute-start(bf16[4,4096]{1,0:T(4,128)(2,1)S(1)} %get-tuple-element.39), channel_id=1, source_target_pairs={{0,24},{1,25},{2,26},{3,27},{4,28},{5,29},{6,30},{7,31},{8,0},{9,1... | collective-permute-start | bytes 98312 | tf_op jit(solution)/shard_map/ppermute | solution.py:39
  173.5 2.4 %collective-permute-done.38 = bf16[4,4096]{1,0:T(4,128)(2,1)S(1)} collective-permute-done((bf16[4,4096]{1,0:T(4,128)(2,1)S(1)}, bf16[4,4096]{1,0:T(4,128)(2,1)S(1)}, u32[]{:S(2)}, u32[]{:S(2)}) %collective-permute-start.38) | collective-permute-done | bytes 32800 | tf_op jit(solution)/shard_map/ppermute | solution.py:39
  (124 shorter events, 38.3 us)
Async XLA Ops:
  3.4 10.5 %collective-permute-start.11 = (bf16[4,4096]{1,0:T(4,128)(2,1)S(1)}, bf16[4,4096]{1,0:T(4,128)(2,1)S(1)}, u32[]{:S(2)}, u32[]{:S(2)}) collective-permute-start(bf16[4,4096]{1,0:T(4,128)(2,1)S(1)} %get-tuple-element.43), channel_id=1, source_target_pairs={{0,128},{1,129},{2,130},{3,131},{4,132},{5,133},{6,134},{7,135},{8... | collective-permute-start | bytes 98312 | tf_op jit(solution)/shard_map/ppermute | solution.py:39
  10.7 8.3 %collective-permute-start = (bf16[8,4096]{1,0:T(8,128)(2,1)}, bf16[8,4096]{1,0:T(8,128)(2,1)S(1)}, u32[]{:S(2)}, u32[]{:S(2)}) collective-permute-start(bf16[8,4096]{1,0:T(8,128)(2,1)} %bitcast.45), channel_id=1, source_target_pairs={{0,224},{1,225},{2,226},{3,227},{4,228},{5,229},{6,230},{7,231},{8... | collective-permute-start | bytes 196616 | tf_op jit(solution)/shard_map/ppermute | solution.py:39
  14.0 6.1 %collective-permute-start.14 = (bf16[8,4096]{1,0:T(8,128)(2,1)S(1)}, bf16[8,4096]{1,0:T(8,128)(2,1)S(1)}, u32[]{:S(2)}, u32[]{:S(2)}) collective-permute-start(bf16[8,4096]{1,0:T(8,128)(2,1)S(1)} %pad_maximum_fusion.1), channel_id=1, source_target_pairs={{0,2},{1,3},{2,4},{3,5},{4,6},{5,7},{6,0},{7,1},{8,10},{9,11},{10,... | collective-permute-start | bytes 196616 | tf_op jit(solution)/shard_map/ppermute | solution.py:39
  15.6 5.9 %collective-permute-start.13 = (bf16[8,4096]{1,0:T(8,128)(2,1)S(1)}, bf16[8,4096]{1,0:T(8,128)(2,1)S(1)}, u32[]{:S(2)}, u32[]{:S(2)}) collective-permute-start(bf16[8,4096]{1,0:T(8,128)(2,1)S(1)} %pad_maximum_fusion.1), channel_id=1, source_target_pairs={{0,4},{1,5},{2,6},{3,7},{4,0},{5,1},{6,2},{7,3},{8,12},{9,13},{10,... | collective-permute-start | bytes 196616 | tf_op jit(solution)/shard_map/ppermute | solution.py:39
  19.0 7.6 %collective-permute-start.3 = (bf16[12,4096]{1,0:T(8,128)(2,1)S(1)}, bf16[12,4096]{1,0:T(8,128)(2,1)S(1)}, u32[]{:S(2)}, u32[]{:S(2)}) collective-permute-start(bf16[12,4096]{1,0:T(8,128)(2,1)S(1)} %pad_maximum_fusion), channel_id=1, source_target_pairs={{0,8},{1,9},{2,10},{3,11},{4,12},{5,13},{6,14},{7,15},{8,16},{9,17... | collective-permute-start | bytes 294920 | tf_op jit(solution)/shard_map/ppermute | solution.py:39
  21.6 28.1 %collective-permute-start.18 = (bf16[32,4096]{1,0:T(8,128)(2,1)S(1)}, bf16[32,4096]{1,0:T(8,128)(2,1)S(1)}, u32[]{:S(2)}, u32[]{:S(2)}) collective-permute-start(bf16[32,4096]{1,0:T(8,128)(2,1)S(1)} %concatenate.44.refs_9_), channel_id=1, source_target_pairs={{0,1},{1,0},{2,3},{3,2},{4,5},{5,4},{6,7},{7,6},{8,9},{9,8},{10,11... | collective-permute-start | bytes 786440 | tf_op jit(solution)/shard_map/ppermute | solution.py:39
  21.7 31.3 %collective-permute-start.17 = (bf16[32,4096]{1,0:T(8,128)(2,1)S(1)}, bf16[32,4096]{1,0:T(8,128)(2,1)}, u32[]{:S(2)}, u32[]{:S(2)}) collective-permute-start(bf16[32,4096]{1,0:T(8,128)(2,1)S(1)} %concatenate.44.refs_9_), channel_id=1, source_target_pairs={{0,8},{1,9},{2,10},{3,11},{4,12},{5,13},{6,14},{7,15},{8,16},{9,17... | collective-permute-start | bytes 786440 | tf_op jit(solution)/shard_map/ppermute | solution.py:39
  22.8 15.6 %collective-permute-start.2 = (bf16[12,4096]{1,0:T(8,128)(2,1)S(1)}, bf16[12,4096]{1,0:T(8,128)(2,1)S(1)}, u32[]{:S(2)}, u32[]{:S(2)}) collective-permute-start(bf16[12,4096]{1,0:T(8,128)(2,1)S(1)} %pad_maximum_fusion), channel_id=1, source_target_pairs={{0,16},{1,17},{2,18},{3,19},{4,20},{5,21},{6,22},{7,23},{8,24},{9,... | collective-permute-start | bytes 294920 | tf_op jit(solution)/shard_map/ppermute | solution.py:39
  25.6 22.1 %collective-permute-start.1 = (bf16[12,4096]{1,0:T(8,128)(2,1)S(1)}, bf16[12,4096]{1,0:T(8,128)(2,1)S(1)}, u32[]{:S(2)}, u32[]{:S(2)}) collective-permute-start(bf16[12,4096]{1,0:T(8,128)(2,1)S(1)} %pad_maximum_fusion), channel_id=1, source_target_pairs={{0,24},{1,25},{2,26},{3,27},{4,28},{5,29},{6,30},{7,31},{8,0},{9,1... | collective-permute-start | bytes 294920 | tf_op jit(solution)/shard_map/ppermute | solution.py:39
  26.6 29.7 %collective-permute-start.16 = (bf16[32,4096]{1,0:T(8,128)(2,1)S(1)}, bf16[32,4096]{1,0:T(8,128)(2,1)}, u32[]{:S(2)}, u32[]{:S(2)}) collective-permute-start(bf16[32,4096]{1,0:T(8,128)(2,1)S(1)} %concatenate.44.refs_9_), channel_id=1, source_target_pairs={{0,16},{1,17},{2,18},{3,19},{4,20},{5,21},{6,22},{7,23},{8,24},{9,... | collective-permute-start | bytes 786440 | tf_op jit(solution)/shard_map/ppermute | solution.py:39
  38.4 18.0 %collective-permute-start.15 = (bf16[32,4096]{1,0:T(8,128)(2,1)S(1)}, bf16[32,4096]{1,0:T(8,128)(2,1)}, u32[]{:S(2)}, u32[]{:S(2)}) collective-permute-start(bf16[32,4096]{1,0:T(8,128)(2,1)S(1)} %concatenate.44.refs_9_), channel_id=1, source_target_pairs={{0,24},{1,25},{2,26},{3,27},{4,28},{5,29},{6,30},{7,31},{8,0},{9,1... | collective-permute-start | bytes 786440 | tf_op jit(solution)/shard_map/ppermute | solution.py:39
  48.4 12.1 %collective-permute-start.6 = (bf16[48,4096]{1,0:T(8,128)(2,1)S(1)}, bf16[48,4096]{1,0:T(8,128)(2,1)S(1)}, u32[]{:S(2)}, u32[]{:S(2)}) collective-permute-start(bf16[48,4096]{1,0:T(8,128)(2,1)S(1)} %concatenate.42.refs_1_), channel_id=1, source_target_pairs={{0,2},{1,3},{2,4},{3,5},{4,6},{5,7},{6,0},{7,1},{8,10},{9,11},{10,... | collective-permute-start | bytes 1179656 | tf_op jit(solution)/shard_map/ppermute | solution.py:39
  50.3 13.6 %collective-permute-start.5 = (bf16[48,4096]{1,0:T(8,128)(2,1)S(1)}, bf16[48,4096]{1,0:T(8,128)(2,1)S(1)}, u32[]{:S(2)}, u32[]{:S(2)}) collective-permute-start(bf16[48,4096]{1,0:T(8,128)(2,1)S(1)} %concatenate.42.refs_1_), channel_id=1, source_target_pairs={{0,4},{1,5},{2,6},{3,7},{4,0},{5,1},{6,2},{7,3},{8,12},{9,13},{10,... | collective-permute-start | bytes 1179656 | tf_op jit(solution)/shard_map/ppermute | solution.py:39
  53.0 16.9 %collective-permute-start.4 = (bf16[48,4096]{1,0:T(8,128)(2,1)S(1)}, bf16[48,4096]{1,0:T(8,128)(2,1)S(1)}, u32[]{:S(2)}, u32[]{:S(2)}) collective-permute-start(bf16[48,4096]{1,0:T(8,128)(2,1)S(1)} %concatenate.42.refs_1_), channel_id=1, source_target_pairs={{0,6},{1,7},{2,0},{3,1},{4,2},{5,3},{6,4},{7,5},{8,14},{9,15},{10,... | collective-permute-start | bytes 1179656 | tf_op jit(solution)/shard_map/ppermute | solution.py:39
  56.4 13.6 %collective-permute-start.7 = (bf16[48,4096]{1,0:T(8,128)(2,1)S(1)}, bf16[48,4096]{1,0:T(8,128)(2,1)S(1)}, u32[]{:S(2)}, u32[]{:S(2)}) collective-permute-start(bf16[48,4096]{1,0:T(8,128)(2,1)S(1)} %concatenate.42.refs_1_), channel_id=1, source_target_pairs={{0,1},{1,0},{2,3},{3,2},{4,5},{5,4},{6,7},{7,6},{8,9},{9,8},{10,11... | collective-permute-start | bytes 1179656 | tf_op jit(solution)/shard_map/ppermute | solution.py:39
  56.4 14.1 %collective-permute-start.21 = (bf16[32,4096]{1,0:T(8,128)(2,1)}, bf16[32,4096]{1,0:T(8,128)(2,1)S(1)}, u32[]{:S(2)}, u32[]{:S(2)}) collective-permute-start(bf16[32,4096]{1,0:T(8,128)(2,1)} %collective-permute-done.17.refs_12_), channel_id=1, source_target_pairs={{0,1},{1,0},{2,3},{3,2},{4,5},{5,4},{6,7},{7,6},{8,9},{9,8},{10,11... | collective-permute-start | bytes 786440 | tf_op jit(solution)/shard_map/ppermute | solution.py:39
  60.6 12.2 %collective-permute-start.10 = (bf16[48,4096]{1,0:T(8,128)(2,1)S(1)}, bf16[48,4096]{1,0:T(8,128)(2,1)S(1)}, u32[]{:S(2)}, u32[]{:S(2)}) collective-permute-start(bf16[48,4096]{1,0:T(8,128)(2,1)S(1)} %collective-permute-done.6.refs_4_), channel_id=1, source_target_pairs={{0,1},{1,0},{2,3},{3,2},{4,5},{5,4},{6,7},{7,6},{8,9},{9,8},{10,11... | collective-permute-start | bytes 1179656 | tf_op jit(solution)/shard_map/ppermute | solution.py:39
  63.9 8.8 %collective-permute-start.9 = (bf16[48,4096]{1,0:T(8,128)(2,1)S(1)}, bf16[48,4096]{1,0:T(8,128)(2,1)S(1)}, u32[]{:S(2)}, u32[]{:S(2)}) collective-permute-start(bf16[48,4096]{1,0:T(8,128)(2,1)S(1)} %collective-permute-done.5.refs_3_), channel_id=1, source_target_pairs={{0,1},{1,0},{2,3},{3,2},{4,5},{5,4},{6,7},{7,6},{8,9},{9,8},{10,11... | collective-permute-start | bytes 1179656 | tf_op jit(solution)/shard_map/ppermute | solution.py:39
  99.1 12.0 %collective-permute-start.23 = (bf16[48,4096]{1,0:T(8,128)(2,1)S(1)}, bf16[48,4096]{1,0:T(8,128)(2,1)S(1)}, u32[]{:S(2)}, u32[]{:S(2)}) collective-permute-start(bf16[48,4096]{1,0:T(8,128)(2,1)S(1)} %get-tuple-element.29), channel_id=1, source_target_pairs={{0,2},{1,3},{2,4},{3,5},{4,6},{5,7},{6,0},{7,1},{8,10},{9,11},{10,... | collective-permute-start | bytes 1179656 | tf_op jit(solution)/shard_map/ppermute | solution.py:39
  99.8 11.7 %collective-permute-start.25 = (bf16[48,4096]{1,0:T(8,128)(2,1)S(1)}, bf16[48,4096]{1,0:T(8,128)(2,1)S(1)}, u32[]{:S(2)}, u32[]{:S(2)}) collective-permute-start(bf16[48,4096]{1,0:T(8,128)(2,1)S(1)} %get-tuple-element.30), channel_id=1, source_target_pairs={{0,6},{1,7},{2,0},{3,1},{4,2},{5,3},{6,4},{7,5},{8,14},{9,15},{10,... | collective-permute-start | bytes 1179656 | tf_op jit(solution)/shard_map/ppermute | solution.py:39
  101.2 19.9 %collective-permute-start.24 = (bf16[48,4096]{1,0:T(8,128)(2,1)S(1)}, bf16[48,4096]{1,0:T(8,128)(2,1)S(1)}, u32[]{:S(2)}, u32[]{:S(2)}) collective-permute-start(bf16[48,4096]{1,0:T(8,128)(2,1)S(1)} %get-tuple-element.31), channel_id=1, source_target_pairs={{0,4},{1,5},{2,6},{3,7},{4,0},{5,1},{6,2},{7,3},{8,12},{9,13},{10,... | collective-permute-start | bytes 1179656 | tf_op jit(solution)/shard_map/ppermute | solution.py:39
  103.8 23.0 %collective-permute-start.26 = (bf16[256,448]{1,0:T(8,128)(2,1)S(1)}, bf16[256,448]{1,0:T(8,128)(2,1)S(1)}, u32[]{:S(2)}, u32[]{:S(2)}) collective-permute-start(bf16[256,448]{1,0:T(8,128)(2,1)S(1)} %get-tuple-element.24), channel_id=1, source_target_pairs={{0,128},{1,129},{2,130},{3,131},{4,132},{5,133},{6,134},{7,135},{8... | collective-permute-start | bytes 688136 | tf_op jit(solution)/shard_map/ppermute | solution.py:39
  109.2 23.0 %collective-permute-start.27 = (bf16[256,448]{1,0:T(8,128)(2,1)S(1)}, bf16[256,448]{1,0:T(8,128)(2,1)S(1)}, u32[]{:S(2)}, u32[]{:S(2)}) collective-permute-start(bf16[256,448]{1,0:T(8,128)(2,1)S(1)} %get-tuple-element.25), channel_id=1, source_target_pairs={{0,128},{1,129},{2,130},{3,131},{4,132},{5,133},{6,134},{7,135},{8... | collective-permute-start | bytes 688136 | tf_op jit(solution)/shard_map/ppermute | solution.py:39
  138.8 8.3 %collective-permute-start.29 = (bf16[12,4096]{1,0:T(8,128)(2,1)S(1)}, bf16[12,4096]{1,0:T(8,128)(2,1)S(1)}, u32[]{:S(2)}, u32[]{:S(2)}) collective-permute-start(bf16[12,4096]{1,0:T(8,128)(2,1)S(1)} %get-tuple-element.35), channel_id=1, source_target_pairs={{0,8},{1,9},{2,10},{3,11},{4,12},{5,13},{6,14},{7,15},{8,16},{9,17... | collective-permute-start | bytes 294920 | tf_op jit(solution)/shard_map/ppermute | solution.py:39
  139.0 9.9 %collective-permute-start.31 = (bf16[12,4096]{1,0:T(8,128)(2,1)S(1)}, bf16[12,4096]{1,0:T(8,128)(2,1)S(1)}, u32[]{:S(2)}, u32[]{:S(2)}) collective-permute-start(bf16[12,4096]{1,0:T(8,128)(2,1)S(1)} %get-tuple-element.36), channel_id=1, source_target_pairs={{0,24},{1,25},{2,26},{3,27},{4,28},{5,29},{6,30},{7,31},{8,0},{9,1... | collective-permute-start | bytes 294920 | tf_op jit(solution)/shard_map/ppermute | solution.py:39
  142.7 9.9 %collective-permute-start.30 = (bf16[12,4096]{1,0:T(8,128)(2,1)S(1)}, bf16[12,4096]{1,0:T(8,128)(2,1)S(1)}, u32[]{:S(2)}, u32[]{:S(2)}) collective-permute-start(bf16[12,4096]{1,0:T(8,128)(2,1)S(1)} %get-tuple-element.37), channel_id=1, source_target_pairs={{0,16},{1,17},{2,18},{3,19},{4,20},{5,21},{6,22},{7,23},{8,24},{9,... | collective-permute-start | bytes 294920 | tf_op jit(solution)/shard_map/ppermute | solution.py:39
  142.7 10.5 %collective-permute-start.33 = (bf16[32,4096]{1,0:T(8,128)(2,1)S(1)}, bf16[32,4096]{1,0:T(8,128)(2,1)S(1)}, u32[]{:S(2)}, u32[]{:S(2)}) collective-permute-start(bf16[32,4096]{1,0:T(8,128)(2,1)S(1)} %get-tuple-element.32), channel_id=1, source_target_pairs={{0,2},{1,3},{2,4},{3,5},{4,6},{5,7},{6,0},{7,1},{8,10},{9,11},{10,... | collective-permute-start | bytes 786440 | tf_op jit(solution)/shard_map/ppermute | solution.py:39
  144.1 9.1 %collective-permute-start.35 = (bf16[32,4096]{1,0:T(8,128)(2,1)S(1)}, bf16[32,4096]{1,0:T(8,128)(2,1)S(1)}, u32[]{:S(2)}, u32[]{:S(2)}) collective-permute-start(bf16[32,4096]{1,0:T(8,128)(2,1)S(1)} %get-tuple-element.33), channel_id=1, source_target_pairs={{0,6},{1,7},{2,0},{3,1},{4,2},{5,3},{6,4},{7,5},{8,14},{9,15},{10,... | collective-permute-start | bytes 786440 | tf_op jit(solution)/shard_map/ppermute | solution.py:39
  147.0 10.2 %collective-permute-start.34 = (bf16[32,4096]{1,0:T(8,128)(2,1)S(1)}, bf16[32,4096]{1,0:T(8,128)(2,1)S(1)}, u32[]{:S(2)}, u32[]{:S(2)}) collective-permute-start(bf16[32,4096]{1,0:T(8,128)(2,1)S(1)} %get-tuple-element.34), channel_id=1, source_target_pairs={{0,4},{1,5},{2,6},{3,7},{4,0},{5,1},{6,2},{7,3},{8,12},{9,13},{10,... | collective-permute-start | bytes 786440 | tf_op jit(solution)/shard_map/ppermute | solution.py:39
  152.6 20.9 %collective-permute-start.32 = (bf16[8,4096]{1,0:T(8,128)(2,1)S(1)}, bf16[8,4096]{1,0:T(8,128)(2,1)S(1)}, u32[]{:S(2)}, u32[]{:S(2)}) collective-permute-start(bf16[8,4096]{1,0:T(8,128)(2,1)S(1)} %slice.172), channel_id=1, source_target_pairs={{0,32},{1,33},{2,34},{3,35},{4,36},{5,37},{6,38},{7,39},{8,40},{9,... | collective-permute-start | bytes 196616 | tf_op jit(solution)/shard_map/ppermute | solution.py:39
  157.3 9.6 %collective-permute-start.36 = (bf16[16,4096]{1,0:T(8,128)(2,1)S(1)}, bf16[16,4096]{1,0:T(8,128)(2,1)S(1)}, u32[]{:S(2)}, u32[]{:S(2)}) collective-permute-start(bf16[16,4096]{1,0:T(8,128)(2,1)S(1)} %broadcast_select_fusion), channel_id=1, source_target_pairs={{0,128},{1,129},{2,130},{3,131},{4,132},{5,133},{6,134},{7,135},{8... | collective-permute-start | bytes 393224 | tf_op jit(solution)/shard_map/ppermute | solution.py:39
  167.1 6.4 %collective-permute-start.37 = (bf16[4,4096]{1,0:T(4,128)(2,1)S(1)}, bf16[4,4096]{1,0:T(4,128)(2,1)S(1)}, u32[]{:S(2)}, u32[]{:S(2)}) collective-permute-start(bf16[4,4096]{1,0:T(4,128)(2,1)S(1)} %get-tuple-element.38), channel_id=1, source_target_pairs={{0,8},{1,9},{2,10},{3,11},{4,12},{5,13},{6,14},{7,15},{8,16},{9,17... | collective-permute-start | bytes 98312 | tf_op jit(solution)/shard_map/ppermute | solution.py:39
  (22 other events, 183.7 us)
where the time goes:
time: 180 us; the launch traced here: 177 us
  waiting for transfers between devices  73.1 us (41%)
  starting transfers between devices  65.4 us (36%)
  Pallas kernels  17.3 us (10%)
  local copies, waits for them, and re-layouts  10.8 us (6%)
  other arithmetic  8.11 us (5%)
    ppermute x40, waiting for transfers between devices, send(): return lax.ppermute(value, ('section', 'rep'), pairs)  73.1 us
    ppermute x40, starting transfers between devices, send(): return lax.ppermute(value, ('section', 'rep'), pairs)  65.4 us
    pallas_call x3, Pallas kernels, run(): pl.pallas_call(kernel, grid=(steps,), in_specs=in_specs, out_shape=outs,...  17.3 us
    unnamed x29, local copies, waits for them, and re-layouts  9.36 us
  transfers between devices with their start and end apart: 40, of which 19 were waited for; matrix products, arithmetic and copies ran while one was open for 4% of the time, Pallas kernels for 0%

commit v1 on v0

--- a/solution.py
+++ b/solution.py
@@ -18,7 +18,7 @@
 F32 = jnp.float32
 BF16 = jnp.bfloat16
 WIDTH = 1024
-VMEM_LIMIT = 18 << 20
+VMEM_LIMIT = 40 << 20
 
 
 def send(value, ds=0, dz=0, dy=0, dc=0):
@@ -32,8 +32,8 @@
                     source = s * replicas + (z * NY + y) * NC + c
                     target = (
                         ((s + ds) % sections) * replicas
-                        + (((z + dz) % NZ) * NY + (y + dy) % NY) * NC
-                        + (c + dc) % NC
+                        + ((z ^ dz) * NY + (y + dy) % NY) * NC
+                        + (c ^ dc)
                     )
                     pairs.append((source, target))
     return lax.ppermute(value, ("section", "rep"), pairs)
@@ -43,7 +43,7 @@
     me = lax.axis_index("rep")
     z, y, c = me // (NY * NC), (me // NC) % NY, me % NC
     dz, dy, dc = index % NZ, (index // NZ) % NY, index // (NZ * NY)
-    return (((z + dz) % NZ) * NY + (y + dy) % NY) * NC + (c + dc) % NC
+    return ((z ^ dz) * NY + (y + dy) % NY) * NC + (c ^ dc)
 
 
 def selection(wiring, blocks_dev, capacity):
@@ -109,11 +109,6 @@
     return [value[i * size : (i + 1) * size] for i in range(count)]
 
 
-def core_sum(terms):
-    mine, other = cut(terms, NC)
-    return add_up([mine, send(other, dc=1)]).astype(BF16)
-
-
 def y_sum(terms):
     parts = cut(terms, NY)
     return add_up(
@@ -125,75 +120,72 @@
     return dot(a, b, 1, 1)
 
 
-def first_kernel(count, factor, *refs):
-    select = refs[0]
-    blocks, nexts = refs[1 : 1 + count], refs[1 + count : 1 + 2 * count]
-    gate_w, up_w, down_w = refs[1 + 2 * count : 4 + 2 * count]
-    cot_out, hidden_out, dgate_out, dup_out, gate_out, up_out, gate_sent, up_sent = refs[
-        4 + 2 * count : 12 + 2 * count
-    ]
-    gate_sum, up_sum, dhidden_sum, inner_sum = refs[12 + 2 * count :]
-    step = pl.program_id(0)
+def first_kernel(count, *refs):
+    select, spread = refs[:2]
+    blocks = refs[2 : 2 + count]
+    own_rows, gate_w, up_w, down_w = refs[2 + count : 6 + count]
+    cot_out, normed_out, hidden_out, dgate_out, dup_out, mine, other = refs[6 + count : 13 + count]
+    gate_sum, up_sum, dhidden_sum = refs[13 + count :]
+    step, steps = pl.program_id(0), pl.num_programs(0) // 2
     tokens = dhidden_sum.shape[0]
-    chosen = dot(select[...], jnp.concatenate([r[...] for r in blocks], axis=0)).astype(BF16)
-    cotangent, normed = chosen[:tokens], chosen[tokens:]
-    cot_out[...] = cotangent
-    ahead = jnp.concatenate([r[...] for r in nexts], axis=0)
-    rows = jnp.concatenate([normed, ahead], axis=0)
-    gate = dot_t(rows, gate_w[...])
-    up = dot_t(rows, up_w[...])
-    dhidden = dot_t(cotangent, down_w[...])
-    inner = dot_t(ahead, normed)
-
-    @pl.when(step == 0)
-    def _():
-        gate_sum[...] = gate
-        up_sum[...] = up
-        dhidden_sum[...] = dhidden
-        inner_sum[...] = inner
-
-    @pl.when(step > 0)
-    def _():
-        gate_sum[...] += gate
-        up_sum[...] += up
-        dhidden_sum[...] += dhidden
-        inner_sum[...] += inner
-
-    @pl.when(step == pl.num_programs(0) - 1)
-    def _():
-        gate_act, up_act = gate_sum[:tokens], up_sum[:tokens]
+
+    @pl.when(step < steps)
+    def _():
+        chosen = dot(select[...], jnp.concatenate([r[...] for r in blocks], axis=0)).astype(BF16)
+        cotangent, normed = chosen[:tokens], chosen[tokens:]
+        cot_out[...] = cotangent
+        normed_out[...] = normed
+        first = step == 0
+        gate_sum[...] = jnp.where(first, 0.0, gate_sum[...]) + dot_t(normed, gate_w[...])
+        up_sum[...] = jnp.where(first, 0.0, up_sum[...]) + dot_t(normed, up_w[...])
+        dhidden_sum[...] = jnp.where(first, 0.0, dhidden_sum[...]) + dot_t(cotangent, down_w[...])
+
+    @pl.when(step == steps - 1)
+    def _():
+        gate_act, up_act, grad = gate_sum[...], up_sum[...], dhidden_sum[...]
         sigmoid_gate = jax.nn.sigmoid(gate_act)
         silu_gate = gate_act * sigmoid_gate
-        grad = dhidden_sum[...]
         hidden_out[...] = (silu_gate * up_act).astype(BF16)
-        dgate = (
+        dgate_out[...] = (
             grad * up_act * sigmoid_gate * (1.0 + gate_act * (1.0 - sigmoid_gate))
         ).astype(BF16)
-        dup = (grad * silu_gate).astype(BF16)
-        dgate_out[...] = dgate
-        dup_out[...] = dup
+        dup_out[...] = (grad * silu_gate).astype(BF16)
+
+    @pl.when(step >= steps)
+    def _():
+        top = own_rows.shape[0]
+        term = dot(hidden_out[...], down_w[...])
+        term = jnp.concatenate([term[:top] + own_rows[...], term[top:]], axis=0)
+        dterm = dot(dgate_out[...], gate_w[...]) + dot(dup_out[...], up_w[...])
+        both = jnp.concatenate([term.astype(BF16), dterm.astype(BF16)], axis=0)
+        terms = dot(spread[...], both).astype(BF16)
+        mine[...] = terms[: mine.shape[0]]
+        other[...] = terms[mine.shape[0] :]
+
+
+def second_kernel(count, factor, *refs):
+    nexts = refs[:count]
+    normed, dgate, dup, gate_w, up_w = refs[count : 5 + count]
+    gate_out, up_out, gate_sent, up_sent, gate_sum, up_sum, inner_sum = refs[5 + count :]
+    first = pl.program_id(0) == 0
+    rows = jnp.concatenate([r[...] for r in nexts], axis=0)
+    gate_sum[...] = jnp.where(first, 0.0, gate_sum[...]) + dot_t(rows, gate_w[...])
+    up_sum[...] = jnp.where(first, 0.0, up_sum[...]) + dot_t(rows, up_w[...])
+    inner_sum[...] = jnp.where(first, 0.0, inner_sum[...]) + dot_t(rows, normed[...])
+
+    @pl.when(pl.program_id(0) == pl.num_programs(0) - 1)
+    def _():
         overlap = (-factor * inner_sum[...]).astype(BF16)
-        gate_next = gate_sum[tokens:] + dot(overlap, dgate)
-        up_next = up_sum[tokens:] + dot(overlap, dup)
+        gate_next = gate_sum[...] + dot(overlap, dgate[...])
+        up_next = up_sum[...] + dot(overlap, dup[...])
         gate_out[...] = gate_next
         up_out[...] = up_next
         gate_sent[...] = gate_next.astype(BF16)
         up_sent[...] = up_next.astype(BF16)
 
 
-def second_kernel(
-    spread, hidden, dgate, dup, own_rows, gate_w, up_w, down_w, out
-):
-    top = own_rows.shape[0]
-    term = dot(hidden[...], down_w[...])
-    term = jnp.concatenate([term[:top] + own_rows[...], term[top:]], axis=0)
-    dterm = dot(dgate[...], gate_w[...]) + dot(dup[...], up_w[...])
-    both = jnp.concatenate([term.astype(BF16), dterm.astype(BF16)], axis=0)
-    out[...] = dot(spread[...], both).astype(BF16)
-
-
 def third_kernel(
-    factor, row_count, gate, up, mate_gate, mate_up, hidden, cotangent, down_w, out, hidden_next, overlap
+    factor, row_count, gate, up, mate_gate, mate_up, hidden, cotangent, down_w, mine, other, hidden_next, overlap
 ):
     @pl.when(pl.program_id(0) == 0)
     def _():
@@ -205,22 +197,25 @@
         at = lax.broadcasted_iota(jnp.int32, (rows, rows), 1)
         i, j = to & (row_count - 1), to // row_count
         z, replica, y, core = j & (NZ - 1), (j // NZ) & 1, (j // (2 * NZ)) & (NY - 1), j // (2 * NZ * NY)
-        source = (((core * NZ + z) * NY + y) * 2 + replica) * row_count + i
+        source = (((core * 2 + z // 2) * NY + y) * 2 + (z & 1)) * 2 + replica
+        source = source * row_count + i
         order = jnp.where(at == source, 1.0, 0.0).astype(BF16)
         units = dot(order, units).astype(BF16)
         hidden_next[...] = units
         overlap[...] = (-factor * dot_t(units, hidden[...])).astype(BF16)
 
     term = dot(hidden_next[...], down_w[...]) + dot(overlap[...], cotangent[...])
-    out[...] = (0.5 * term).astype(BF16)
+    term = (0.5 * term).astype(BF16)
+    mine[...] = term[: mine.shape[0]]
+    other[...] = term[mine.shape[0] :]
 
 
 def whole(shape):
     return pl.BlockSpec(shape, lambda i: (0,) * len(shape))
 
 
-def columns(rows, width):
-    return pl.BlockSpec((rows, width), lambda i: (0, i))
+def columns(rows, width, at=lambda i: i):
+    return pl.BlockSpec((rows, width), lambda i: (0, at(i)))
 
 
 def run(kernel, steps, in_specs, outs, out_specs, scratch, flops, name, args):
@@ -262,12 +257,6 @@
     select = selection(wiring[0], blocks_dev, capacity)
     spread = lax.optimization_barrier(select.T)
 
-    block_z = jnp.concatenate([shifted, normed], axis=0)
-    block_y = jnp.concatenate(
-        [block_z] + [send(block_z, dz=-k) for k in range(1, NZ)], axis=0
-    )
-    blocks = [block_y] + [send(block_y, dy=-k) for k in range(1, NY)]
-    blocks = blocks + [send(block, dc=1) for block in blocks]
     next_y = jnp.concatenate(
         [
             jnp.where(first_half, next_normed, mate_normed),
@@ -275,70 +264,91 @@
         ],
         axis=0,
     )
+    next_y = jnp.concatenate([next_y, send(next_y, dz=1)], axis=0)
     next_z = jnp.concatenate([next_y] + [send(next_y, dy=-k) for k in range(1, NY)], axis=0)
-    nexts = [next_z] + [send(next_z, dz=-k) for k in range(1, NZ)]
+    block_z = jnp.concatenate([shifted, normed], axis=0)
+    block_y = jnp.concatenate(
+        [block_z] + [send(block_z, dz=k) for k in range(1, NZ)], axis=0
+    )
+    block_y, next_z = lax.optimization_barrier((block_y, next_z))
+    blocks = [block_y] + [send(block_y, dy=-k) for k in range(1, NY)]
+    blocks = blocks + [send(block, dc=1) for block in blocks]
+    nexts = [next_z, send(next_z, dz=2)]
+    select, *nexts = lax.optimization_barrier((select, *nexts))
     nexts = nexts + [send(block, dc=1) for block in nexts]
 
     pair_tokens = 2 * token_count
     part = jax.ShapeDtypeStruct((token_count, units), BF16)
     product = jax.ShapeDtypeStruct((pair_tokens, units), F32)
     product_sent = jax.ShapeDtypeStruct((pair_tokens, units), BF16)
+    rows = jax.ShapeDtypeStruct((token_count, width), BF16)
+    half = jax.ShapeDtypeStruct((spread.shape[0] // NC, width), BF16)
     per_row = 2 * width * units
-    cotangent, hidden, grad_gate_act, grad_up_act, gate_part, up_part, gate_sent, up_sent = run(
-        functools.partial(first_kernel, len(blocks), update_factor),
+    own_rows = jnp.concatenate([values, jnp.zeros_like(values)], axis=0)
+
+    def up_to(i):
+        return jnp.minimum(i, steps - 1)
+
+    def back(i):
+        return steps - 1 - jnp.maximum(i - steps, 0)
+
+    def there_and_back(i):
+        return jnp.minimum(i, 2 * steps - 1 - i)
+
+    cotangent, normed_all, hidden, grad_gate_act, grad_up_act, mine, other = run(
+        functools.partial(first_kernel, len(blocks)),
+        2 * steps,
+        [whole(select.shape), whole(spread.shape)]
+        + [columns(block.shape[0], chunk, up_to) for block in blocks]
+        + [columns(own_rows.shape[0], chunk, back)]
+        + [columns(units, chunk, there_and_back)] * 3,
+        [rows, rows, part, part, part, half, half],
+        [columns(token_count, chunk, up_to)] * 2
+        + [whole(part.shape)] * 3
+        + [columns(half.shape[0], chunk, back)] * 2,
+        [pltpu.VMEM((token_count, units), F32)] * 3,
+        per_row * token_count * 9,
+        "first",
+        [select, spread] + blocks + [own_rows, gate_local, up_local, down_local],
+    )
+    from_core = send(other, dc=1)
+    gate_part, up_part, gate_sent, up_sent = run(
+        functools.partial(second_kernel, len(nexts), update_factor),
         steps,
-        [whole(select.shape)]
-        + [columns(block.shape[0], chunk) for block in blocks + nexts]
-        + [columns(units, chunk)] * 3,
-        [jax.ShapeDtypeStruct((token_count, width), BF16), part, part, part]
-        + [product, product, product_sent, product_sent],
-        [columns(token_count, chunk)]
-        + [whole(part.shape)] * 3
-        + [whole(product.shape)] * 4,
+        [columns(block.shape[0], chunk) for block in nexts]
+        + [columns(token_count, chunk), whole(part.shape), whole(part.shape)]
+        + [columns(units, chunk)] * 2,
+        [product, product, product_sent, product_sent],
+        [whole(product.shape)] * 4,
         [
-            pltpu.VMEM((token_count + pair_tokens, units), F32),
-            pltpu.VMEM((token_count + pair_tokens, units), F32),
-            pltpu.VMEM((token_count, units), F32),
+            pltpu.VMEM((pair_tokens, units), F32),
+            pltpu.VMEM((pair_tokens, units), F32),
             pltpu.VMEM((pair_tokens, token_count), F32),
         ],
-        per_row * token_count * 9,
-        "first",
-        [select] + blocks + nexts + [gate_local, up_local, down_local],
+        per_row * token_count * 5,
+        "second",
+        nexts + [normed_all, grad_gate_act, grad_up_act, gate_local, up_local],
     )
     mate_gate = send(gate_sent, ds=half_ring)
     mate_up = send(up_sent, ds=half_ring)
-
-    own_rows = jnp.concatenate([values, jnp.zeros_like(values)], axis=0)
-    terms = run(
-        second_kernel,
-        steps,
-        [whole(spread.shape)]
-        + [whole(part.shape)] * 3
-        + [columns(own_rows.shape[0], chunk)]
-        + [columns(units, chunk)] * 3,
-        jax.ShapeDtypeStruct((spread.shape[0], width), BF16),
-        columns(spread.shape[0], chunk),
-        [],
-        per_row * token_count * 5,
-        "second",
-        [spread, hidden, grad_gate_act, grad_up_act, own_rows, gate_local, up_local, down_local],
-    )
-    both = y_sum(core_sum(terms))
+    both = add_up([mine, after(from_core, gate_sent, up_sent)]).astype(BF16)
+    both = y_sum(both)
     gate_part, up_part, both = lax.optimization_barrier((gate_part, up_part, both))
 
-    term_next = run(
+    half = jax.ShapeDtypeStruct((pair_tokens // NC, width), BF16)
+    mine, other = run(
         functools.partial(third_kernel, update_factor, row_count),
         steps,
         [whole(product.shape)] * 4
         + [whole(part.shape), columns(token_count, chunk), columns(units, chunk)],
-        jax.ShapeDtypeStruct((pair_tokens, width), BF16),
-        columns(pair_tokens, chunk),
+        [half, half],
+        [columns(half.shape[0], chunk)] * 2,
         [pltpu.VMEM((pair_tokens, units), BF16), pltpu.VMEM((pair_tokens, token_count), BF16)],
         per_row * token_count * 3,
         "third",
         [gate_part, up_part, mate_gate, mate_up, hidden, cotangent, down_local],
     )
-    pair = core_sum(term_next)
+    pair = add_up([mine, send(other, dc=1)]).astype(BF16)
     both = cut(after(both, pair), NZ)
     both = add_up([both[0]] + [send(both[k], dz=k) for k in range(1, NZ)])
     forwarded = send(both[: slot_rows.shape[0]].astype(BF16), ds=1)

time: 180 us -> 178 us (0.989)
  starting transfers between devices: 65.4 us -> 55.7 us
  waiting for transfers between devices: 73.1 us -> 81 us
  Pallas kernels: 17.3 us -> 20.8 us
  local copies, waits for them, and re-layouts: 10.8 us -> 8.65 us
    ppermute x40 -> x37, starting transfers between devices: 65.4 us -> 55.7 us  [send(): return lax.ppermute(value, ('section', 'rep'), pairs)]
    ppermute x40 -> x37, waiting for transfers between devices: 73.1 us -> 81 us  [send(): return lax.ppermute(value, ('section', 'rep'), pairs)]
    pallas_call x3, Pallas kernels: 17.3 us -> 20.8 us  [run(): pl.pallas_call(kernel, grid=(steps,), in_specs=in_specs, out_shape=outs,...]
    unnamed x29 -> x33, local copies, waits for them, and re-layouts: 9.36 us -> 7.45 us
  transfers between devices with their start and end apart: 40 -> 37, of which waited for: 19 -> 20; matrix products, arithmetic and copies ran while one was open for 4% -> 4% of each run, Pallas kernels for 0% -> 3%
where the time goes in v1:
time: 178 us; the launch traced here: 177 us
  waiting for transfers between devices  81 us (46%)
  starting transfers between devices  55.7 us (31%)
  Pallas kernels  20.8 us (12%)
  local copies, waits for them, and re-layouts  8.65 us (5%)
  other arithmetic  8.29 us (5%)
    ppermute x37, waiting for transfers between devices, send(): return lax.ppermute(value, ('section', 'rep'), pairs)  81 us
    ppermute x37, starting transfers between devices, send(): return lax.ppermute(value, ('section', 'rep'), pairs)  55.7 us
    pallas_call x3, Pallas kernels, run(): pl.pallas_call(kernel, grid=(steps,), in_specs=in_specs, out_shape=outs,...  20.8 us
    unnamed x33, local copies, waits for them, and re-layouts  7.45 us
  transfers between devices with their start and end apart: 37, of which 20 were waited for; matrix products, arithmetic and copies ran while one was open for 4% of the time, Pallas kernels for 3%

profile of v1, /device:TPU:8, one launch (start us, length us, event | category | flops | bytes accessed | tf_op | source)
XLA Modules:
  0.0 176.9 jit_solution(10249273877883471681)
XLA Ops:
  3.4 7.3 %collective-permute-start.4 = (bf16[4,4096]{1,0:T(4,128)(2,1)S(1)}, bf16[4,4096]{1,0:T(4,128)(2,1)S(1)}, u32[]{:S(2)}, u32[]{:S(2)}) collective-permute-start(bf16[4,4096]{1,0:T(4,128)(2,1)S(1)} %get-tuple-element.65), channel_id=1, source_target_pairs={{0,128},{1,129},{2,130},{3,131},{4,132},{5,133},{6,134},{7,135},{8... | collective-permute-start | bytes 98312 | tf_op jit(solution)/shard_map/ppermute | solution.py:39
  10.6 2.3 %collective-permute-start = (bf16[8,4096]{1,0:T(8,128)(2,1)}, bf16[8,4096]{1,0:T(8,128)(2,1)S(1)}, u32[]{:S(2)}, u32[]{:S(2)}) collective-permute-start(bf16[8,4096]{1,0:T(8,128)(2,1)} %bitcast.44), channel_id=1, source_target_pairs={{0,224},{1,225},{2,226},{3,227},{4,228},{5,229},{6,230},{7,231},{8... | collective-permute-start | bytes 196616 | tf_op jit(solution)/shard_map/ppermute | solution.py:39
  16.5 3.2 %collective-permute-done.5 = bf16[8,4096]{1,0:T(8,128)(2,1)S(1)} collective-permute-done((bf16[8,4096]{1,0:T(8,128)(2,1)S(1)}, bf16[8,4096]{1,0:T(8,128)(2,1)S(1)}, u32[]{:S(2)}, u32[]{:S(2)}) %collective-permute-start.5) | collective-permute-done | bytes 65568 | tf_op jit(solution)/shard_map/ppermute | solution.py:39
  20.3 2.6 %collective-permute-start.7 = (bf16[16,4096]{1,0:T(8,128)(2,1)S(1)}, bf16[16,4096]{1,0:T(8,128)(2,1)S(1)}, u32[]{:S(2)}, u32[]{:S(2)}) collective-permute-start(bf16[16,4096]{1,0:T(8,128)(2,1)S(1)} %pad_maximum_fusion.1), channel_id=1, source_target_pairs={{0,4},{1,5},{2,6},{3,7},{4,0},{5,1},{6,2},{7,3},{8,12},{9,13},{10,... | collective-permute-start | bytes 393224 | tf_op jit(solution)/shard_map/ppermute | solution.py:39
  22.9 1.9 %collective-permute-start.8 = (bf16[16,4096]{1,0:T(8,128)(2,1)S(1)}, bf16[16,4096]{1,0:T(8,128)(2,1)S(1)}, u32[]{:S(2)}, u32[]{:S(2)}) collective-permute-start(bf16[16,4096]{1,0:T(8,128)(2,1)S(1)} %pad_maximum_fusion.1), channel_id=1, source_target_pairs={{0,2},{1,3},{2,4},{3,5},{4,6},{5,7},{6,0},{7,1},{8,10},{9,11},{10,... | collective-permute-start | bytes 393224 | tf_op jit(solution)/shard_map/ppermute | solution.py:39
  24.8 1.9 %collective-permute-start.2 = (bf16[12,4096]{1,0:T(8,128)(2,1)S(1)}, bf16[12,4096]{1,0:T(8,128)(2,1)S(1)}, u32[]{:S(2)}, u32[]{:S(2)}) collective-permute-start(bf16[12,4096]{1,0:T(8,128)(2,1)S(1)} %pad_maximum_fusion), channel_id=1, source_target_pairs={{0,16},{1,17},{2,18},{3,19},{4,20},{5,21},{6,22},{7,23},{8,24},{9,... | collective-permute-start | bytes 294920 | tf_op jit(solution)/shard_map/ppermute | solution.py:39
  28.4 6.7 %collective-permute-done.2 = bf16[12,4096]{1,0:T(8,128)(2,1)S(1)} collective-permute-done((bf16[12,4096]{1,0:T(8,128)(2,1)S(1)}, bf16[12,4096]{1,0:T(8,128)(2,1)S(1)}, u32[]{:S(2)}, u32[]{:S(2)}) %collective-permute-start.2) | collective-permute-done | bytes 98336 | tf_op jit(solution)/shard_map/ppermute | solution.py:39
  37.4 2.4 %collective-permute-start.14 = (bf16[48,4096]{1,0:T(8,128)(2,1)S(1)}, bf16[48,4096]{1,0:T(8,128)(2,1)S(1)}, u32[]{:S(2)}, u32[]{:S(2)}) collective-permute-start(bf16[48,4096]{1,0:T(8,128)(2,1)S(1)} %concatenate.46.refs_2_), channel_id=1, source_target_pairs={{0,2},{1,3},{2,4},{3,5},{4,6},{5,7},{6,0},{7,1},{8,10},{9,11},{10,... | collective-permute-start | bytes 1179656 | tf_op jit(solution)/shard_map/ppermute | solution.py:39
  41.2 2.8 %collective-permute-start.9 = (bf16[64,4096]{1,0:T(8,128)(2,1)S(1)}, bf16[64,4096]{1,0:T(8,128)(2,1)S(1)}, u32[]{:S(2)}, u32[]{:S(2)}) collective-permute-start(bf16[64,4096]{1,0:T(8,128)(2,1)S(1)} %concatenate.49.refs_0_), channel_id=1, source_target_pairs={{0,16},{1,17},{2,18},{3,19},{4,20},{5,21},{6,22},{7,23},{8,24},{9,... | collective-permute-start | bytes 1572872 | tf_op jit(solution)/shard_map/ppermute | solution.py:39
  44.0 6.1 %collective-permute-done.12.refs_3_ = bf16[48,4096]{1,0:T(8,128)(2,1)S(1)} collective-permute-done((bf16[48,4096]{1,0:T(8,128)(2,1)S(1)}, bf16[48,4096]{1,0:T(8,128)(2,1)S(1)}, u32[]{:S(2)}, u32[]{:S(2)}) %collective-permute-start.12) | collective-permute-done | bytes 393248 | tf_op jit(solution)/shard_map/ppermute | solution.py:39
  53.2 11.4 %collective-permute-done.9.refs_1_ = bf16[64,4096]{1,0:T(8,128)(2,1)S(1)} collective-permute-done((bf16[64,4096]{1,0:T(8,128)(2,1)S(1)}, bf16[64,4096]{1,0:T(8,128)(2,1)S(1)}, u32[]{:S(2)}, u32[]{:S(2)}) %collective-permute-start.9) | collective-permute-done | bytes 524320 | tf_op jit(solution)/shard_map/ppermute | solution.py:39
  65.6 2.0 %copy-done.1 = bf16[1,4096,448]{1,2,0:T(8,128)(2,1)S(1)} copy-done((bf16[1,4096,448]{1,2,0:T(8,128)(2,1)S(1)}, bf16[1,4096,448]{1,2,0:T(8,128)(2,1)}, u32[]{:S(2)}) %copy-start.1) | copy-done | bytes 3670040
  71.6 12.9 %first.1 = (bf16[128,4096]{1,0:T(8,128)(2,1)S(1)}, bf16[128,4096]{1,0:T(8,128)(2,1)S(1)}, bf16[128,448]{1,0:T(8,128)(2,1)S(1)}, bf16[128,448]{1,0:T(8,128)(2,1)S...) custom-call(bf16[256,384]{1,0:T(8,128)(2,1)S(1)} %copy.14.refs_0_, ...), custom_call_target="tpu_custom_call" | custom-call | flops 4227858432 | bytes 14680064 | tf_op jit(solution)/shard_map/first/pallas_call | solution.py:223
  85.2 3.5 %collective-permute-done.10.refs_2_ = bf16[64,4096]{1,0:T(8,128)(2,1)S(1)} collective-permute-done((bf16[64,4096]{1,0:T(8,128)(2,1)S(1)}, bf16[64,4096]{1,0:T(8,128)(2,1)S(1)}, u32[]{:S(2)}, u32[]{:S(2)}) %collective-permute-start.10) | collective-permute-done | bytes 524320 | tf_op jit(solution)/shard_map/ppermute | solution.py:39
  89.5 4.5 %second.1 = (f32[256,448]{1,0:T(8,128)S(1)}, f32[256,448]{1,0:T(8,128)S(1)}, bf16[256,448]{1,0:T(8,128)(2,1)S(1)}, bf16[256,448]{1,0:T(8,128)(2,1)S(1)}) custom-call(bf16[64,4096]{1,0:T(8,128)(2,1)S(1)} %concatenate.49.refs_0_, bf16[64,4096]{1,0:T(8,128)(2,1)S(1)} %collective-permute-done.9.refs_1_, bf16[64,4096]{1,0:T(8,128)(2,1)S(1)} %collective-permute-done.10.refs_2_, ...), custom_call_target="tpu_custom_call" | custom-call | flops 2348810240 | bytes 10715136 | tf_op jit(solution)/shard_map/second/pallas_call | solution.py:223
  95.4 2.0 %collective-permute-start.21 = (bf16[48,4096]{1,0:T(8,128)(2,1)S(1)}, bf16[48,4096]{1,0:T(8,128)(2,1)S(1)}, u32[]{:S(2)}, u32[]{:S(2)}) collective-permute-start(bf16[48,4096]{1,0:T(8,128)(2,1)S(1)} %get-tuple-element.53), channel_id=1, source_target_pairs={{0,4},{1,5},{2,6},{3,7},{4,0},{5,1},{6,2},{7,3},{8,12},{9,13},{10,... | collective-permute-start | bytes 1179656 | tf_op jit(solution)/shard_map/ppermute | solution.py:39
  97.4 2.4 %collective-permute-start.22 = (bf16[48,4096]{1,0:T(8,128)(2,1)S(1)}, bf16[48,4096]{1,0:T(8,128)(2,1)S(1)}, u32[]{:S(2)}, u32[]{:S(2)}) collective-permute-start(bf16[48,4096]{1,0:T(8,128)(2,1)S(1)} %get-tuple-element.52), channel_id=1, source_target_pairs={{0,6},{1,7},{2,0},{3,1},{4,2},{5,3},{6,4},{7,5},{8,14},{9,15},{10,... | collective-permute-start | bytes 1179656 | tf_op jit(solution)/shard_map/ppermute | solution.py:39
  99.7 7.6 %collective-permute-start.23 = (bf16[256,448]{1,0:T(8,128)(2,1)S(1)}, bf16[256,448]{1,0:T(8,128)(2,1)S(1)}, u32[]{:S(2)}, u32[]{:S(2)}) collective-permute-start(bf16[256,448]{1,0:T(8,128)(2,1)S(1)} %get-tuple-element.39), channel_id=1, source_target_pairs={{0,128},{1,129},{2,130},{3,131},{4,132},{5,133},{6,134},{7,135},{8... | collective-permute-start | bytes 688136 | tf_op jit(solution)/shard_map/ppermute | solution.py:39
  108.9 7.3 %collective-permute-done.22 = bf16[48,4096]{1,0:T(8,128)(2,1)S(1)} collective-permute-done((bf16[48,4096]{1,0:T(8,128)(2,1)S(1)}, bf16[48,4096]{1,0:T(8,128)(2,1)S(1)}, u32[]{:S(2)}, u32[]{:S(2)}) %collective-permute-start.22) | collective-permute-done | bytes 393248 | tf_op jit(solution)/shard_map/ppermute | solution.py:39
  116.4 7.3 %collective-permute-done.23.mate_gate = bf16[256,448]{1,0:T(8,128)(2,1)S(1)} collective-permute-done((bf16[256,448]{1,0:T(8,128)(2,1)S(1)}, bf16[256,448]{1,0:T(8,128)(2,1)S(1)}, u32[]{:S(2)}, u32[]{:S(2)}) %collective-permute-start.23) | collective-permute-done | bytes 229408 | tf_op jit(solution)/shard_map/ppermute | solution.py:39
  123.7 6.4 %collective-permute-done.24.mate_up = bf16[256,448]{1,0:T(8,128)(2,1)S(1)} collective-permute-done((bf16[256,448]{1,0:T(8,128)(2,1)S(1)}, bf16[256,448]{1,0:T(8,128)(2,1)S(1)}, u32[]{:S(2)}, u32[]{:S(2)}) %collective-permute-start.24) | collective-permute-done | bytes 229408 | tf_op jit(solution)/shard_map/ppermute | solution.py:39
  130.1 3.3 %third.1 = (bf16[128,4096]{1,0:T(8,128)(2,1)S(1)}, bf16[128,4096]{1,0:T(8,128)(2,1)S(1)}) custom-call(f32[256,448]{1,0:T(8,128)S(1)} %get-tuple-element.43.gate, f32[256,448]{1,0:T(8,128)S(1)} %get-tuple-element.44.up, bf16[256,448]{1,0:T(8,128)(2,1)S(1)} %collective-permute-done.23.mate_gate, bf16[256,448]{1,0:T(8,128)(2,1)S(1)} %collective-permute-done.24.mate_up, ...), custom_call_target="tpu_custom_call" | custom-call | flops 1409286144 | bytes 6209536 | tf_op jit(solution)/shard_map/third/pallas_call | solution.py:223
  133.5 2.6 %collective-permute-done.25 = bf16[128,4096]{1,0:T(8,128)(2,1)S(1)} collective-permute-done((bf16[128,4096]{1,0:T(8,128)(2,1)S(1)}, bf16[128,4096]{1,0:T(8,128)(2,1)S(1)}, u32[]{:S(2)}, u32[]{:S(2)}) %collective-permute-start.25) | collective-permute-done | bytes 1048608 | tf_op jit(solution)/shard_map/ppermute | solution.py:39
  138.1 2.9 %collective-permute-start.28 = (bf16[12,4096]{1,0:T(8,128)(2,1)S(1)}, bf16[12,4096]{1,0:T(8,128)(2,1)S(1)}, u32[]{:S(2)}, u32[]{:S(2)}) collective-permute-start(bf16[12,4096]{1,0:T(8,128)(2,1)S(1)} %get-tuple-element.58), channel_id=1, source_target_pairs={{0,24},{1,25},{2,26},{3,27},{4,28},{5,29},{6,30},{7,31},{8,16},{9,... | collective-permute-start | bytes 294920 | tf_op jit(solution)/shard_map/ppermute | solution.py:39
  141.2 2.4 %collective-permute-start.31 = (bf16[32,4096]{1,0:T(8,128)(2,1)S(1)}, bf16[32,4096]{1,0:T(8,128)(2,1)S(1)}, u32[]{:S(2)}, u32[]{:S(2)}) collective-permute-start(bf16[32,4096]{1,0:T(8,128)(2,1)S(1)} %get-tuple-element.56), channel_id=1, source_target_pairs={{0,4},{1,5},{2,6},{3,7},{4,0},{5,1},{6,2},{7,3},{8,12},{9,13},{10,... | collective-permute-start | bytes 786440 | tf_op jit(solution)/shard_map/ppermute | solution.py:39
  143.8 6.0 %collective-permute-done.27 = bf16[12,4096]{1,0:T(8,128)(2,1)S(1)} collective-permute-done((bf16[12,4096]{1,0:T(8,128)(2,1)S(1)}, bf16[12,4096]{1,0:T(8,128)(2,1)S(1)}, u32[]{:S(2)}, u32[]{:S(2)}) %collective-permute-start.27) | collective-permute-done | bytes 98336 | tf_op jit(solution)/shard_map/ppermute | solution.py:39
  152.1 3.8 %collective-permute-done.32 = bf16[32,4096]{1,0:T(8,128)(2,1)S(1)} collective-permute-done((bf16[32,4096]{1,0:T(8,128)(2,1)S(1)}, bf16[32,4096]{1,0:T(8,128)(2,1)S(1)}, u32[]{:S(2)}, u32[]{:S(2)}) %collective-permute-start.32) | collective-permute-done | bytes 262176 | tf_op jit(solution)/shard_map/ppermute | solution.py:39
  156.0 2.9 %collective-permute-start.33 = (bf16[16,4096]{1,0:T(8,128)(2,1)S(1)}, bf16[16,4096]{1,0:T(8,128)(2,1)S(1)}, u32[]{:S(2)}, u32[]{:S(2)}) collective-permute-start(bf16[16,4096]{1,0:T(8,128)(2,1)S(1)} %broadcast_select_fusion), channel_id=1, source_target_pairs={{0,128},{1,129},{2,130},{3,131},{4,132},{5,133},{6,134},{7,135},{8... | collective-permute-start | bytes 393224 | tf_op jit(solution)/shard_map/ppermute | solution.py:39
  159.0 8.6 %collective-permute-done.33 = bf16[16,4096]{1,0:T(8,128)(2,1)S(1)} collective-permute-done((bf16[16,4096]{1,0:T(8,128)(2,1)S(1)}, bf16[16,4096]{1,0:T(8,128)(2,1)S(1)}, u32[]{:S(2)}, u32[]{:S(2)}) %collective-permute-start.33) | collective-permute-done | bytes 131104 | tf_op jit(solution)/shard_map/ppermute | solution.py:39
  167.9 2.0 %collective-permute-start.35 = (bf16[4,4096]{1,0:T(4,128)(2,1)S(1)}, bf16[4,4096]{1,0:T(4,128)(2,1)S(1)}, u32[]{:S(2)}, u32[]{:S(2)}) collective-permute-start(bf16[4,4096]{1,0:T(4,128)(2,1)S(1)} %get-tuple-element.62), channel_id=1, source_target_pairs={{0,16},{1,17},{2,18},{3,19},{4,20},{5,21},{6,22},{7,23},{8,24},{9,... | collective-permute-start | bytes 98312 | tf_op jit(solution)/shard_map/ppermute | solution.py:39
  169.9 2.3 %collective-permute-start.36 = (bf16[4,4096]{1,0:T(4,128)(2,1)S(1)}, bf16[4,4096]{1,0:T(4,128)(2,1)S(1)}, u32[]{:S(2)}, u32[]{:S(2)}) collective-permute-start(bf16[4,4096]{1,0:T(4,128)(2,1)S(1)} %get-tuple-element.61), channel_id=1, source_target_pairs={{0,24},{1,25},{2,26},{3,27},{4,28},{5,29},{6,30},{7,31},{8,16},{9,... | collective-permute-start | bytes 98312 | tf_op jit(solution)/shard_map/ppermute | solution.py:39
  173.4 2.2 %collective-permute-done.36 = bf16[4,4096]{1,0:T(4,128)(2,1)S(1)} collective-permute-done((bf16[4,4096]{1,0:T(4,128)(2,1)S(1)}, bf16[4,4096]{1,0:T(4,128)(2,1)S(1)}, u32[]{:S(2)}, u32[]{:S(2)}) %collective-permute-start.36) | collective-permute-done | bytes 32800 | tf_op jit(solution)/shard_map/ppermute | solution.py:39
  (120 shorter events, 32.4 us)
Async XLA Ops:
  3.4 10.5 %collective-permute-start.4 = (bf16[4,4096]{1,0:T(4,128)(2,1)S(1)}, bf16[4,4096]{1,0:T(4,128)(2,1)S(1)}, u32[]{:S(2)}, u32[]{:S(2)}) collective-permute-start(bf16[4,4096]{1,0:T(4,128)(2,1)S(1)} %get-tuple-element.65), channel_id=1, source_target_pairs={{0,128},{1,129},{2,130},{3,131},{4,132},{5,133},{6,134},{7,135},{8... | collective-permute-start | bytes 98312 | tf_op jit(solution)/shard_map/ppermute | solution.py:39
  13.9 5.8 %collective-permute-start.5 = (bf16[8,4096]{1,0:T(8,128)(2,1)S(1)}, bf16[8,4096]{1,0:T(8,128)(2,1)S(1)}, u32[]{:S(2)}, u32[]{:S(2)}) collective-permute-start(bf16[8,4096]{1,0:T(8,128)(2,1)S(1)} %pad_maximum_fusion.2), channel_id=1, source_target_pairs={{0,8},{1,9},{2,10},{3,11},{4,12},{5,13},{6,14},{7,15},{8,0},{9,1},... | collective-permute-start | bytes 196616 | tf_op jit(solution)/shard_map/ppermute | solution.py:39
  15.3 11.4 %collective-permute-start.1 = (bf16[12,4096]{1,0:T(8,128)(2,1)S(1)}, bf16[12,4096]{1,0:T(8,128)(2,1)S(1)}, u32[]{:S(2)}, u32[]{:S(2)}) collective-permute-start(bf16[12,4096]{1,0:T(8,128)(2,1)S(1)} %pad_maximum_fusion), channel_id=1, source_target_pairs={{0,8},{1,9},{2,10},{3,11},{4,12},{5,13},{6,14},{7,15},{8,0},{9,1},... | collective-permute-start | bytes 294920 | tf_op jit(solution)/shard_map/ppermute | solution.py:39
  19.8 15.9 %collective-permute-start.6 = (bf16[16,4096]{1,0:T(8,128)(2,1)S(1)}, bf16[16,4096]{1,0:T(8,128)(2,1)S(1)}, u32[]{:S(2)}, u32[]{:S(2)}) collective-permute-start(bf16[16,4096]{1,0:T(8,128)(2,1)S(1)} %pad_maximum_fusion.1), channel_id=1, source_target_pairs={{0,6},{1,7},{2,0},{3,1},{4,2},{5,3},{6,4},{7,5},{8,14},{9,15},{10,... | collective-permute-start | bytes 393224 | tf_op jit(solution)/shard_map/ppermute | solution.py:39
  20.3 15.4 %collective-permute-start.7 = (bf16[16,4096]{1,0:T(8,128)(2,1)S(1)}, bf16[16,4096]{1,0:T(8,128)(2,1)S(1)}, u32[]{:S(2)}, u32[]{:S(2)}) collective-permute-start(bf16[16,4096]{1,0:T(8,128)(2,1)S(1)} %pad_maximum_fusion.1), channel_id=1, source_target_pairs={{0,4},{1,5},{2,6},{3,7},{4,0},{5,1},{6,2},{7,3},{8,12},{9,13},{10,... | collective-permute-start | bytes 393224 | tf_op jit(solution)/shard_map/ppermute | solution.py:39
  22.9 12.8 %collective-permute-start.8 = (bf16[16,4096]{1,0:T(8,128)(2,1)S(1)}, bf16[16,4096]{1,0:T(8,128)(2,1)S(1)}, u32[]{:S(2)}, u32[]{:S(2)}) collective-permute-start(bf16[16,4096]{1,0:T(8,128)(2,1)S(1)} %pad_maximum_fusion.1), channel_id=1, source_target_pairs={{0,2},{1,3},{2,4},{3,5},{4,6},{5,7},{6,0},{7,1},{8,10},{9,11},{10,... | collective-permute-start | bytes 393224 | tf_op jit(solution)/shard_map/ppermute | solution.py:39
  24.8 10.2 %collective-permute-start.2 = (bf16[12,4096]{1,0:T(8,128)(2,1)S(1)}, bf16[12,4096]{1,0:T(8,128)(2,1)S(1)}, u32[]{:S(2)}, u32[]{:S(2)}) collective-permute-start(bf16[12,4096]{1,0:T(8,128)(2,1)S(1)} %pad_maximum_fusion), channel_id=1, source_target_pairs={{0,16},{1,17},{2,18},{3,19},{4,20},{5,21},{6,22},{7,23},{8,24},{9,... | collective-permute-start | bytes 294920 | tf_op jit(solution)/shard_map/ppermute | solution.py:39
  26.8 8.3 %collective-permute-start.3 = (bf16[12,4096]{1,0:T(8,128)(2,1)S(1)}, bf16[12,4096]{1,0:T(8,128)(2,1)S(1)}, u32[]{:S(2)}, u32[]{:S(2)}) collective-permute-start(bf16[12,4096]{1,0:T(8,128)(2,1)S(1)} %pad_maximum_fusion), channel_id=1, source_target_pairs={{0,24},{1,25},{2,26},{3,27},{4,28},{5,29},{6,30},{7,31},{8,16},{9,... | collective-permute-start | bytes 294920 | tf_op jit(solution)/shard_map/ppermute | solution.py:39
  35.8 14.2 %collective-permute-start.12 = (bf16[48,4096]{1,0:T(8,128)(2,1)S(1)}, bf16[48,4096]{1,0:T(8,128)(2,1)S(1)}, u32[]{:S(2)}, u32[]{:S(2)}) collective-permute-start(bf16[48,4096]{1,0:T(8,128)(2,1)S(1)} %concatenate.46.refs_2_), channel_id=1, source_target_pairs={{0,6},{1,7},{2,0},{3,1},{4,2},{5,3},{6,4},{7,5},{8,14},{9,15},{10,... | collective-permute-start | bytes 1179656 | tf_op jit(solution)/shard_map/ppermute | solution.py:39
  36.1 14.0 %collective-permute-start.13 = (bf16[48,4096]{1,0:T(8,128)(2,1)S(1)}, bf16[48,4096]{1,0:T(8,128)(2,1)S(1)}, u32[]{:S(2)}, u32[]{:S(2)}) collective-permute-start(bf16[48,4096]{1,0:T(8,128)(2,1)S(1)} %concatenate.46.refs_2_), channel_id=1, source_target_pairs={{0,4},{1,5},{2,6},{3,7},{4,0},{5,1},{6,2},{7,3},{8,12},{9,13},{10,... | collective-permute-start | bytes 1179656 | tf_op jit(solution)/shard_map/ppermute | solution.py:39
  37.4 14.0 %collective-permute-start.14 = (bf16[48,4096]{1,0:T(8,128)(2,1)S(1)}, bf16[48,4096]{1,0:T(8,128)(2,1)S(1)}, u32[]{:S(2)}, u32[]{:S(2)}) collective-permute-start(bf16[48,4096]{1,0:T(8,128)(2,1)S(1)} %concatenate.46.refs_2_), channel_id=1, source_target_pairs={{0,2},{1,3},{2,4},{3,5},{4,6},{5,7},{6,0},{7,1},{8,10},{9,11},{10,... | collective-permute-start | bytes 1179656 | tf_op jit(solution)/shard_map/ppermute | solution.py:39
  41.2 23.4 %collective-permute-start.9 = (bf16[64,4096]{1,0:T(8,128)(2,1)S(1)}, bf16[64,4096]{1,0:T(8,128)(2,1)S(1)}, u32[]{:S(2)}, u32[]{:S(2)}) collective-permute-start(bf16[64,4096]{1,0:T(8,128)(2,1)S(1)} %concatenate.49.refs_0_), channel_id=1, source_target_pairs={{0,16},{1,17},{2,18},{3,19},{4,20},{5,21},{6,22},{7,23},{8,24},{9,... | collective-permute-start | bytes 1572872 | tf_op jit(solution)/shard_map/ppermute | solution.py:39
  44.0 20.8 %collective-permute-start.15 = (bf16[48,4096]{1,0:T(8,128)(2,1)S(1)}, bf16[48,4096]{1,0:T(8,128)(2,1)S(1)}, u32[]{:S(2)}, u32[]{:S(2)}) collective-permute-start(bf16[48,4096]{1,0:T(8,128)(2,1)S(1)} %concatenate.46.refs_2_), channel_id=1, source_target_pairs={{0,1},{1,0},{2,3},{3,2},{4,5},{5,4},{6,7},{7,6},{8,9},{9,8},{10,11... | collective-permute-start | bytes 1179656 | tf_op jit(solution)/shard_map/ppermute | solution.py:39
  50.1 15.5 %collective-permute-start.16 = (bf16[48,4096]{1,0:T(8,128)(2,1)S(1)}, bf16[48,4096]{1,0:T(8,128)(2,1)}, u32[]{:S(2)}, u32[]{:S(2)}) collective-permute-start(bf16[48,4096]{1,0:T(8,128)(2,1)S(1)} %collective-permute-done.12.refs_3_), channel_id=1, source_target_pairs={{0,1},{1,0},{2,3},{3,2},{4,5},{5,4},{6,7},{7,6},{8,9},{9,8},{10,11... | collective-permute-start | bytes 1179656 | tf_op jit(solution)/shard_map/ppermute | solution.py:39
  50.1 15.5 %collective-permute-start.17 = (bf16[48,4096]{1,0:T(8,128)(2,1)S(1)}, bf16[48,4096]{1,0:T(8,128)(2,1)}, u32[]{:S(2)}, u32[]{:S(2)}) collective-permute-start(bf16[48,4096]{1,0:T(8,128)(2,1)S(1)} %collective-permute-done.13.refs_4_), channel_id=1, source_target_pairs={{0,1},{1,0},{2,3},{3,2},{4,5},{5,4},{6,7},{7,6},{8,9},{9,8},{10,11... | collective-permute-start | bytes 1179656 | tf_op jit(solution)/shard_map/ppermute | solution.py:39
  51.4 14.1 %collective-permute-start.18 = (bf16[48,4096]{1,0:T(8,128)(2,1)S(1)}, bf16[48,4096]{1,0:T(8,128)(2,1)}, u32[]{:S(2)}, u32[]{:S(2)}) collective-permute-start(bf16[48,4096]{1,0:T(8,128)(2,1)S(1)} %collective-permute-done.14.refs_5_), channel_id=1, source_target_pairs={{0,1},{1,0},{2,3},{3,2},{4,5},{5,4},{6,7},{7,6},{8,9},{9,8},{10,11... | collective-permute-start | bytes 1179656 | tf_op jit(solution)/shard_map/ppermute | solution.py:39
  84.5 9.5 %collective-permute-start.19 = (bf16[192,4096]{1,0:T(8,128)(2,1)S(1)}, bf16[192,4096]{1,0:T(8,128)(2,1)S(1)}, u32[]{:S(2)}, u32[]{:S(2)}) collective-permute-start(bf16[192,4096]{1,0:T(8,128)(2,1)S(1)} %get-tuple-element.38), channel_id=1, source_target_pairs={{0,1},{1,0},{2,3},{3,2},{4,5},{5,4},{6,7},{7,6},{8,9},{9,8},{10,11... | collective-permute-start | bytes 4718600 | tf_op jit(solution)/shard_map/ppermute | solution.py:39
  94.7 12.6 %collective-permute-start.20 = (bf16[48,4096]{1,0:T(8,128)(2,1)S(1)}, bf16[48,4096]{1,0:T(8,128)(2,1)S(1)}, u32[]{:S(2)}, u32[]{:S(2)}) collective-permute-start(bf16[48,4096]{1,0:T(8,128)(2,1)S(1)} %get-tuple-element.51), channel_id=1, source_target_pairs={{0,2},{1,3},{2,4},{3,5},{4,6},{5,7},{6,0},{7,1},{8,10},{9,11},{10,... | collective-permute-start | bytes 1179656 | tf_op jit(solution)/shard_map/ppermute | solution.py:39
  95.4 13.6 %collective-permute-start.21 = (bf16[48,4096]{1,0:T(8,128)(2,1)S(1)}, bf16[48,4096]{1,0:T(8,128)(2,1)S(1)}, u32[]{:S(2)}, u32[]{:S(2)}) collective-permute-start(bf16[48,4096]{1,0:T(8,128)(2,1)S(1)} %get-tuple-element.53), channel_id=1, source_target_pairs={{0,4},{1,5},{2,6},{3,7},{4,0},{5,1},{6,2},{7,3},{8,12},{9,13},{10,... | collective-permute-start | bytes 1179656 | tf_op jit(solution)/shard_map/ppermute | solution.py:39
  97.4 18.8 %collective-permute-start.22 = (bf16[48,4096]{1,0:T(8,128)(2,1)S(1)}, bf16[48,4096]{1,0:T(8,128)(2,1)S(1)}, u32[]{:S(2)}, u32[]{:S(2)}) collective-permute-start(bf16[48,4096]{1,0:T(8,128)(2,1)S(1)} %get-tuple-element.52), channel_id=1, source_target_pairs={{0,6},{1,7},{2,0},{3,1},{4,2},{5,3},{6,4},{7,5},{8,14},{9,15},{10,... | collective-permute-start | bytes 1179656 | tf_op jit(solution)/shard_map/ppermute | solution.py:39
  99.7 24.0 %collective-permute-start.23 = (bf16[256,448]{1,0:T(8,128)(2,1)S(1)}, bf16[256,448]{1,0:T(8,128)(2,1)S(1)}, u32[]{:S(2)}, u32[]{:S(2)}) collective-permute-start(bf16[256,448]{1,0:T(8,128)(2,1)S(1)} %get-tuple-element.39), channel_id=1, source_target_pairs={{0,128},{1,129},{2,130},{3,131},{4,132},{5,133},{6,134},{7,135},{8... | collective-permute-start | bytes 688136 | tf_op jit(solution)/shard_map/ppermute | solution.py:39
  107.3 22.8 %collective-permute-start.24 = (bf16[256,448]{1,0:T(8,128)(2,1)S(1)}, bf16[256,448]{1,0:T(8,128)(2,1)S(1)}, u32[]{:S(2)}, u32[]{:S(2)}) collective-permute-start(bf16[256,448]{1,0:T(8,128)(2,1)S(1)} %get-tuple-element.40), channel_id=1, source_target_pairs={{0,128},{1,129},{2,130},{3,131},{4,132},{5,133},{6,134},{7,135},{8... | collective-permute-start | bytes 688136 | tf_op jit(solution)/shard_map/ppermute | solution.py:39
  136.5 7.1 %collective-permute-start.26 = (bf16[12,4096]{1,0:T(8,128)(2,1)S(1)}, bf16[12,4096]{1,0:T(8,128)(2,1)S(1)}, u32[]{:S(2)}, u32[]{:S(2)}) collective-permute-start(bf16[12,4096]{1,0:T(8,128)(2,1)S(1)} %get-tuple-element.57), channel_id=1, source_target_pairs={{0,8},{1,9},{2,10},{3,11},{4,12},{5,13},{6,14},{7,15},{8,0},{9,1},... | collective-permute-start | bytes 294920 | tf_op jit(solution)/shard_map/ppermute | solution.py:39
  136.6 13.2 %collective-permute-start.27 = (bf16[12,4096]{1,0:T(8,128)(2,1)S(1)}, bf16[12,4096]{1,0:T(8,128)(2,1)S(1)}, u32[]{:S(2)}, u32[]{:S(2)}) collective-permute-start(bf16[12,4096]{1,0:T(8,128)(2,1)S(1)} %get-tuple-element.59), channel_id=1, source_target_pairs={{0,16},{1,17},{2,18},{3,19},{4,20},{5,21},{6,22},{7,23},{8,24},{9,... | collective-permute-start | bytes 294920 | tf_op jit(solution)/shard_map/ppermute | solution.py:39
  138.1 11.7 %collective-permute-start.28 = (bf16[12,4096]{1,0:T(8,128)(2,1)S(1)}, bf16[12,4096]{1,0:T(8,128)(2,1)S(1)}, u32[]{:S(2)}, u32[]{:S(2)}) collective-permute-start(bf16[12,4096]{1,0:T(8,128)(2,1)S(1)} %get-tuple-element.58), channel_id=1, source_target_pairs={{0,24},{1,25},{2,26},{3,27},{4,28},{5,29},{6,30},{7,31},{8,16},{9,... | collective-permute-start | bytes 294920 | tf_op jit(solution)/shard_map/ppermute | solution.py:39
  141.1 9.3 %collective-permute-start.30 = (bf16[32,4096]{1,0:T(8,128)(2,1)S(1)}, bf16[32,4096]{1,0:T(8,128)(2,1)S(1)}, u32[]{:S(2)}, u32[]{:S(2)}) collective-permute-start(bf16[32,4096]{1,0:T(8,128)(2,1)S(1)} %get-tuple-element.54), channel_id=1, source_target_pairs={{0,2},{1,3},{2,4},{3,5},{4,6},{5,7},{6,0},{7,1},{8,10},{9,11},{10,... | collective-permute-start | bytes 786440 | tf_op jit(solution)/shard_map/ppermute | solution.py:39
  141.2 10.9 %collective-permute-start.31 = (bf16[32,4096]{1,0:T(8,128)(2,1)S(1)}, bf16[32,4096]{1,0:T(8,128)(2,1)S(1)}, u32[]{:S(2)}, u32[]{:S(2)}) collective-permute-start(bf16[32,4096]{1,0:T(8,128)(2,1)S(1)} %get-tuple-element.56), channel_id=1, source_target_pairs={{0,4},{1,5},{2,6},{3,7},{4,0},{5,1},{6,2},{7,3},{8,12},{9,13},{10,... | collective-permute-start | bytes 786440 | tf_op jit(solution)/shard_map/ppermute | solution.py:39
  143.6 12.3 %collective-permute-start.32 = (bf16[32,4096]{1,0:T(8,128)(2,1)S(1)}, bf16[32,4096]{1,0:T(8,128)(2,1)S(1)}, u32[]{:S(2)}, u32[]{:S(2)}) collective-permute-start(bf16[32,4096]{1,0:T(8,128)(2,1)S(1)} %get-tuple-element.55), channel_id=1, source_target_pairs={{0,6},{1,7},{2,0},{3,1},{4,2},{5,3},{6,4},{7,5},{8,14},{9,15},{10,... | collective-permute-start | bytes 786440 | tf_op jit(solution)/shard_map/ppermute | solution.py:39
  149.9 23.0 %collective-permute-start.29 = (bf16[8,4096]{1,0:T(8,128)(2,1)S(1)}, bf16[8,4096]{1,0:T(8,128)(2,1)S(1)}, u32[]{:S(2)}, u32[]{:S(2)}) collective-permute-start(bf16[8,4096]{1,0:T(8,128)(2,1)S(1)} %slice.150), channel_id=1, source_target_pairs={{0,32},{1,33},{2,34},{3,35},{4,36},{5,37},{6,38},{7,39},{8,40},{9,... | collective-permute-start | bytes 196616 | tf_op jit(solution)/shard_map/ppermute | solution.py:39
  156.0 11.6 %collective-permute-start.33 = (bf16[16,4096]{1,0:T(8,128)(2,1)S(1)}, bf16[16,4096]{1,0:T(8,128)(2,1)S(1)}, u32[]{:S(2)}, u32[]{:S(2)}) collective-permute-start(bf16[16,4096]{1,0:T(8,128)(2,1)S(1)} %broadcast_select_fusion), channel_id=1, source_target_pairs={{0,128},{1,129},{2,130},{3,131},{4,132},{5,133},{6,134},{7,135},{8... | collective-permute-start | bytes 393224 | tf_op jit(solution)/shard_map/ppermute | solution.py:39
  167.9 5.5 %collective-permute-start.35 = (bf16[4,4096]{1,0:T(4,128)(2,1)S(1)}, bf16[4,4096]{1,0:T(4,128)(2,1)S(1)}, u32[]{:S(2)}, u32[]{:S(2)}) collective-permute-start(bf16[4,4096]{1,0:T(4,128)(2,1)S(1)} %get-tuple-element.62), channel_id=1, source_target_pairs={{0,16},{1,17},{2,18},{3,19},{4,20},{5,21},{6,22},{7,23},{8,24},{9,... | collective-permute-start | bytes 98312 | tf_op jit(solution)/shard_map/ppermute | solution.py:39
  169.9 5.7 %collective-permute-start.36 = (bf16[4,4096]{1,0:T(4,128)(2,1)S(1)}, bf16[4,4096]{1,0:T(4,128)(2,1)S(1)}, u32[]{:S(2)}, u32[]{:S(2)}) collective-permute-start(bf16[4,4096]{1,0:T(4,128)(2,1)S(1)} %get-tuple-element.61), channel_id=1, source_target_pairs={{0,24},{1,25},{2,26},{3,27},{4,28},{5,29},{6,30},{7,31},{8,16},{9,... | collective-permute-start | bytes 98312 | tf_op jit(solution)/shard_map/ppermute | solution.py:39
  (21 other events, 245.1 us)

commit v2 on v1

--- a/solution.py
+++ b/solution.py
@@ -18,7 +18,7 @@
 F32 = jnp.float32
 BF16 = jnp.bfloat16
 WIDTH = 1024
-VMEM_LIMIT = 40 << 20
+VMEM_LIMIT = 16 << 20
 
 
 def send(value, ds=0, dz=0, dy=0, dc=0):
@@ -121,26 +121,21 @@
 
 
 def first_kernel(count, *refs):
-    select, spread = refs[:2]
-    blocks = refs[2 : 2 + count]
-    own_rows, gate_w, up_w, down_w = refs[2 + count : 6 + count]
-    cot_out, normed_out, hidden_out, dgate_out, dup_out, mine, other = refs[6 + count : 13 + count]
-    gate_sum, up_sum, dhidden_sum = refs[13 + count :]
-    step, steps = pl.program_id(0), pl.num_programs(0) // 2
+    select, blocks = refs[0], refs[1 : 1 + count]
+    gate_w, up_w, down_w = refs[1 + count : 4 + count]
+    cot_out, normed_out, hidden_out, dgate_out, dup_out = refs[4 + count : 9 + count]
+    gate_sum, up_sum, dhidden_sum = refs[9 + count :]
     tokens = dhidden_sum.shape[0]
-
-    @pl.when(step < steps)
-    def _():
-        chosen = dot(select[...], jnp.concatenate([r[...] for r in blocks], axis=0)).astype(BF16)
-        cotangent, normed = chosen[:tokens], chosen[tokens:]
-        cot_out[...] = cotangent
-        normed_out[...] = normed
-        first = step == 0
-        gate_sum[...] = jnp.where(first, 0.0, gate_sum[...]) + dot_t(normed, gate_w[...])
-        up_sum[...] = jnp.where(first, 0.0, up_sum[...]) + dot_t(normed, up_w[...])
-        dhidden_sum[...] = jnp.where(first, 0.0, dhidden_sum[...]) + dot_t(cotangent, down_w[...])
-
-    @pl.when(step == steps - 1)
+    chosen = dot(select[...], jnp.concatenate([r[...] for r in blocks], axis=0)).astype(BF16)
+    cotangent, normed = chosen[:tokens], chosen[tokens:]
+    cot_out[...] = cotangent
+    normed_out[...] = normed
+    first = pl.program_id(0) == 0
+    gate_sum[...] = jnp.where(first, 0.0, gate_sum[...]) + dot_t(normed, gate_w[...])
+    up_sum[...] = jnp.where(first, 0.0, up_sum[...]) + dot_t(normed, up_w[...])
+    dhidden_sum[...] = jnp.where(first, 0.0, dhidden_sum[...]) + dot_t(cotangent, down_w[...])
+
+    @pl.when(pl.program_id(0) == pl.num_programs(0) - 1)
     def _():
         gate_act, up_act, grad = gate_sum[...], up_sum[...], dhidden_sum[...]
         sigmoid_gate = jax.nn.sigmoid(gate_act)
@@ -151,16 +146,16 @@
         ).astype(BF16)
         dup_out[...] = (grad * silu_gate).astype(BF16)
 
-    @pl.when(step >= steps)
-    def _():
-        top = own_rows.shape[0]
-        term = dot(hidden_out[...], down_w[...])
-        term = jnp.concatenate([term[:top] + own_rows[...], term[top:]], axis=0)
-        dterm = dot(dgate_out[...], gate_w[...]) + dot(dup_out[...], up_w[...])
-        both = jnp.concatenate([term.astype(BF16), dterm.astype(BF16)], axis=0)
-        terms = dot(spread[...], both).astype(BF16)
-        mine[...] = terms[: mine.shape[0]]
-        other[...] = terms[mine.shape[0] :]
+
+def terms_kernel(spread, hidden, dgate, dup, own_rows, gate_w, up_w, down_w, mine, other):
+    top = own_rows.shape[0]
+    term = dot(hidden[...], down_w[...])
+    term = jnp.concatenate([term[:top] + own_rows[...], term[top:]], axis=0)
+    dterm = dot(dgate[...], gate_w[...]) + dot(dup[...], up_w[...])
+    both = jnp.concatenate([term.astype(BF16), dterm.astype(BF16)], axis=0)
+    terms = dot(spread[...], both).astype(BF16)
+    mine[...] = terms[: mine.shape[0]]
+    other[...] = terms[mine.shape[0] :]
 
 
 def second_kernel(count, factor, *refs):
@@ -241,7 +236,10 @@
     capacity = returned.shape[1] // BLK
     token_count = row_count * lax.axis_size("rep")
     gain_row = norm_gain[0]
-    gate_local, up_local, down_local = gate_weight[0].T, up_weight[0].T, down_weight[0]
+    gate_local, up_local, down_local = [
+        pltpu.with_memory_space_constraint(w, pltpu.HBM)
+        for w in (gate_weight[0].T, up_weight[0].T, down_weight[0])
+    ]
     slot_rows = returned[0]
 
     update_factor = step_rate / token_count
@@ -264,6 +262,7 @@
         ],
         axis=0,
     )
+    next_y = after(next_y, shifted)
     next_y = jnp.concatenate([next_y, send(next_y, dz=1)], axis=0)
     next_z = jnp.concatenate([next_y] + [send(next_y, dy=-k) for k in range(1, NY)], axis=0)
     block_z = jnp.concatenate([shifted, normed], axis=0)
@@ -274,8 +273,6 @@
     blocks = [block_y] + [send(block_y, dy=-k) for k in range(1, NY)]
     blocks = blocks + [send(block, dc=1) for block in blocks]
     nexts = [next_z, send(next_z, dz=2)]
-    select, *nexts = lax.optimization_barrier((select, *nexts))
-    nexts = nexts + [send(block, dc=1) for block in nexts]
 
     pair_tokens = 2 * token_count
     part = jax.ShapeDtypeStruct((token_count, units), BF16)
@@ -286,30 +283,34 @@
     per_row = 2 * width * units
     own_rows = jnp.concatenate([values, jnp.zeros_like(values)], axis=0)
 
-    def up_to(i):
-        return jnp.minimum(i, steps - 1)
-
-    def back(i):
-        return steps - 1 - jnp.maximum(i - steps, 0)
-
-    def there_and_back(i):
-        return jnp.minimum(i, 2 * steps - 1 - i)
-
-    cotangent, normed_all, hidden, grad_gate_act, grad_up_act, mine, other = run(
+    cotangent, normed_all, hidden, grad_gate_act, grad_up_act = run(
         functools.partial(first_kernel, len(blocks)),
-        2 * steps,
-        [whole(select.shape), whole(spread.shape)]
-        + [columns(block.shape[0], chunk, up_to) for block in blocks]
-        + [columns(own_rows.shape[0], chunk, back)]
-        + [columns(units, chunk, there_and_back)] * 3,
-        [rows, rows, part, part, part, half, half],
-        [columns(token_count, chunk, up_to)] * 2
+        steps,
+        [whole(select.shape)]
+        + [columns(block.shape[0], chunk) for block in blocks]
+        + [columns(units, chunk)] * 3,
+        [rows, rows, part, part, part],
+        [columns(token_count, chunk)] * 2 + [whole(part.shape)] * 3,
+        [pltpu.VMEM((token_count, units), F32)] * 3,
+        per_row * token_count * 4,
+        "first",
+        [select] + blocks + [gate_local, up_local, down_local],
+    )
+    nexts = nexts + [send(block, dc=1) for block in nexts]
+    spread, *nexts = lax.optimization_barrier((spread, *nexts))
+    mine, other = run(
+        terms_kernel,
+        steps,
+        [whole(spread.shape)]
         + [whole(part.shape)] * 3
-        + [columns(half.shape[0], chunk, back)] * 2,
-        [pltpu.VMEM((token_count, units), F32)] * 3,
-        per_row * token_count * 9,
-        "first",
-        [select, spread] + blocks + [own_rows, gate_local, up_local, down_local],
+        + [columns(own_rows.shape[0], chunk)]
+        + [columns(units, chunk)] * 3,
+        [half, half],
+        [columns(half.shape[0], chunk)] * 2,
+        [],
+        per_row * token_count * 5,
+        "terms",
+        [spread, hidden, grad_gate_act, grad_up_act, own_rows, gate_local, up_local, down_local],
     )
     from_core = send(other, dc=1)
     gate_part, up_part, gate_sent, up_sent = run(
@@ -354,12 +355,12 @@
     forwarded = send(both[: slot_rows.shape[0]].astype(BF16), ds=1)
     dnormed = both[slot_rows.shape[0] :]
     first, second = cut(after(y_sum(pair), both), 2)
-    own_part = jnp.where(first_half, first, second)
-    mate_part = jnp.where(first_half, second, first)
-    pair_sum = add_up([own_part, send(mate_part, ds=half_ring)]).astype(BF16)
-    nparts = cut(pair_sum, NZ)
+    own_parts = cut(jnp.where(first_half, first, second), NZ)
+    mate_parts = cut(jnp.where(first_half, second, first), NZ)
     next_out = add_up(
-        [next_values, nparts[0]] + [send(nparts[k], dz=k) for k in range(1, NZ)]
+        [next_values, own_parts[0]]
+        + [send(mate_parts[k], ds=half_ring, dz=k) for k in range(NZ)]
+        + [send(own_parts[k], dz=k) for k in range(1, NZ)]
     ).astype(BF16)
     scaled_grad = gain_row[None, :] * dnormed
     input_grad = (

time: 178 us -> 173 us (0.972)
  waiting for transfers between devices: 81 us -> 67.9 us
  starting transfers between devices: 55.7 us -> 62.8 us
  local copies, waits for them, and re-layouts: 8.65 us -> 3.6 us
  Pallas kernels: 20.8 us -> 25.5 us
    ppermute x37 -> x40, waiting for transfers between devices: 81 us -> 67.9 us  [send(): return lax.ppermute(value, ('section', 'rep'), pairs)]
    ppermute x37 -> x40, starting transfers between devices: 55.7 us -> 62.8 us  [send(): return lax.ppermute(value, ('section', 'rep'), pairs)]
    unnamed x33 -> x16, local copies, waits for them, and re-layouts: 7.45 us -> 2.43 us
    pallas_call x3 -> x4, Pallas kernels: 20.8 us -> 25.5 us  [run(): pl.pallas_call(kernel, grid=(steps,), in_specs=in_specs, out_shape=outs,...]
  transfers between devices with their start and end apart: 37 -> 40, of which waited for: 20 -> 22; matrix products, arithmetic and copies ran while one was open for 4% -> 5% of each run, Pallas kernels for 3% -> 8%
where the time goes in v2:
time: 173 us; the launch traced here: 171 us
  waiting for transfers between devices  67.9 us (39%)
  starting transfers between devices  62.8 us (36%)
  Pallas kernels  25.5 us (15%)
  other arithmetic  8.09 us (5%)
  local copies, waits for them, and re-layouts  3.6 us (2%)
    ppermute x40, waiting for transfers between devices, send(): return lax.ppermute(value, ('section', 'rep'), pairs)  67.9 us
    ppermute x40, starting transfers between devices, send(): return lax.ppermute(value, ('section', 'rep'), pairs)  62.8 us
    pallas_call x4, Pallas kernels, run(): pl.pallas_call(kernel, grid=(steps,), in_specs=in_specs, out_shape=outs,...  25.5 us
  transfers between devices with their start and end apart: 40, of which 22 were waited for; matrix products, arithmetic and copies ran while one was open for 5% of the time, Pallas kernels for 8%

profile of v2, /device:TPU:8, one launch (start us, length us, event | category | flops | bytes accessed | tf_op | source)
XLA Modules:
  0.0 170.5 jit_solution(13787103474887750665)
XLA Ops:
  0.6 9.5 %collective-permute-start = (bf16[8,4096]{1,0:T(8,128)(2,1)}, bf16[8,4096]{1,0:T(8,128)(2,1)S(1)}, u32[]{:S(2)}, u32[]{:S(2)}) collective-permute-start(bf16[8,4096]{1,0:T(8,128)(2,1)} %bitcast.49), channel_id=1, source_target_pairs={{0,224},{1,225},{2,226},{3,227},{4,228},{5,229},{6,230},{7,231},{8... | collective-permute-start | bytes 196616 | tf_op jit(solution)/shard_map/ppermute | solution.py:39
  13.9 6.8 %collective-permute-done.4 = bf16[4,4096]{1,0:T(4,128)(2,1)S(1)} collective-permute-done((bf16[4,4096]{1,0:T(4,128)(2,1)S(1)}, bf16[4,4096]{1,0:T(4,128)(2,1)S(1)}, u32[]{:S(2)}, u32[]{:S(2)}) %collective-permute-start.4) | collective-permute-done | bytes 32800 | tf_op jit(solution)/shard_map/ppermute | solution.py:39
  22.1 3.1 %collective-permute-done.5 = bf16[8,4096]{1,0:T(8,128)(2,1)S(1)} collective-permute-done((bf16[8,4096]{1,0:T(8,128)(2,1)S(1)}, bf16[8,4096]{1,0:T(8,128)(2,1)S(1)}, u32[]{:S(2)}, u32[]{:S(2)}) %collective-permute-start.5) | collective-permute-done | bytes 65568 | tf_op jit(solution)/shard_map/ppermute | solution.py:39
  28.4 1.8 %collective-permute-start.3 = (bf16[12,4096]{1,0:T(8,128)(2,1)S(1)}, bf16[12,4096]{1,0:T(8,128)(2,1)S(1)}, u32[]{:S(2)}, u32[]{:S(2)}) collective-permute-start(bf16[12,4096]{1,0:T(8,128)(2,1)S(1)} %pad_maximum_fusion), channel_id=1, source_target_pairs={{0,24},{1,25},{2,26},{3,27},{4,28},{5,29},{6,30},{7,31},{8,16},{9,... | collective-permute-start | bytes 294920 | tf_op jit(solution)/shard_map/ppermute | solution.py:39
  30.2 2.6 %collective-permute-start.7 = (bf16[16,4096]{1,0:T(8,128)(2,1)S(1)}, bf16[16,4096]{1,0:T(8,128)(2,1)S(1)}, u32[]{:S(2)}, u32[]{:S(2)}) collective-permute-start(bf16[16,4096]{1,0:T(8,128)(2,1)S(1)} %get-tuple-element.75), channel_id=1, source_target_pairs={{0,4},{1,5},{2,6},{3,7},{4,0},{5,1},{6,2},{7,3},{8,12},{9,13},{10,... | collective-permute-start | bytes 393224 | tf_op jit(solution)/shard_map/ppermute | solution.py:39
  33.0 1.7 %collective-permute-start.8 = (bf16[16,4096]{1,0:T(8,128)(2,1)S(1)}, bf16[16,4096]{1,0:T(8,128)(2,1)S(1)}, u32[]{:S(2)}, u32[]{:S(2)}) collective-permute-start(bf16[16,4096]{1,0:T(8,128)(2,1)S(1)} %get-tuple-element.75), channel_id=1, source_target_pairs={{0,2},{1,3},{2,4},{3,5},{4,6},{5,7},{6,0},{7,1},{8,10},{9,11},{10,... | collective-permute-start | bytes 393224 | tf_op jit(solution)/shard_map/ppermute | solution.py:39
  34.7 2.2 %collective-permute-done.2 = bf16[12,4096]{1,0:T(8,128)(2,1)S(1)} collective-permute-done((bf16[12,4096]{1,0:T(8,128)(2,1)S(1)}, bf16[12,4096]{1,0:T(8,128)(2,1)S(1)}, u32[]{:S(2)}, u32[]{:S(2)}) %collective-permute-start.2) | collective-permute-done | bytes 98336 | tf_op jit(solution)/shard_map/ppermute | solution.py:39
  37.7 1.6 collective-permute-done.8
  39.3 7.7 %collective-permute-start.12 = (bf16[48,4096]{1,0:T(8,128)(2,1)S(1)}, bf16[48,4096]{1,0:T(8,128)(2,1)S(1)}, u32[]{:S(2)}, u32[]{:S(2)}) collective-permute-start(bf16[48,4096]{1,0:T(8,128)(2,1)S(1)} %concatenate.45.refs_1_), channel_id=1, source_target_pairs={{0,6},{1,7},{2,0},{3,1},{4,2},{5,3},{6,4},{7,5},{8,14},{9,15},{10,... | collective-permute-start | bytes 1179656 | tf_op jit(solution)/shard_map/ppermute | solution.py:39
  47.0 1.6 collective-permute-start.14
  50.0 2.3 %collective-permute-done.12.refs_2_ = bf16[48,4096]{1,0:T(8,128)(2,1)S(1)} collective-permute-done((bf16[48,4096]{1,0:T(8,128)(2,1)S(1)}, bf16[48,4096]{1,0:T(8,128)(2,1)S(1)}, u32[]{:S(2)}, u32[]{:S(2)}) %collective-permute-start.12) | collective-permute-done | bytes 393248 | tf_op jit(solution)/shard_map/ppermute | solution.py:39
  52.3 4.2 %collective-permute-done.13.refs_3_ = bf16[48,4096]{1,0:T(8,128)(2,1)} collective-permute-done((bf16[48,4096]{1,0:T(8,128)(2,1)S(1)}, bf16[48,4096]{1,0:T(8,128)(2,1)}, u32[]{:S(2)}, u32[]{:S(2)}) %collective-permute-start.13) | collective-permute-done | bytes 393248 | tf_op jit(solution)/shard_map/ppermute | solution.py:39
  58.5 7.6 %collective-permute-done.9.refs_1_ = bf16[64,4096]{1,0:T(8,128)(2,1)S(1)} collective-permute-done((bf16[64,4096]{1,0:T(8,128)(2,1)S(1)}, bf16[64,4096]{1,0:T(8,128)(2,1)S(1)}, u32[]{:S(2)}, u32[]{:S(2)}) %collective-permute-start.9) | collective-permute-done | bytes 524320 | tf_op jit(solution)/shard_map/ppermute | solution.py:39
  69.0 8.0 %first.1 = (bf16[128,4096]{1,0:T(8,128)(2,1)S(1)}, bf16[128,4096]{1,0:T(8,128)(2,1)S(1)}, bf16[128,448]{1,0:T(8,128)(2,1)S(1)}, bf16[128,448]{1,0:T(8,128)(2,1)S(1)}, bf16[128,448]{1,0:T(8,128)(2,1)S(1)}) custom-call(bf16[256,384]{1,0:T(8,128)(2,1)S(1)} %copy.14.refs_0_, bf16[48,4096]{1,0:T(8,128)(2,1)S(1)} %concatenate.45.refs_1_, ...), custom_call_target="tpu_custom_call" | custom-call | flops 1879048192 | bytes 14352384 | tf_op jit(solution)/shard_map/first/pallas_call | solution.py:218
  77.0 6.4 %terms.1 = (bf16[192,4096]{1,0:T(8,128)(2,1)S(1)}, bf16[192,4096]{1,0:T(8,128)(2,1)S(1)}) custom-call(bf16[384,256]{1,0:T(8,128)(2,1)S(1)} %bitcast.35, bf16[128,448]{1,0:T(8,128)(2,1)S(1)} %get-tuple-element.43.hidden, bf16[128,448]{1,0:T(8,128)(2,1)S(1)} %get-tuple-element.38.refs_5_.dgate, bf16[128,448]{1,0:T(8,128)(2,1)S(1)} %get-tuple-element.39.refs_6_.dup, ...), custom_call_target="tpu_custom_call" | custom-call | flops 2348810240 | bytes 11681792 | tf_op jit(solution)/shard_map/terms/pallas_call | solution.py:218
  84.0 6.2 %second.1 = (f32[256,448]{1,0:T(8,128)S(1)}, f32[256,448]{1,0:T(8,128)S(1)}, bf16[256,448]{1,0:T(8,128)(2,1)S(1)}, bf16[256,448]{1,0:T(8,128)(2,1)S(1)}) custom-call(bf16[64,4096]{1,0:T(8,128)(2,1)S(1)} %constant_dynamic-update-slice_fusion.2.refs_0_, bf16[64,4096]{1,0:T(8,128)(2,1)S(1)} %collective-permute-done.9.refs_1_, ...), custom_call_target="tpu_custom_call" | custom-call | flops 2348810240 | bytes 10715136 | tf_op jit(solution)/shard_map/second/pallas_call | solution.py:218
  91.0 3.1 %collective-permute-start.21 = (bf16[48,4096]{1,0:T(8,128)(2,1)S(1)}, bf16[48,4096]{1,0:T(8,128)(2,1)S(1)}, u32[]{:S(2)}, u32[]{:S(2)}) collective-permute-start(bf16[48,4096]{1,0:T(8,128)(2,1)S(1)} %get-tuple-element.59), channel_id=1, source_target_pairs={{0,4},{1,5},{2,6},{3,7},{4,0},{5,1},{6,2},{7,3},{8,12},{9,13},{10,... | collective-permute-start | bytes 1179656 | tf_op jit(solution)/shard_map/ppermute | solution.py:39
  95.0 2.3 %collective-permute-start.23 = (bf16[256,448]{1,0:T(8,128)(2,1)S(1)}, bf16[256,448]{1,0:T(8,128)(2,1)S(1)}, u32[]{:S(2)}, u32[]{:S(2)}) collective-permute-start(bf16[256,448]{1,0:T(8,128)(2,1)S(1)} %get-tuple-element.46), channel_id=1, source_target_pairs={{0,128},{1,129},{2,130},{3,131},{4,132},{5,133},{6,134},{7,135},{8... | collective-permute-start | bytes 688136 | tf_op jit(solution)/shard_map/ppermute | solution.py:39
  97.3 3.6 %collective-permute-start.24 = (bf16[256,448]{1,0:T(8,128)(2,1)S(1)}, bf16[256,448]{1,0:T(8,128)(2,1)S(1)}, u32[]{:S(2)}, u32[]{:S(2)}) collective-permute-start(bf16[256,448]{1,0:T(8,128)(2,1)S(1)} %get-tuple-element.47), channel_id=1, source_target_pairs={{0,128},{1,129},{2,130},{3,131},{4,132},{5,133},{6,134},{7,135},{8... | collective-permute-start | bytes 688136 | tf_op jit(solution)/shard_map/ppermute | solution.py:39
  102.0 9.5 %collective-permute-done.21 = bf16[48,4096]{1,0:T(8,128)(2,1)S(1)} collective-permute-done((bf16[48,4096]{1,0:T(8,128)(2,1)S(1)}, bf16[48,4096]{1,0:T(8,128)(2,1)S(1)}, u32[]{:S(2)}, u32[]{:S(2)}) %collective-permute-start.21) | collective-permute-done | bytes 393248 | tf_op jit(solution)/shard_map/ppermute | solution.py:39
  112.5 4.1 %collective-permute-done.23.mate_gate = bf16[256,448]{1,0:T(8,128)(2,1)S(1)} collective-permute-done((bf16[256,448]{1,0:T(8,128)(2,1)S(1)}, bf16[256,448]{1,0:T(8,128)(2,1)S(1)}, u32[]{:S(2)}, u32[]{:S(2)}) %collective-permute-start.23) | collective-permute-done | bytes 229408 | tf_op jit(solution)/shard_map/ppermute | solution.py:39
  116.6 5.5 %collective-permute-done.24.mate_up = bf16[256,448]{1,0:T(8,128)(2,1)S(1)} collective-permute-done((bf16[256,448]{1,0:T(8,128)(2,1)S(1)}, bf16[256,448]{1,0:T(8,128)(2,1)S(1)}, u32[]{:S(2)}, u32[]{:S(2)}) %collective-permute-start.24) | collective-permute-done | bytes 229408 | tf_op jit(solution)/shard_map/ppermute | solution.py:39
  122.1 4.9 %third.1 = (bf16[128,4096]{1,0:T(8,128)(2,1)S(1)}, bf16[128,4096]{1,0:T(8,128)(2,1)S(1)}) custom-call(f32[256,448]{1,0:T(8,128)S(1)} %get-tuple-element.50.gate, f32[256,448]{1,0:T(8,128)S(1)} %get-tuple-element.51.up, bf16[256,448]{1,0:T(8,128)(2,1)S(1)} %collective-permute-done.23.mate_gate, bf16[256,448]{1,0:T(8,128)(2,1)S(1)} %collective-permute-done.24.mate_up, ...), custom_call_target="tpu_custom_call" | custom-call | flops 1409286144 | bytes 6209536 | tf_op jit(solution)/shard_map/third/pallas_call | solution.py:218
  127.1 2.6 %collective-permute-done.25 = bf16[128,4096]{1,0:T(8,128)(2,1)S(1)} collective-permute-done((bf16[128,4096]{1,0:T(8,128)(2,1)S(1)}, bf16[128,4096]{1,0:T(8,128)(2,1)S(1)}, u32[]{:S(2)}, u32[]{:S(2)}) %collective-permute-start.25) | collective-permute-done | bytes 1048608 | tf_op jit(solution)/shard_map/ppermute | solution.py:39
  130.8 3.8 %collective-permute-start.26 = (bf16[12,4096]{1,0:T(8,128)(2,1)S(1)}, bf16[12,4096]{1,0:T(8,128)(2,1)S(1)}, u32[]{:S(2)}, u32[]{:S(2)}) collective-permute-start(bf16[12,4096]{1,0:T(8,128)(2,1)S(1)} %get-tuple-element.63), channel_id=1, source_target_pairs={{0,8},{1,9},{2,10},{3,11},{4,12},{5,13},{6,14},{7,15},{8,0},{9,1},... | collective-permute-start | bytes 294920 | tf_op jit(solution)/shard_map/ppermute | solution.py:39
  139.7 2.9 %collective-permute-done.27 = bf16[12,4096]{1,0:T(8,128)(2,1)S(1)} collective-permute-done((bf16[12,4096]{1,0:T(8,128)(2,1)S(1)}, bf16[12,4096]{1,0:T(8,128)(2,1)S(1)}, u32[]{:S(2)}, u32[]{:S(2)}) %collective-permute-start.27) | collective-permute-done | bytes 98336 | tf_op jit(solution)/shard_map/ppermute | solution.py:39
  143.5 5.0 %collective-permute-done.31 = bf16[32,4096]{1,0:T(8,128)(2,1)S(1)} collective-permute-done((bf16[32,4096]{1,0:T(8,128)(2,1)S(1)}, bf16[32,4096]{1,0:T(8,128)(2,1)S(1)}, u32[]{:S(2)}, u32[]{:S(2)}) %collective-permute-start.31) | collective-permute-done | bytes 262176 | tf_op jit(solution)/shard_map/ppermute | solution.py:39
  152.0 2.6 %collective-permute-start.37 = (bf16[4,4096]{1,0:T(4,128)(2,1)S(1)}, bf16[4,4096]{1,0:T(4,128)(2,1)S(1)}, u32[]{:S(2)}, u32[]{:S(2)}) collective-permute-start(bf16[4,4096]{1,0:T(4,128)(2,1)S(1)} %get-tuple-element.72), channel_id=1, source_target_pairs={{0,8},{1,9},{2,10},{3,11},{4,12},{5,13},{6,14},{7,15},{8,0},{9,1},... | collective-permute-start | bytes 98312 | tf_op jit(solution)/shard_map/ppermute | solution.py:39
  155.5 2.9 %collective-permute-start.35 = (bf16[4,4096]{1,0:T(4,128)(2,1)S(1)}, bf16[4,4096]{1,0:T(4,128)(2,1)S(1)}, u32[]{:S(2)}, u32[]{:S(2)}) collective-permute-start(bf16[4,4096]{1,0:T(4,128)(2,1)S(1)} %get-tuple-element.70), channel_id=1, source_target_pairs={{0,144},{1,145},{2,146},{3,147},{4,148},{5,149},{6,150},{7,151},{8... | collective-permute-start | bytes 98312 | tf_op jit(solution)/shard_map/ppermute | solution.py:39
  158.3 3.1 %collective-permute-start.34 = (bf16[4,4096]{1,0:T(4,128)(2,1)S(1)}, bf16[4,4096]{1,0:T(4,128)(2,1)S(1)}, u32[]{:S(2)}, u32[]{:S(2)}) collective-permute-start(bf16[4,4096]{1,0:T(4,128)(2,1)S(1)} %get-tuple-element.71), channel_id=1, source_target_pairs={{0,136},{1,137},{2,138},{3,139},{4,140},{5,141},{6,142},{7,143},{8... | collective-permute-start | bytes 98312 | tf_op jit(solution)/shard_map/ppermute | solution.py:39
  161.4 2.5 %collective-permute-start.33 = (bf16[4,4096]{1,0:T(4,128)(2,1)S(1)}, bf16[4,4096]{1,0:T(4,128)(2,1)S(1)}, u32[]{:S(2)}, u32[]{:S(2)}) collective-permute-start(bf16[4,4096]{1,0:T(4,128)(2,1)S(1)} %get-tuple-element.68), channel_id=1, source_target_pairs={{0,128},{1,129},{2,130},{3,131},{4,132},{5,133},{6,134},{7,135},{8... | collective-permute-start | bytes 98312 | tf_op jit(solution)/shard_map/ppermute | solution.py:39
  165.2 4.0 %collective-permute-done.33 = bf16[4,4096]{1,0:T(4,128)(2,1)S(1)} collective-permute-done((bf16[4,4096]{1,0:T(4,128)(2,1)S(1)}, bf16[4,4096]{1,0:T(4,128)(2,1)S(1)}, u32[]{:S(2)}, u32[]{:S(2)}) %collective-permute-start.33) | collective-permute-done | bytes 32800 | tf_op jit(solution)/shard_map/ppermute | solution.py:39
  (110 shorter events, 33.6 us)
Async XLA Ops:
  0.6 20.2 %collective-permute-start = (bf16[8,4096]{1,0:T(8,128)(2,1)}, bf16[8,4096]{1,0:T(8,128)(2,1)S(1)}, u32[]{:S(2)}, u32[]{:S(2)}) collective-permute-start(bf16[8,4096]{1,0:T(8,128)(2,1)} %bitcast.49), channel_id=1, source_target_pairs={{0,224},{1,225},{2,226},{3,227},{4,228},{5,229},{6,230},{7,231},{8... | collective-permute-start | bytes 196616 | tf_op jit(solution)/shard_map/ppermute | solution.py:39
  12.8 7.9 %collective-permute-start.4 = (bf16[4,4096]{1,0:T(4,128)(2,1)S(1)}, bf16[4,4096]{1,0:T(4,128)(2,1)S(1)}, u32[]{:S(2)}, u32[]{:S(2)}) collective-permute-start(bf16[4,4096]{1,0:T(4,128)(2,1)S(1)} %get-tuple-element.81), channel_id=1, source_target_pairs={{0,128},{1,129},{2,130},{3,131},{4,132},{5,133},{6,134},{7,135},{8... | collective-permute-start | bytes 98312 | tf_op jit(solution)/shard_map/ppermute | solution.py:39
  25.2 12.5 %collective-permute-start.6 = (bf16[16,4096]{1,0:T(8,128)(2,1)S(1)}, bf16[16,4096]{1,0:T(8,128)(2,1)S(1)}, u32[]{:S(2)}, u32[]{:S(2)}) collective-permute-start(bf16[16,4096]{1,0:T(8,128)(2,1)S(1)} %get-tuple-element.75), channel_id=1, source_target_pairs={{0,6},{1,7},{2,0},{3,1},{4,2},{5,3},{6,4},{7,5},{8,14},{9,15},{10,... | collective-permute-start | bytes 393224 | tf_op jit(solution)/shard_map/ppermute | solution.py:39
  27.0 10.0 %collective-permute-start.2 = (bf16[12,4096]{1,0:T(8,128)(2,1)S(1)}, bf16[12,4096]{1,0:T(8,128)(2,1)S(1)}, u32[]{:S(2)}, u32[]{:S(2)}) collective-permute-start(bf16[12,4096]{1,0:T(8,128)(2,1)S(1)} %pad_maximum_fusion), channel_id=1, source_target_pairs={{0,16},{1,17},{2,18},{3,19},{4,20},{5,21},{6,22},{7,23},{8,24},{9,... | collective-permute-start | bytes 294920 | tf_op jit(solution)/shard_map/ppermute | solution.py:39
  28.4 8.5 %collective-permute-start.3 = (bf16[12,4096]{1,0:T(8,128)(2,1)S(1)}, bf16[12,4096]{1,0:T(8,128)(2,1)S(1)}, u32[]{:S(2)}, u32[]{:S(2)}) collective-permute-start(bf16[12,4096]{1,0:T(8,128)(2,1)S(1)} %pad_maximum_fusion), channel_id=1, source_target_pairs={{0,24},{1,25},{2,26},{3,27},{4,28},{5,29},{6,30},{7,31},{8,16},{9,... | collective-permute-start | bytes 294920 | tf_op jit(solution)/shard_map/ppermute | solution.py:39
  39.3 13.0 %collective-permute-start.12 = (bf16[48,4096]{1,0:T(8,128)(2,1)S(1)}, bf16[48,4096]{1,0:T(8,128)(2,1)S(1)}, u32[]{:S(2)}, u32[]{:S(2)}) collective-permute-start(bf16[48,4096]{1,0:T(8,128)(2,1)S(1)} %concatenate.45.refs_1_), channel_id=1, source_target_pairs={{0,6},{1,7},{2,0},{3,1},{4,2},{5,3},{6,4},{7,5},{8,14},{9,15},{10,... | collective-permute-start | bytes 1179656 | tf_op jit(solution)/shard_map/ppermute | solution.py:39
  47.0 9.5 %collective-permute-start.13 = (bf16[48,4096]{1,0:T(8,128)(2,1)S(1)}, bf16[48,4096]{1,0:T(8,128)(2,1)}, u32[]{:S(2)}, u32[]{:S(2)}) collective-permute-start(bf16[48,4096]{1,0:T(8,128)(2,1)S(1)} %concatenate.45.refs_1_), channel_id=1, source_target_pairs={{0,4},{1,5},{2,6},{3,7},{4,0},{5,1},{6,2},{7,3},{8,12},{9,13},{10,... | collective-permute-start | bytes 1179656 | tf_op jit(solution)/shard_map/ppermute | solution.py:39
  47.0 10.2 %collective-permute-start.14 = (bf16[48,4096]{1,0:T(8,128)(2,1)S(1)}, bf16[48,4096]{1,0:T(8,128)(2,1)}, u32[]{:S(2)}, u32[]{:S(2)}) collective-permute-start(bf16[48,4096]{1,0:T(8,128)(2,1)S(1)} %concatenate.45.refs_1_), channel_id=1, source_target_pairs={{0,2},{1,3},{2,4},{3,5},{4,6},{5,7},{6,0},{7,1},{8,10},{9,11},{10,... | collective-permute-start | bytes 1179656 | tf_op jit(solution)/shard_map/ppermute | solution.py:39
  48.6 17.6 %collective-permute-start.9 = (bf16[64,4096]{1,0:T(8,128)(2,1)S(1)}, bf16[64,4096]{1,0:T(8,128)(2,1)S(1)}, u32[]{:S(2)}, u32[]{:S(2)}) collective-permute-start(bf16[64,4096]{1,0:T(8,128)(2,1)S(1)} %constant_dynamic-update-slice_fusion.2.refs_0_), channel_id=1, source_target_pairs={{0,16},{1,17},{2,18},{3,19},{4,20},{5,21},{6,22},{7,23},{8,24},{9,... | collective-permute-start | bytes 1572872 | tf_op jit(solution)/shard_map/ppermute | solution.py:39
  48.6 8.7 %collective-permute-start.15 = (bf16[48,4096]{1,0:T(8,128)(2,1)S(1)}, bf16[48,4096]{1,0:T(8,128)(2,1)S(1)}, u32[]{:S(2)}, u32[]{:S(2)}) collective-permute-start(bf16[48,4096]{1,0:T(8,128)(2,1)S(1)} %concatenate.45.refs_1_), channel_id=1, source_target_pairs={{0,1},{1,0},{2,3},{3,2},{4,5},{5,4},{6,7},{7,6},{8,9},{9,8},{10,11... | collective-permute-start | bytes 1179656 | tf_op jit(solution)/shard_map/ppermute | solution.py:39
  52.3 15.7 %collective-permute-start.16 = (bf16[48,4096]{1,0:T(8,128)(2,1)S(1)}, bf16[48,4096]{1,0:T(8,128)(2,1)}, u32[]{:S(2)}, u32[]{:S(2)}) collective-permute-start(bf16[48,4096]{1,0:T(8,128)(2,1)S(1)} %collective-permute-done.12.refs_2_), channel_id=1, source_target_pairs={{0,1},{1,0},{2,3},{3,2},{4,5},{5,4},{6,7},{7,6},{8,9},{9,8},{10,11... | collective-permute-start | bytes 1179656 | tf_op jit(solution)/shard_map/ppermute | solution.py:39
  56.5 11.5 %collective-permute-start.17 = (bf16[48,4096]{1,0:T(8,128)(2,1)}, bf16[48,4096]{1,0:T(8,128)(2,1)}, u32[]{:S(2)}, u32[]{:S(2)}) collective-permute-start(bf16[48,4096]{1,0:T(8,128)(2,1)} %collective-permute-done.13.refs_3_), channel_id=1, source_target_pairs={{0,1},{1,0},{2,3},{3,2},{4,5},{5,4},{6,7},{7,6},{8,9},{9,8},{10,11... | collective-permute-start | bytes 1179656 | tf_op jit(solution)/shard_map/ppermute | solution.py:39
  57.2 10.8 %collective-permute-start.18 = (bf16[48,4096]{1,0:T(8,128)(2,1)}, bf16[48,4096]{1,0:T(8,128)(2,1)}, u32[]{:S(2)}, u32[]{:S(2)}) collective-permute-start(bf16[48,4096]{1,0:T(8,128)(2,1)} %collective-permute-done.14.refs_4_), channel_id=1, source_target_pairs={{0,1},{1,0},{2,3},{3,2},{4,5},{5,4},{6,7},{7,6},{8,9},{9,8},{10,11... | collective-permute-start | bytes 1179656 | tf_op jit(solution)/shard_map/ppermute | solution.py:39
  58.0 19.0 %collective-permute-start.10 = (bf16[64,4096]{1,0:T(8,128)(2,1)S(1)}, bf16[64,4096]{1,0:T(8,128)(2,1)S(1)}, u32[]{:S(2)}, u32[]{:S(2)}) collective-permute-start(bf16[64,4096]{1,0:T(8,128)(2,1)S(1)} %constant_dynamic-update-slice_fusion.2.refs_0_), channel_id=1, source_target_pairs={{0,1},{1,0},{2,3},{3,2},{4,5},{5,4},{6,7},{7,6},{8,9},{9,8},{10,11... | collective-permute-start | bytes 1572872 | tf_op jit(solution)/shard_map/ppermute | solution.py:39
  66.2 10.8 %collective-permute-start.11 = (bf16[64,4096]{1,0:T(8,128)(2,1)S(1)}, bf16[64,4096]{1,0:T(8,128)(2,1)S(1)}, u32[]{:S(2)}, u32[]{:S(2)}) collective-permute-start(bf16[64,4096]{1,0:T(8,128)(2,1)S(1)} %collective-permute-done.9.refs_1_), channel_id=1, source_target_pairs={{0,1},{1,0},{2,3},{3,2},{4,5},{5,4},{6,7},{7,6},{8,9},{9,8},{10,11... | collective-permute-start | bytes 1572872 | tf_op jit(solution)/shard_map/ppermute | solution.py:39
  90.9 11.1 %collective-permute-start.22 = (bf16[48,4096]{1,0:T(8,128)(2,1)S(1)}, bf16[48,4096]{1,0:T(8,128)(2,1)S(1)}, u32[]{:S(2)}, u32[]{:S(2)}) collective-permute-start(bf16[48,4096]{1,0:T(8,128)(2,1)S(1)} %get-tuple-element.58), channel_id=1, source_target_pairs={{0,6},{1,7},{2,0},{3,1},{4,2},{5,3},{6,4},{7,5},{8,14},{9,15},{10,... | collective-permute-start | bytes 1179656 | tf_op jit(solution)/shard_map/ppermute | solution.py:39
  91.0 20.6 %collective-permute-start.21 = (bf16[48,4096]{1,0:T(8,128)(2,1)S(1)}, bf16[48,4096]{1,0:T(8,128)(2,1)S(1)}, u32[]{:S(2)}, u32[]{:S(2)}) collective-permute-start(bf16[48,4096]{1,0:T(8,128)(2,1)S(1)} %get-tuple-element.59), channel_id=1, source_target_pairs={{0,4},{1,5},{2,6},{3,7},{4,0},{5,1},{6,2},{7,3},{8,12},{9,13},{10,... | collective-permute-start | bytes 1179656 | tf_op jit(solution)/shard_map/ppermute | solution.py:39
  94.1 18.2 %collective-permute-start.20 = (bf16[48,4096]{1,0:T(8,128)(2,1)S(1)}, bf16[48,4096]{1,0:T(8,128)(2,1)S(1)}, u32[]{:S(2)}, u32[]{:S(2)}) collective-permute-start(bf16[48,4096]{1,0:T(8,128)(2,1)S(1)} %get-tuple-element.57), channel_id=1, source_target_pairs={{0,2},{1,3},{2,4},{3,5},{4,6},{5,7},{6,0},{7,1},{8,10},{9,11},{10,... | collective-permute-start | bytes 1179656 | tf_op jit(solution)/shard_map/ppermute | solution.py:39
  95.0 21.5 %collective-permute-start.23 = (bf16[256,448]{1,0:T(8,128)(2,1)S(1)}, bf16[256,448]{1,0:T(8,128)(2,1)S(1)}, u32[]{:S(2)}, u32[]{:S(2)}) collective-permute-start(bf16[256,448]{1,0:T(8,128)(2,1)S(1)} %get-tuple-element.46), channel_id=1, source_target_pairs={{0,128},{1,129},{2,130},{3,131},{4,132},{5,133},{6,134},{7,135},{8... | collective-permute-start | bytes 688136 | tf_op jit(solution)/shard_map/ppermute | solution.py:39
  97.3 24.8 %collective-permute-start.24 = (bf16[256,448]{1,0:T(8,128)(2,1)S(1)}, bf16[256,448]{1,0:T(8,128)(2,1)S(1)}, u32[]{:S(2)}, u32[]{:S(2)}) collective-permute-start(bf16[256,448]{1,0:T(8,128)(2,1)S(1)} %get-tuple-element.47), channel_id=1, source_target_pairs={{0,128},{1,129},{2,130},{3,131},{4,132},{5,133},{6,134},{7,135},{8... | collective-permute-start | bytes 688136 | tf_op jit(solution)/shard_map/ppermute | solution.py:39
  130.1 8.4 %collective-permute-start.28 = (bf16[12,4096]{1,0:T(8,128)(2,1)S(1)}, bf16[12,4096]{1,0:T(8,128)(2,1)S(1)}, u32[]{:S(2)}, u32[]{:S(2)}) collective-permute-start(bf16[12,4096]{1,0:T(8,128)(2,1)S(1)} %get-tuple-element.64), channel_id=1, source_target_pairs={{0,24},{1,25},{2,26},{3,27},{4,28},{5,29},{6,30},{7,31},{8,16},{9,... | collective-permute-start | bytes 294920 | tf_op jit(solution)/shard_map/ppermute | solution.py:39
  130.8 11.8 %collective-permute-start.27 = (bf16[12,4096]{1,0:T(8,128)(2,1)S(1)}, bf16[12,4096]{1,0:T(8,128)(2,1)S(1)}, u32[]{:S(2)}, u32[]{:S(2)}) collective-permute-start(bf16[12,4096]{1,0:T(8,128)(2,1)S(1)} %get-tuple-element.65), channel_id=1, source_target_pairs={{0,16},{1,17},{2,18},{3,19},{4,20},{5,21},{6,22},{7,23},{8,24},{9,... | collective-permute-start | bytes 294920 | tf_op jit(solution)/shard_map/ppermute | solution.py:39
  130.8 11.8 %collective-permute-start.26 = (bf16[12,4096]{1,0:T(8,128)(2,1)S(1)}, bf16[12,4096]{1,0:T(8,128)(2,1)S(1)}, u32[]{:S(2)}, u32[]{:S(2)}) collective-permute-start(bf16[12,4096]{1,0:T(8,128)(2,1)S(1)} %get-tuple-element.63), channel_id=1, source_target_pairs={{0,8},{1,9},{2,10},{3,11},{4,12},{5,13},{6,14},{7,15},{8,0},{9,1},... | collective-permute-start | bytes 294920 | tf_op jit(solution)/shard_map/ppermute | solution.py:39
  134.6 8.8 %collective-permute-start.32 = (bf16[32,4096]{1,0:T(8,128)(2,1)S(1)}, bf16[32,4096]{1,0:T(8,128)(2,1)S(1)}, u32[]{:S(2)}, u32[]{:S(2)}) collective-permute-start(bf16[32,4096]{1,0:T(8,128)(2,1)S(1)} %get-tuple-element.61), channel_id=1, source_target_pairs={{0,6},{1,7},{2,0},{3,1},{4,2},{5,3},{6,4},{7,5},{8,14},{9,15},{10,... | collective-permute-start | bytes 786440 | tf_op jit(solution)/shard_map/ppermute | solution.py:39
  136.1 12.4 %collective-permute-start.31 = (bf16[32,4096]{1,0:T(8,128)(2,1)S(1)}, bf16[32,4096]{1,0:T(8,128)(2,1)S(1)}, u32[]{:S(2)}, u32[]{:S(2)}) collective-permute-start(bf16[32,4096]{1,0:T(8,128)(2,1)S(1)} %get-tuple-element.62), channel_id=1, source_target_pairs={{0,4},{1,5},{2,6},{3,7},{4,0},{5,1},{6,2},{7,3},{8,12},{9,13},{10,... | collective-permute-start | bytes 786440 | tf_op jit(solution)/shard_map/ppermute | solution.py:39
  138.5 11.4 %collective-permute-start.30 = (bf16[32,4096]{1,0:T(8,128)(2,1)S(1)}, bf16[32,4096]{1,0:T(8,128)(2,1)S(1)}, u32[]{:S(2)}, u32[]{:S(2)}) collective-permute-start(bf16[32,4096]{1,0:T(8,128)(2,1)S(1)} %get-tuple-element.60), channel_id=1, source_target_pairs={{0,2},{1,3},{2,4},{3,5},{4,6},{5,7},{6,0},{7,1},{8,10},{9,11},{10,... | collective-permute-start | bytes 786440 | tf_op jit(solution)/shard_map/ppermute | solution.py:39
  142.9 12.6 %collective-permute-start.29 = (bf16[8,4096]{1,0:T(8,128)(2,1)S(1)}, bf16[8,4096]{1,0:T(8,128)(2,1)S(1)}, u32[]{:S(2)}, u32[]{:S(2)}) collective-permute-start(bf16[8,4096]{1,0:T(8,128)(2,1)S(1)} %slice.172), channel_id=1, source_target_pairs={{0,32},{1,33},{2,34},{3,35},{4,36},{5,37},{6,38},{7,39},{8,40},{9,... | collective-permute-start | bytes 196616 | tf_op jit(solution)/shard_map/ppermute | solution.py:39
  150.1 8.2 %collective-permute-start.39 = (bf16[4,4096]{1,0:T(4,128)(2,1)S(1)}, bf16[4,4096]{1,0:T(4,128)(2,1)S(1)}, u32[]{:S(2)}, u32[]{:S(2)}) collective-permute-start(bf16[4,4096]{1,0:T(4,128)(2,1)S(1)} %get-tuple-element.73), channel_id=1, source_target_pairs={{0,24},{1,25},{2,26},{3,27},{4,28},{5,29},{6,30},{7,31},{8,16},{9,... | collective-permute-start | bytes 98312 | tf_op jit(solution)/shard_map/ppermute | solution.py:39
  150.8 10.5 %collective-permute-start.38 = (bf16[4,4096]{1,0:T(4,128)(2,1)S(1)}, bf16[4,4096]{1,0:T(4,128)(2,1)S(1)}, u32[]{:S(2)}, u32[]{:S(2)}) collective-permute-start(bf16[4,4096]{1,0:T(4,128)(2,1)S(1)} %get-tuple-element.74), channel_id=1, source_target_pairs={{0,16},{1,17},{2,18},{3,19},{4,20},{5,21},{6,22},{7,23},{8,24},{9,... | collective-permute-start | bytes 98312 | tf_op jit(solution)/shard_map/ppermute | solution.py:39
  152.0 12.7 %collective-permute-start.37 = (bf16[4,4096]{1,0:T(4,128)(2,1)S(1)}, bf16[4,4096]{1,0:T(4,128)(2,1)S(1)}, u32[]{:S(2)}, u32[]{:S(2)}) collective-permute-start(bf16[4,4096]{1,0:T(4,128)(2,1)S(1)} %get-tuple-element.72), channel_id=1, source_target_pairs={{0,8},{1,9},{2,10},{3,11},{4,12},{5,13},{6,14},{7,15},{8,0},{9,1},... | collective-permute-start | bytes 98312 | tf_op jit(solution)/shard_map/ppermute | solution.py:39
  154.6 10.0 %collective-permute-start.36 = (bf16[4,4096]{1,0:T(4,128)(2,1)S(1)}, bf16[4,4096]{1,0:T(4,128)(2,1)S(1)}, u32[]{:S(2)}, u32[]{:S(2)}) collective-permute-start(bf16[4,4096]{1,0:T(4,128)(2,1)S(1)} %get-tuple-element.69), channel_id=1, source_target_pairs={{0,152},{1,153},{2,154},{3,155},{4,156},{5,157},{6,158},{7,159},{8... | collective-permute-start | bytes 98312 | tf_op jit(solution)/shard_map/ppermute | solution.py:39
  155.5 9.2 %collective-permute-start.35 = (bf16[4,4096]{1,0:T(4,128)(2,1)S(1)}, bf16[4,4096]{1,0:T(4,128)(2,1)S(1)}, u32[]{:S(2)}, u32[]{:S(2)}) collective-permute-start(bf16[4,4096]{1,0:T(4,128)(2,1)S(1)} %get-tuple-element.70), channel_id=1, source_target_pairs={{0,144},{1,145},{2,146},{3,147},{4,148},{5,149},{6,150},{7,151},{8... | collective-permute-start | bytes 98312 | tf_op jit(solution)/shard_map/ppermute | solution.py:39
  (14 other events, 159.4 us)

commit v3 on v2

--- a/solution.py
+++ b/solution.py
@@ -161,7 +161,7 @@
 def second_kernel(count, factor, *refs):
     nexts = refs[:count]
     normed, dgate, dup, gate_w, up_w = refs[count : 5 + count]
-    gate_out, up_out, gate_sent, up_sent, gate_sum, up_sum, inner_sum = refs[5 + count :]
+    gate_out, up_out, sent, gate_sum, up_sum, inner_sum = refs[5 + count :]
     first = pl.program_id(0) == 0
     rows = jnp.concatenate([r[...] for r in nexts], axis=0)
     gate_sum[...] = jnp.where(first, 0.0, gate_sum[...]) + dot_t(rows, gate_w[...])
@@ -175,25 +175,25 @@
         up_next = up_sum[...] + dot(overlap, dup[...])
         gate_out[...] = gate_next
         up_out[...] = up_next
-        gate_sent[...] = gate_next.astype(BF16)
-        up_sent[...] = up_next.astype(BF16)
+        sent[: gate_next.shape[0]] = gate_next.astype(BF16)
+        sent[gate_next.shape[0] :] = up_next.astype(BF16)
 
 
 def third_kernel(
-    factor, row_count, gate, up, mate_gate, mate_up, hidden, cotangent, down_w, mine, other, hidden_next, overlap
+    factor, row_count, gate, up, from_mate, hidden, cotangent, down_w, mine, other, hidden_next, overlap
 ):
     @pl.when(pl.program_id(0) == 0)
     def _():
-        gate_next = 0.5 * (gate[...] + mate_gate[...].astype(F32))
-        up_next = 0.5 * (up[...] + mate_up[...].astype(F32))
+        pairs = gate.shape[0]
+        gate_next = 0.5 * (gate[...] + from_mate[:pairs].astype(F32))
+        up_next = 0.5 * (up[...] + from_mate[pairs:].astype(F32))
         units = (gate_next * jax.nn.sigmoid(gate_next) * up_next).astype(BF16)
         rows = units.shape[0]
         to = lax.broadcasted_iota(jnp.int32, (rows, rows), 0)
         at = lax.broadcasted_iota(jnp.int32, (rows, rows), 1)
         i, j = to & (row_count - 1), to // row_count
         z, replica, y, core = j & (NZ - 1), (j // NZ) & 1, (j // (2 * NZ)) & (NY - 1), j // (2 * NZ * NY)
-        source = (((core * 2 + z // 2) * NY + y) * 2 + (z & 1)) * 2 + replica
-        source = source * row_count + i
+        source = (((core * NZ + z) * 2 + replica) * NY + y) * row_count + i
         order = jnp.where(at == source, 1.0, 0.0).astype(BF16)
         units = dot(order, units).astype(BF16)
         hidden_next[...] = units
@@ -248,28 +248,23 @@
     chunk = min(WIDTH, width)
     steps = width // chunk
 
-    shifted = send(slot_rows, ds=-1)
     next_values, _, next_normed = normalize(next_in[0], gain_row)
-    mate_normed = send(next_normed, ds=half_ring)
     values, row_scale, normed = normalize(layer_in[0], gain_row)
+    shifted = send(after(slot_rows, normed, next_normed), ds=-1)
     select = selection(wiring[0], blocks_dev, capacity)
     spread = lax.optimization_barrier(select.T)
 
-    next_y = jnp.concatenate(
-        [
-            jnp.where(first_half, next_normed, mate_normed),
-            jnp.where(first_half, mate_normed, next_normed),
-        ],
-        axis=0,
-    )
-    next_y = after(next_y, shifted)
-    next_y = jnp.concatenate([next_y, send(next_y, dz=1)], axis=0)
-    next_z = jnp.concatenate([next_y] + [send(next_y, dy=-k) for k in range(1, NY)], axis=0)
+    next_y = jnp.concatenate([next_normed] + [send(next_normed, dy=-k) for k in range(1, NY)], axis=0)
+    mate_y = send(next_y, ds=half_ring)
+    next_z = jnp.concatenate(
+        [jnp.where(first_half, next_y, mate_y), jnp.where(first_half, mate_y, next_y)], axis=0
+    )
     block_z = jnp.concatenate([shifted, normed], axis=0)
     block_y = jnp.concatenate(
         [block_z] + [send(block_z, dz=k) for k in range(1, NZ)], axis=0
     )
     block_y, next_z = lax.optimization_barrier((block_y, next_z))
+    next_z = jnp.concatenate([next_z, send(next_z, dz=1)], axis=0)
     blocks = [block_y] + [send(block_y, dy=-k) for k in range(1, NY)]
     blocks = blocks + [send(block, dc=1) for block in blocks]
     nexts = [next_z, send(next_z, dz=2)]
@@ -277,7 +272,7 @@
     pair_tokens = 2 * token_count
     part = jax.ShapeDtypeStruct((token_count, units), BF16)
     product = jax.ShapeDtypeStruct((pair_tokens, units), F32)
-    product_sent = jax.ShapeDtypeStruct((pair_tokens, units), BF16)
+    product_sent = jax.ShapeDtypeStruct((2 * pair_tokens, units), BF16)
     rows = jax.ShapeDtypeStruct((token_count, width), BF16)
     half = jax.ShapeDtypeStruct((spread.shape[0] // NC, width), BF16)
     per_row = 2 * width * units
@@ -313,14 +308,14 @@
         [spread, hidden, grad_gate_act, grad_up_act, own_rows, gate_local, up_local, down_local],
     )
     from_core = send(other, dc=1)
-    gate_part, up_part, gate_sent, up_sent = run(
+    gate_part, up_part, sent = run(
         functools.partial(second_kernel, len(nexts), update_factor),
         steps,
         [columns(block.shape[0], chunk) for block in nexts]
         + [columns(token_count, chunk), whole(part.shape), whole(part.shape)]
         + [columns(units, chunk)] * 2,
-        [product, product, product_sent, product_sent],
-        [whole(product.shape)] * 4,
+        [product, product, product_sent],
+        [whole(product.shape)] * 2 + [whole(product_sent.shape)],
         [
             pltpu.VMEM((pair_tokens, units), F32),
             pltpu.VMEM((pair_tokens, units), F32),
@@ -330,9 +325,8 @@
         "second",
         nexts + [normed_all, grad_gate_act, grad_up_act, gate_local, up_local],
     )
-    mate_gate = send(gate_sent, ds=half_ring)
-    mate_up = send(up_sent, ds=half_ring)
-    both = add_up([mine, after(from_core, gate_sent, up_sent)]).astype(BF16)
+    from_mate = send(sent, ds=half_ring)
+    both = add_up([mine, after(from_core, sent)]).astype(BF16)
     both = y_sum(both)
     gate_part, up_part, both = lax.optimization_barrier((gate_part, up_part, both))
 
@@ -340,14 +334,15 @@
     mine, other = run(
         functools.partial(third_kernel, update_factor, row_count),
         steps,
-        [whole(product.shape)] * 4
-        + [whole(part.shape), columns(token_count, chunk), columns(units, chunk)],
+        [whole(product.shape)] * 2
+        + [whole(product_sent.shape), whole(part.shape)]
+        + [columns(token_count, chunk), columns(units, chunk)],
         [half, half],
         [columns(half.shape[0], chunk)] * 2,
         [pltpu.VMEM((pair_tokens, units), BF16), pltpu.VMEM((pair_tokens, token_count), BF16)],
         per_row * token_count * 3,
         "third",
-        [gate_part, up_part, mate_gate, mate_up, hidden, cotangent, down_local],
+        [gate_part, up_part, from_mate, hidden, cotangent, down_local],
     )
     pair = add_up([mine, send(other, dc=1)]).astype(BF16)
     both = cut(after(both, pair), NZ)

time: 173 us -> 178 us (1.029)
  waiting for transfers between devices: 67.9 us -> 74.5 us
    ppermute x40 -> x39, waiting for transfers between devices: 67.9 us -> 74.5 us  [send(): return lax.ppermute(value, ('section', 'rep'), pairs)]
    ppermute x40 -> x39, starting transfers between devices: 62.8 us -> 62.5 us  [send(): return lax.ppermute(value, ('section', 'rep'), pairs)]
  transfers between devices with their start and end apart: 40 -> 39, of which waited for: 22 -> 19; matrix products, arithmetic and copies ran while one was open for 5% -> 3% of each run, Pallas kernels for 8% -> 8%
where the time goes in v3:
time: 178 us; the launch traced here: 177 us
  waiting for transfers between devices  74.5 us (42%)
  starting transfers between devices  62.5 us (35%)
  Pallas kernels  25.5 us (14%)
  other arithmetic  8.24 us (5%)
  local copies, waits for them, and re-layouts  3.57 us (2%)
    ppermute x39, waiting for transfers between devices, send(): return lax.ppermute(value, ('section', 'rep'), pairs)  74.5 us
    ppermute x39, starting transfers between devices, send(): return lax.ppermute(value, ('section', 'rep'), pairs)  62.5 us
    pallas_call x4, Pallas kernels, run(): pl.pallas_call(kernel, grid=(steps,), in_specs=in_specs, out_shape=outs,...  25.5 us
  transfers between devices with their start and end apart: 39, of which 19 were waited for; matrix products, arithmetic and copies ran while one was open for 3% of the time, Pallas kernels for 8%

profile of v3, /device:TPU:8, one launch (start us, length us, event | category | flops | bytes accessed | tf_op | source)
XLA Modules:
  0.0 176.7 jit_solution(18086236828940012521)
XLA Ops:
  5.0 2.7 %collective-permute-start.5 = (bf16[4,4096]{1,0:T(4,128)(2,1)S(1)}, bf16[4,4096]{1,0:T(4,128)(2,1)S(1)}, u32[]{:S(2)}, u32[]{:S(2)}) collective-permute-start(bf16[4,4096]{1,0:T(4,128)(2,1)S(1)} %get-tuple-element.75), channel_id=1, source_target_pairs={{0,4},{1,5},{2,6},{3,7},{4,0},{5,1},{6,2},{7,3},{8,12},{9,13},{10,... | collective-permute-start | bytes 98312 | tf_op jit(solution)/shard_map/ppermute | solution.py:39
  8.4 9.4 %collective-permute-start = (bf16[8,4096]{1,0:T(8,128)(2,1)}, bf16[8,4096]{1,0:T(8,128)(2,1)S(1)}, u32[]{:S(2)}, u32[]{:S(2)}) collective-permute-start(bf16[8,4096]{1,0:T(8,128)(2,1)} %bitcast.49), channel_id=1, source_target_pairs={{0,224},{1,225},{2,226},{3,227},{4,228},{5,229},{6,230},{7,231},{8... | collective-permute-start | bytes 196616 | tf_op jit(solution)/shard_map/ppermute | solution.py:39
  20.6 4.8 %collective-permute-start.1 = (bf16[12,4096]{1,0:T(8,128)(2,1)S(1)}, bf16[12,4096]{1,0:T(8,128)(2,1)S(1)}, u32[]{:S(2)}, u32[]{:S(2)}) collective-permute-start(bf16[12,4096]{1,0:T(8,128)(2,1)S(1)} %pad_maximum_fusion.1), channel_id=1, source_target_pairs={{0,8},{1,9},{2,10},{3,11},{4,12},{5,13},{6,14},{7,15},{8,0},{9,1},... | collective-permute-start | bytes 294920 | tf_op jit(solution)/shard_map/ppermute | solution.py:39
  25.5 2.3 %collective-permute-start.3 = (bf16[12,4096]{1,0:T(8,128)(2,1)S(1)}, bf16[12,4096]{1,0:T(8,128)(2,1)S(1)}, u32[]{:S(2)}, u32[]{:S(2)}) collective-permute-start(bf16[12,4096]{1,0:T(8,128)(2,1)S(1)} %pad_maximum_fusion.1), channel_id=1, source_target_pairs={{0,24},{1,25},{2,26},{3,27},{4,28},{5,29},{6,30},{7,31},{8,16},{9,... | collective-permute-start | bytes 294920 | tf_op jit(solution)/shard_map/ppermute | solution.py:39
  27.8 2.9 %collective-permute-done.7 = bf16[16,4096]{1,0:T(8,128)(2,1)S(1)} collective-permute-done((bf16[16,4096]{1,0:T(8,128)(2,1)S(1)}, bf16[16,4096]{1,0:T(8,128)(2,1)S(1)}, u32[]{:S(2)}, u32[]{:S(2)}) %collective-permute-start.7) | collective-permute-done | bytes 131104 | tf_op jit(solution)/shard_map/ppermute | solution.py:39
  32.7 4.9 %collective-permute-done.2 = bf16[12,4096]{1,0:T(8,128)(2,1)S(1)} collective-permute-done((bf16[12,4096]{1,0:T(8,128)(2,1)S(1)}, bf16[12,4096]{1,0:T(8,128)(2,1)S(1)}, u32[]{:S(2)}, u32[]{:S(2)}) %collective-permute-start.2) | collective-permute-done | bytes 98336 | tf_op jit(solution)/shard_map/ppermute | solution.py:39
  41.3 2.0 %collective-permute-start.8 = (bf16[32,4096]{1,0:T(8,128)(2,1)S(1)}, bf16[32,4096]{1,0:T(8,128)(2,1)S(1)}, u32[]{:S(2)}, u32[]{:S(2)}) collective-permute-start(bf16[32,4096]{1,0:T(8,128)(2,1)S(1)} %pad_maximum_fusion), channel_id=1, source_target_pairs={{0,8},{1,9},{2,10},{3,11},{4,12},{5,13},{6,14},{7,15},{8,0},{9,1},... | collective-permute-start | bytes 786440 | tf_op jit(solution)/shard_map/ppermute | solution.py:39
  43.3 4.4 %collective-permute-done.8 = bf16[32,4096]{1,0:T(8,128)(2,1)S(1)} collective-permute-done((bf16[32,4096]{1,0:T(8,128)(2,1)S(1)}, bf16[32,4096]{1,0:T(8,128)(2,1)S(1)}, u32[]{:S(2)}, u32[]{:S(2)}) %collective-permute-start.8) | collective-permute-done | bytes 262176 | tf_op jit(solution)/shard_map/ppermute | solution.py:39
  47.7 2.7 %collective-permute-start.9 = (bf16[64,4096]{1,0:T(8,128)(2,1)S(1)}, bf16[64,4096]{1,0:T(8,128)(2,1)S(1)}, u32[]{:S(2)}, u32[]{:S(2)}) collective-permute-start(bf16[64,4096]{1,0:T(8,128)(2,1)S(1)} %constant_dynamic-update-slice_fusion.refs_0_), channel_id=1, source_target_pairs={{0,16},{1,17},{2,18},{3,19},{4,20},{5,21},{6,22},{7,23},{8,24},{9,... | collective-permute-start | bytes 1572872 | tf_op jit(solution)/shard_map/ppermute | solution.py:39
  51.9 2.2 %collective-permute-done.12.refs_2_ = bf16[48,4096]{1,0:T(8,128)(2,1)S(1)} collective-permute-done((bf16[48,4096]{1,0:T(8,128)(2,1)S(1)}, bf16[48,4096]{1,0:T(8,128)(2,1)S(1)}, u32[]{:S(2)}, u32[]{:S(2)}) %collective-permute-start.12) | collective-permute-done | bytes 393248 | tf_op jit(solution)/shard_map/ppermute | solution.py:39
  57.3 13.0 %collective-permute-done.9.refs_1_ = bf16[64,4096]{1,0:T(8,128)(2,1)S(1)} collective-permute-done((bf16[64,4096]{1,0:T(8,128)(2,1)S(1)}, bf16[64,4096]{1,0:T(8,128)(2,1)S(1)}, u32[]{:S(2)}, u32[]{:S(2)}) %collective-permute-start.9) | collective-permute-done | bytes 524320 | tf_op jit(solution)/shard_map/ppermute | solution.py:39
  73.1 8.0 %first.1 = (bf16[128,4096]{1,0:T(8,128)(2,1)S(1)}, bf16[128,4096]{1,0:T(8,128)(2,1)S(1)}, bf16[128,448]{1,0:T(8,128)(2,1)S(1)}, bf16[128,448]{1,0:T(8,128)(2,1)S(1)}, bf16[128,448]{1,0:T(8,128)(2,1)S(1)}) custom-call(bf16[256,384]{1,0:T(8,128)(2,1)S(1)} %copy.14.refs_0_, bf16[48,4096]{1,0:T(8,128)(2,1)S(1)} %concatenate.44.refs_1_, ...), custom_call_target="tpu_custom_call" | custom-call | flops 1879048192 | bytes 14352384 | tf_op jit(solution)/shard_map/first/pallas_call | solution.py:218
  81.1 6.4 %terms.1 = (bf16[192,4096]{1,0:T(8,128)(2,1)S(1)}, bf16[192,4096]{1,0:T(8,128)(2,1)S(1)}) custom-call(bf16[384,256]{1,0:T(8,128)(2,1)S(1)} %bitcast.35, bf16[128,448]{1,0:T(8,128)(2,1)S(1)} %get-tuple-element.42.hidden, bf16[128,448]{1,0:T(8,128)(2,1)S(1)} %get-tuple-element.37.refs_5_.dgate, bf16[128,448]{1,0:T(8,128)(2,1)S(1)} %get-tuple-element.38.refs_6_.dup, ...), custom_call_target="tpu_custom_call" | custom-call | flops 2348810240 | bytes 11681792 | tf_op jit(solution)/shard_map/terms/pallas_call | solution.py:218
  88.2 6.2 %second.1 = (f32[256,448]{1,0:T(8,128)S(1)}, f32[256,448]{1,0:T(8,128)S(1)}, bf16[512,448]{1,0:T(8,128)(2,1)S(1)}) custom-call(bf16[64,4096]{1,0:T(8,128)(2,1)S(1)} %constant_dynamic-update-slice_fusion.refs_0_, bf16[64,4096]{1,0:T(8,128)(2,1)S(1)} %collective-permute-done.9.refs_1_, bf16[64,4096]{1,0:T(8,128)(2,1)S(1)} %collective-permute-done.10.refs_2_, ...), custom_call_target="tpu_custom_call" | custom-call | flops 2348810240 | bytes 10715136 | tf_op jit(solution)/shard_map/second/pallas_call | solution.py:218
  96.4 2.5 %collective-permute-start.21 = (bf16[48,4096]{1,0:T(8,128)(2,1)S(1)}, bf16[48,4096]{1,0:T(8,128)(2,1)S(1)}, u32[]{:S(2)}, u32[]{:S(2)}) collective-permute-start(bf16[48,4096]{1,0:T(8,128)(2,1)S(1)} %get-tuple-element.57), channel_id=1, source_target_pairs={{0,4},{1,5},{2,6},{3,7},{4,0},{5,1},{6,2},{7,3},{8,12},{9,13},{10,... | collective-permute-start | bytes 1179656 | tf_op jit(solution)/shard_map/ppermute | solution.py:39
  98.9 1.8 %collective-permute-start.20 = (bf16[48,4096]{1,0:T(8,128)(2,1)S(1)}, bf16[48,4096]{1,0:T(8,128)(2,1)S(1)}, u32[]{:S(2)}, u32[]{:S(2)}) collective-permute-start(bf16[48,4096]{1,0:T(8,128)(2,1)S(1)} %get-tuple-element.55), channel_id=1, source_target_pairs={{0,2},{1,3},{2,4},{3,5},{4,6},{5,7},{6,0},{7,1},{8,10},{9,11},{10,... | collective-permute-start | bytes 1179656 | tf_op jit(solution)/shard_map/ppermute | solution.py:39
  100.7 5.0 %collective-permute-start.23 = (bf16[512,448]{1,0:T(8,128)(2,1)S(1)}, bf16[512,448]{1,0:T(8,128)(2,1)S(1)}, u32[]{:S(2)}, u32[]{:S(2)}) collective-permute-start(bf16[512,448]{1,0:T(8,128)(2,1)S(1)} %get-tuple-element.45), channel_id=1, source_target_pairs={{0,128},{1,129},{2,130},{3,131},{4,132},{5,133},{6,134},{7,135},{8... | collective-permute-start | bytes 1376264 | tf_op jit(solution)/shard_map/ppermute | solution.py:39
  106.8 9.6 %collective-permute-done.21 = bf16[48,4096]{1,0:T(8,128)(2,1)S(1)} collective-permute-done((bf16[48,4096]{1,0:T(8,128)(2,1)S(1)}, bf16[48,4096]{1,0:T(8,128)(2,1)S(1)}, u32[]{:S(2)}, u32[]{:S(2)}) %collective-permute-start.21) | collective-permute-done | bytes 393248 | tf_op jit(solution)/shard_map/ppermute | solution.py:39
  117.3 11.8 %collective-permute-done.23.from_mate = bf16[512,448]{1,0:T(8,128)(2,1)S(1)} collective-permute-done((bf16[512,448]{1,0:T(8,128)(2,1)S(1)}, bf16[512,448]{1,0:T(8,128)(2,1)S(1)}, u32[]{:S(2)}, u32[]{:S(2)}) %collective-permute-start.23) | collective-permute-done | bytes 458784 | tf_op jit(solution)/shard_map/ppermute | solution.py:39
  129.1 4.9 %third.1 = (bf16[128,4096]{1,0:T(8,128)(2,1)S(1)}, bf16[128,4096]{1,0:T(8,128)(2,1)S(1)}) custom-call(f32[256,448]{1,0:T(8,128)S(1)} %get-tuple-element.48.gate, f32[256,448]{1,0:T(8,128)S(1)} %get-tuple-element.49.up, bf16[512,448]{1,0:T(8,128)(2,1)S(1)} %collective-permute-done.23.from_mate, bf16[128,448]{1,0:T(8,128)(2,1)S(1)} %get-tuple-element.42.hidden, ...), custom_call_target="tpu_custom_call" | custom-call | flops 1409286144 | bytes 6209536 | tf_op jit(solution)/shard_map/third/pallas_call | solution.py:218
  134.0 2.6 %collective-permute-done.24 = bf16[128,4096]{1,0:T(8,128)(2,1)S(1)} collective-permute-done((bf16[128,4096]{1,0:T(8,128)(2,1)S(1)}, bf16[128,4096]{1,0:T(8,128)(2,1)S(1)}, u32[]{:S(2)}, u32[]{:S(2)}) %collective-permute-start.24) | collective-permute-done | bytes 1048608 | tf_op jit(solution)/shard_map/ppermute | solution.py:39
  137.1 2.1 %collective-permute-start.27 = (bf16[12,4096]{1,0:T(8,128)(2,1)S(1)}, bf16[12,4096]{1,0:T(8,128)(2,1)S(1)}, u32[]{:S(2)}, u32[]{:S(2)}) collective-permute-start(bf16[12,4096]{1,0:T(8,128)(2,1)S(1)} %get-tuple-element.62), channel_id=1, source_target_pairs={{0,24},{1,25},{2,26},{3,27},{4,28},{5,29},{6,30},{7,31},{8,16},{9,... | collective-permute-start | bytes 294920 | tf_op jit(solution)/shard_map/ppermute | solution.py:39
  139.1 2.4 %collective-permute-start.25 = (bf16[12,4096]{1,0:T(8,128)(2,1)S(1)}, bf16[12,4096]{1,0:T(8,128)(2,1)S(1)}, u32[]{:S(2)}, u32[]{:S(2)}) collective-permute-start(bf16[12,4096]{1,0:T(8,128)(2,1)S(1)} %get-tuple-element.61), channel_id=1, source_target_pairs={{0,8},{1,9},{2,10},{3,11},{4,12},{5,13},{6,14},{7,15},{8,0},{9,1},... | collective-permute-start | bytes 294920 | tf_op jit(solution)/shard_map/ppermute | solution.py:39
  145.8 4.4 %collective-permute-done.26 = bf16[12,4096]{1,0:T(8,128)(2,1)S(1)} collective-permute-done((bf16[12,4096]{1,0:T(8,128)(2,1)S(1)}, bf16[12,4096]{1,0:T(8,128)(2,1)S(1)}, u32[]{:S(2)}, u32[]{:S(2)}) %collective-permute-start.26) | collective-permute-done | bytes 98336 | tf_op jit(solution)/shard_map/ppermute | solution.py:39
  150.5 4.5 %collective-permute-done.31 = bf16[32,4096]{1,0:T(8,128)(2,1)S(1)} collective-permute-done((bf16[32,4096]{1,0:T(8,128)(2,1)S(1)}, bf16[32,4096]{1,0:T(8,128)(2,1)S(1)}, u32[]{:S(2)}, u32[]{:S(2)}) %collective-permute-start.31) | collective-permute-done | bytes 262176 | tf_op jit(solution)/shard_map/ppermute | solution.py:39
  155.0 1.8 %collective-permute-done.29 = bf16[32,4096]{1,0:T(8,128)(2,1)S(1)} collective-permute-done((bf16[32,4096]{1,0:T(8,128)(2,1)S(1)}, bf16[32,4096]{1,0:T(8,128)(2,1)S(1)}, u32[]{:S(2)}, u32[]{:S(2)}) %collective-permute-start.29) | collective-permute-done | bytes 262176 | tf_op jit(solution)/shard_map/ppermute | solution.py:39
  157.1 2.1 %collective-permute-start.38 = (bf16[4,4096]{1,0:T(4,128)(2,1)S(1)}, bf16[4,4096]{1,0:T(4,128)(2,1)S(1)}, u32[]{:S(2)}, u32[]{:S(2)}) collective-permute-start(bf16[4,4096]{1,0:T(4,128)(2,1)S(1)} %get-tuple-element.73), channel_id=1, source_target_pairs={{0,24},{1,25},{2,26},{3,27},{4,28},{5,29},{6,30},{7,31},{8,16},{9,... | collective-permute-start | bytes 98312 | tf_op jit(solution)/shard_map/ppermute | solution.py:39
  159.1 2.4 %collective-permute-start.36 = (bf16[4,4096]{1,0:T(4,128)(2,1)S(1)}, bf16[4,4096]{1,0:T(4,128)(2,1)S(1)}, u32[]{:S(2)}, u32[]{:S(2)}) collective-permute-start(bf16[4,4096]{1,0:T(4,128)(2,1)S(1)} %get-tuple-element.72), channel_id=1, source_target_pairs={{0,8},{1,9},{2,10},{3,11},{4,12},{5,13},{6,14},{7,15},{8,0},{9,1},... | collective-permute-start | bytes 98312 | tf_op jit(solution)/shard_map/ppermute | solution.py:39
  163.2 2.1 %collective-permute-start.34 = (bf16[4,4096]{1,0:T(4,128)(2,1)S(1)}, bf16[4,4096]{1,0:T(4,128)(2,1)S(1)}, u32[]{:S(2)}, u32[]{:S(2)}) collective-permute-start(bf16[4,4096]{1,0:T(4,128)(2,1)S(1)} %get-tuple-element.70), channel_id=1, source_target_pairs={{0,144},{1,145},{2,146},{3,147},{4,148},{5,149},{6,150},{7,151},{8... | collective-permute-start | bytes 98312 | tf_op jit(solution)/shard_map/ppermute | solution.py:39
  165.3 2.3 %collective-permute-start.33 = (bf16[4,4096]{1,0:T(4,128)(2,1)S(1)}, bf16[4,4096]{1,0:T(4,128)(2,1)S(1)}, u32[]{:S(2)}, u32[]{:S(2)}) collective-permute-start(bf16[4,4096]{1,0:T(4,128)(2,1)S(1)} %get-tuple-element.71), channel_id=1, source_target_pairs={{0,136},{1,137},{2,138},{3,139},{4,140},{5,141},{6,142},{7,143},{8... | collective-permute-start | bytes 98312 | tf_op jit(solution)/shard_map/ppermute | solution.py:39
  167.6 3.3 %collective-permute-start.32 = (bf16[4,4096]{1,0:T(4,128)(2,1)S(1)}, bf16[4,4096]{1,0:T(4,128)(2,1)S(1)}, u32[]{:S(2)}, u32[]{:S(2)}) collective-permute-start(bf16[4,4096]{1,0:T(4,128)(2,1)S(1)} %get-tuple-element.68), channel_id=1, source_target_pairs={{0,128},{1,129},{2,130},{3,131},{4,132},{5,133},{6,134},{7,135},{8... | collective-permute-start | bytes 98312 | tf_op jit(solution)/shard_map/ppermute | solution.py:39
  172.2 3.2 %collective-permute-done.32 = bf16[4,4096]{1,0:T(4,128)(2,1)S(1)} collective-permute-done((bf16[4,4096]{1,0:T(4,128)(2,1)S(1)}, bf16[4,4096]{1,0:T(4,128)(2,1)S(1)}, u32[]{:S(2)}, u32[]{:S(2)}) %collective-permute-start.32) | collective-permute-done | bytes 32800 | tf_op jit(solution)/shard_map/ppermute | solution.py:39
  (106 shorter events, 35.0 us)
Async XLA Ops:
  3.4 15.4 %collective-permute-start.6 = (bf16[4,4096]{1,0:T(4,128)(2,1)S(1)}, bf16[4,4096]{1,0:T(4,128)(2,1)S(1)}, u32[]{:S(2)}, u32[]{:S(2)}) collective-permute-start(bf16[4,4096]{1,0:T(4,128)(2,1)S(1)} %get-tuple-element.75), channel_id=1, source_target_pairs={{0,2},{1,3},{2,4},{3,5},{4,6},{5,7},{6,0},{7,1},{8,10},{9,11},{10,... | collective-permute-start | bytes 98312 | tf_op jit(solution)/shard_map/ppermute | solution.py:39
  5.0 13.7 %collective-permute-start.5 = (bf16[4,4096]{1,0:T(4,128)(2,1)S(1)}, bf16[4,4096]{1,0:T(4,128)(2,1)S(1)}, u32[]{:S(2)}, u32[]{:S(2)}) collective-permute-start(bf16[4,4096]{1,0:T(4,128)(2,1)S(1)} %get-tuple-element.75), channel_id=1, source_target_pairs={{0,4},{1,5},{2,6},{3,7},{4,0},{5,1},{6,2},{7,3},{8,12},{9,13},{10,... | collective-permute-start | bytes 98312 | tf_op jit(solution)/shard_map/ppermute | solution.py:39
  7.7 11.0 %collective-permute-start.4 = (bf16[4,4096]{1,0:T(4,128)(2,1)S(1)}, bf16[4,4096]{1,0:T(4,128)(2,1)S(1)}, u32[]{:S(2)}, u32[]{:S(2)}) collective-permute-start(bf16[4,4096]{1,0:T(4,128)(2,1)S(1)} %get-tuple-element.75), channel_id=1, source_target_pairs={{0,6},{1,7},{2,0},{3,1},{4,2},{5,3},{6,4},{7,5},{8,14},{9,15},{10,... | collective-permute-start | bytes 98312 | tf_op jit(solution)/shard_map/ppermute | solution.py:39
  8.4 12.2 %collective-permute-start = (bf16[8,4096]{1,0:T(8,128)(2,1)}, bf16[8,4096]{1,0:T(8,128)(2,1)S(1)}, u32[]{:S(2)}, u32[]{:S(2)}) collective-permute-start(bf16[8,4096]{1,0:T(8,128)(2,1)} %bitcast.49), channel_id=1, source_target_pairs={{0,224},{1,225},{2,226},{3,227},{4,228},{5,229},{6,230},{7,231},{8... | collective-permute-start | bytes 196616 | tf_op jit(solution)/shard_map/ppermute | solution.py:39
  18.8 11.9 %collective-permute-start.7 = (bf16[16,4096]{1,0:T(8,128)(2,1)S(1)}, bf16[16,4096]{1,0:T(8,128)(2,1)S(1)}, u32[]{:S(2)}, u32[]{:S(2)}) collective-permute-start(bf16[16,4096]{1,0:T(8,128)(2,1)S(1)} %pad_maximum_fusion.2), channel_id=1, source_target_pairs={{0,128},{1,129},{2,130},{3,131},{4,132},{5,133},{6,134},{7,135},{8... | collective-permute-start | bytes 393224 | tf_op jit(solution)/shard_map/ppermute | solution.py:39
  20.6 12.1 %collective-permute-start.1 = (bf16[12,4096]{1,0:T(8,128)(2,1)S(1)}, bf16[12,4096]{1,0:T(8,128)(2,1)S(1)}, u32[]{:S(2)}, u32[]{:S(2)}) collective-permute-start(bf16[12,4096]{1,0:T(8,128)(2,1)S(1)} %pad_maximum_fusion.1), channel_id=1, source_target_pairs={{0,8},{1,9},{2,10},{3,11},{4,12},{5,13},{6,14},{7,15},{8,0},{9,1},... | collective-permute-start | bytes 294920 | tf_op jit(solution)/shard_map/ppermute | solution.py:39
  25.3 12.3 %collective-permute-start.2 = (bf16[12,4096]{1,0:T(8,128)(2,1)S(1)}, bf16[12,4096]{1,0:T(8,128)(2,1)S(1)}, u32[]{:S(2)}, u32[]{:S(2)}) collective-permute-start(bf16[12,4096]{1,0:T(8,128)(2,1)S(1)} %pad_maximum_fusion.1), channel_id=1, source_target_pairs={{0,16},{1,17},{2,18},{3,19},{4,20},{5,21},{6,22},{7,23},{8,24},{9,... | collective-permute-start | bytes 294920 | tf_op jit(solution)/shard_map/ppermute | solution.py:39
  25.5 12.1 %collective-permute-start.3 = (bf16[12,4096]{1,0:T(8,128)(2,1)S(1)}, bf16[12,4096]{1,0:T(8,128)(2,1)S(1)}, u32[]{:S(2)}, u32[]{:S(2)}) collective-permute-start(bf16[12,4096]{1,0:T(8,128)(2,1)S(1)} %pad_maximum_fusion.1), channel_id=1, source_target_pairs={{0,24},{1,25},{2,26},{3,27},{4,28},{5,29},{6,30},{7,31},{8,16},{9,... | collective-permute-start | bytes 294920 | tf_op jit(solution)/shard_map/ppermute | solution.py:39
  38.3 15.7 %collective-permute-start.12 = (bf16[48,4096]{1,0:T(8,128)(2,1)S(1)}, bf16[48,4096]{1,0:T(8,128)(2,1)S(1)}, u32[]{:S(2)}, u32[]{:S(2)}) collective-permute-start(bf16[48,4096]{1,0:T(8,128)(2,1)S(1)} %concatenate.44.refs_1_), channel_id=1, source_target_pairs={{0,6},{1,7},{2,0},{3,1},{4,2},{5,3},{6,4},{7,5},{8,14},{9,15},{10,... | collective-permute-start | bytes 1179656 | tf_op jit(solution)/shard_map/ppermute | solution.py:39
  39.7 14.3 %collective-permute-start.13 = (bf16[48,4096]{1,0:T(8,128)(2,1)S(1)}, bf16[48,4096]{1,0:T(8,128)(2,1)}, u32[]{:S(2)}, u32[]{:S(2)}) collective-permute-start(bf16[48,4096]{1,0:T(8,128)(2,1)S(1)} %concatenate.44.refs_1_), channel_id=1, source_target_pairs={{0,4},{1,5},{2,6},{3,7},{4,0},{5,1},{6,2},{7,3},{8,12},{9,13},{10,... | collective-permute-start | bytes 1179656 | tf_op jit(solution)/shard_map/ppermute | solution.py:39
  39.7 16.3 %collective-permute-start.14 = (bf16[48,4096]{1,0:T(8,128)(2,1)S(1)}, bf16[48,4096]{1,0:T(8,128)(2,1)}, u32[]{:S(2)}, u32[]{:S(2)}) collective-permute-start(bf16[48,4096]{1,0:T(8,128)(2,1)S(1)} %concatenate.44.refs_1_), channel_id=1, source_target_pairs={{0,2},{1,3},{2,4},{3,5},{4,6},{5,7},{6,0},{7,1},{8,10},{9,11},{10,... | collective-permute-start | bytes 1179656 | tf_op jit(solution)/shard_map/ppermute | solution.py:39
  47.7 22.6 %collective-permute-start.9 = (bf16[64,4096]{1,0:T(8,128)(2,1)S(1)}, bf16[64,4096]{1,0:T(8,128)(2,1)S(1)}, u32[]{:S(2)}, u32[]{:S(2)}) collective-permute-start(bf16[64,4096]{1,0:T(8,128)(2,1)S(1)} %constant_dynamic-update-slice_fusion.refs_0_), channel_id=1, source_target_pairs={{0,16},{1,17},{2,18},{3,19},{4,20},{5,21},{6,22},{7,23},{8,24},{9,... | collective-permute-start | bytes 1572872 | tf_op jit(solution)/shard_map/ppermute | solution.py:39
  54.1 18.0 %collective-permute-start.16 = (bf16[48,4096]{1,0:T(8,128)(2,1)S(1)}, bf16[48,4096]{1,0:T(8,128)(2,1)}, u32[]{:S(2)}, u32[]{:S(2)}) collective-permute-start(bf16[48,4096]{1,0:T(8,128)(2,1)S(1)} %collective-permute-done.12.refs_2_), channel_id=1, source_target_pairs={{0,1},{1,0},{2,3},{3,2},{4,5},{5,4},{6,7},{7,6},{8,9},{9,8},{10,11... | collective-permute-start | bytes 1179656 | tf_op jit(solution)/shard_map/ppermute | solution.py:39
  54.1 18.0 %collective-permute-start.17 = (bf16[48,4096]{1,0:T(8,128)(2,1)}, bf16[48,4096]{1,0:T(8,128)(2,1)}, u32[]{:S(2)}, u32[]{:S(2)}) collective-permute-start(bf16[48,4096]{1,0:T(8,128)(2,1)} %collective-permute-done.13.refs_3_), channel_id=1, source_target_pairs={{0,1},{1,0},{2,3},{3,2},{4,5},{5,4},{6,7},{7,6},{8,9},{9,8},{10,11... | collective-permute-start | bytes 1179656 | tf_op jit(solution)/shard_map/ppermute | solution.py:39
  56.0 16.1 %collective-permute-start.18 = (bf16[48,4096]{1,0:T(8,128)(2,1)}, bf16[48,4096]{1,0:T(8,128)(2,1)}, u32[]{:S(2)}, u32[]{:S(2)}) collective-permute-start(bf16[48,4096]{1,0:T(8,128)(2,1)} %collective-permute-done.14.refs_4_), channel_id=1, source_target_pairs={{0,1},{1,0},{2,3},{3,2},{4,5},{5,4},{6,7},{7,6},{8,9},{9,8},{10,11... | collective-permute-start | bytes 1179656 | tf_op jit(solution)/shard_map/ppermute | solution.py:39
  56.8 24.4 %collective-permute-start.10 = (bf16[64,4096]{1,0:T(8,128)(2,1)S(1)}, bf16[64,4096]{1,0:T(8,128)(2,1)S(1)}, u32[]{:S(2)}, u32[]{:S(2)}) collective-permute-start(bf16[64,4096]{1,0:T(8,128)(2,1)S(1)} %constant_dynamic-update-slice_fusion.refs_0_), channel_id=1, source_target_pairs={{0,1},{1,0},{2,3},{3,2},{4,5},{5,4},{6,7},{7,6},{8,9},{9,8},{10,11... | collective-permute-start | bytes 1572872 | tf_op jit(solution)/shard_map/ppermute | solution.py:39
  70.3 10.8 %collective-permute-start.11 = (bf16[64,4096]{1,0:T(8,128)(2,1)S(1)}, bf16[64,4096]{1,0:T(8,128)(2,1)S(1)}, u32[]{:S(2)}, u32[]{:S(2)}) collective-permute-start(bf16[64,4096]{1,0:T(8,128)(2,1)S(1)} %collective-permute-done.9.refs_1_), channel_id=1, source_target_pairs={{0,1},{1,0},{2,3},{3,2},{4,5},{5,4},{6,7},{7,6},{8,9},{9,8},{10,11... | collective-permute-start | bytes 1572872 | tf_op jit(solution)/shard_map/ppermute | solution.py:39
  95.0 11.8 %collective-permute-start.22 = (bf16[48,4096]{1,0:T(8,128)(2,1)S(1)}, bf16[48,4096]{1,0:T(8,128)(2,1)S(1)}, u32[]{:S(2)}, u32[]{:S(2)}) collective-permute-start(bf16[48,4096]{1,0:T(8,128)(2,1)S(1)} %get-tuple-element.56), channel_id=1, source_target_pairs={{0,6},{1,7},{2,0},{3,1},{4,2},{5,3},{6,4},{7,5},{8,14},{9,15},{10,... | collective-permute-start | bytes 1179656 | tf_op jit(solution)/shard_map/ppermute | solution.py:39
  96.4 20.0 %collective-permute-start.21 = (bf16[48,4096]{1,0:T(8,128)(2,1)S(1)}, bf16[48,4096]{1,0:T(8,128)(2,1)S(1)}, u32[]{:S(2)}, u32[]{:S(2)}) collective-permute-start(bf16[48,4096]{1,0:T(8,128)(2,1)S(1)} %get-tuple-element.57), channel_id=1, source_target_pairs={{0,4},{1,5},{2,6},{3,7},{4,0},{5,1},{6,2},{7,3},{8,12},{9,13},{10,... | collective-permute-start | bytes 1179656 | tf_op jit(solution)/shard_map/ppermute | solution.py:39
  98.9 18.2 %collective-permute-start.20 = (bf16[48,4096]{1,0:T(8,128)(2,1)S(1)}, bf16[48,4096]{1,0:T(8,128)(2,1)S(1)}, u32[]{:S(2)}, u32[]{:S(2)}) collective-permute-start(bf16[48,4096]{1,0:T(8,128)(2,1)S(1)} %get-tuple-element.55), channel_id=1, source_target_pairs={{0,2},{1,3},{2,4},{3,5},{4,6},{5,7},{6,0},{7,1},{8,10},{9,11},{10,... | collective-permute-start | bytes 1179656 | tf_op jit(solution)/shard_map/ppermute | solution.py:39
  100.7 28.3 %collective-permute-start.23 = (bf16[512,448]{1,0:T(8,128)(2,1)S(1)}, bf16[512,448]{1,0:T(8,128)(2,1)S(1)}, u32[]{:S(2)}, u32[]{:S(2)}) collective-permute-start(bf16[512,448]{1,0:T(8,128)(2,1)S(1)} %get-tuple-element.45), channel_id=1, source_target_pairs={{0,128},{1,129},{2,130},{3,131},{4,132},{5,133},{6,134},{7,135},{8... | collective-permute-start | bytes 1376264 | tf_op jit(solution)/shard_map/ppermute | solution.py:39
  137.1 8.4 %collective-permute-start.27 = (bf16[12,4096]{1,0:T(8,128)(2,1)S(1)}, bf16[12,4096]{1,0:T(8,128)(2,1)S(1)}, u32[]{:S(2)}, u32[]{:S(2)}) collective-permute-start(bf16[12,4096]{1,0:T(8,128)(2,1)S(1)} %get-tuple-element.62), channel_id=1, source_target_pairs={{0,24},{1,25},{2,26},{3,27},{4,28},{5,29},{6,30},{7,31},{8,16},{9,... | collective-permute-start | bytes 294920 | tf_op jit(solution)/shard_map/ppermute | solution.py:39
  139.1 11.0 %collective-permute-start.26 = (bf16[12,4096]{1,0:T(8,128)(2,1)S(1)}, bf16[12,4096]{1,0:T(8,128)(2,1)S(1)}, u32[]{:S(2)}, u32[]{:S(2)}) collective-permute-start(bf16[12,4096]{1,0:T(8,128)(2,1)S(1)} %get-tuple-element.63), channel_id=1, source_target_pairs={{0,16},{1,17},{2,18},{3,19},{4,20},{5,21},{6,22},{7,23},{8,24},{9,... | collective-permute-start | bytes 294920 | tf_op jit(solution)/shard_map/ppermute | solution.py:39
  139.1 11.0 %collective-permute-start.25 = (bf16[12,4096]{1,0:T(8,128)(2,1)S(1)}, bf16[12,4096]{1,0:T(8,128)(2,1)S(1)}, u32[]{:S(2)}, u32[]{:S(2)}) collective-permute-start(bf16[12,4096]{1,0:T(8,128)(2,1)S(1)} %get-tuple-element.61), channel_id=1, source_target_pairs={{0,8},{1,9},{2,10},{3,11},{4,12},{5,13},{6,14},{7,15},{8,0},{9,1},... | collective-permute-start | bytes 294920 | tf_op jit(solution)/shard_map/ppermute | solution.py:39
  141.6 13.4 %collective-permute-start.31 = (bf16[32,4096]{1,0:T(8,128)(2,1)S(1)}, bf16[32,4096]{1,0:T(8,128)(2,1)S(1)}, u32[]{:S(2)}, u32[]{:S(2)}) collective-permute-start(bf16[32,4096]{1,0:T(8,128)(2,1)S(1)} %get-tuple-element.59), channel_id=1, source_target_pairs={{0,6},{1,7},{2,0},{3,1},{4,2},{5,3},{6,4},{7,5},{8,14},{9,15},{10,... | collective-permute-start | bytes 786440 | tf_op jit(solution)/shard_map/ppermute | solution.py:39
  142.1 12.9 %collective-permute-start.30 = (bf16[32,4096]{1,0:T(8,128)(2,1)S(1)}, bf16[32,4096]{1,0:T(8,128)(2,1)S(1)}, u32[]{:S(2)}, u32[]{:S(2)}) collective-permute-start(bf16[32,4096]{1,0:T(8,128)(2,1)S(1)} %get-tuple-element.60), channel_id=1, source_target_pairs={{0,4},{1,5},{2,6},{3,7},{4,0},{5,1},{6,2},{7,3},{8,12},{9,13},{10,... | collective-permute-start | bytes 786440 | tf_op jit(solution)/shard_map/ppermute | solution.py:39
  145.4 11.4 %collective-permute-start.29 = (bf16[32,4096]{1,0:T(8,128)(2,1)S(1)}, bf16[32,4096]{1,0:T(8,128)(2,1)S(1)}, u32[]{:S(2)}, u32[]{:S(2)}) collective-permute-start(bf16[32,4096]{1,0:T(8,128)(2,1)S(1)} %get-tuple-element.58), channel_id=1, source_target_pairs={{0,2},{1,3},{2,4},{3,5},{4,6},{5,7},{6,0},{7,1},{8,10},{9,11},{10,... | collective-permute-start | bytes 786440 | tf_op jit(solution)/shard_map/ppermute | solution.py:39
  150.4 12.8 %collective-permute-start.28 = (bf16[8,4096]{1,0:T(8,128)(2,1)S(1)}, bf16[8,4096]{1,0:T(8,128)(2,1)S(1)}, u32[]{:S(2)}, u32[]{:S(2)}) collective-permute-start(bf16[8,4096]{1,0:T(8,128)(2,1)S(1)} %slice.172), channel_id=1, source_target_pairs={{0,32},{1,33},{2,34},{3,35},{4,36},{5,37},{6,38},{7,39},{8,40},{9,... | collective-permute-start | bytes 196616 | tf_op jit(solution)/shard_map/ppermute | solution.py:39
  159.1 8.4 %collective-permute-start.37 = (bf16[4,4096]{1,0:T(4,128)(2,1)S(1)}, bf16[4,4096]{1,0:T(4,128)(2,1)S(1)}, u32[]{:S(2)}, u32[]{:S(2)}) collective-permute-start(bf16[4,4096]{1,0:T(4,128)(2,1)S(1)} %get-tuple-element.74), channel_id=1, source_target_pairs={{0,16},{1,17},{2,18},{3,19},{4,20},{5,21},{6,22},{7,23},{8,24},{9,... | collective-permute-start | bytes 98312 | tf_op jit(solution)/shard_map/ppermute | solution.py:39
  159.1 12.4 %collective-permute-start.36 = (bf16[4,4096]{1,0:T(4,128)(2,1)S(1)}, bf16[4,4096]{1,0:T(4,128)(2,1)S(1)}, u32[]{:S(2)}, u32[]{:S(2)}) collective-permute-start(bf16[4,4096]{1,0:T(4,128)(2,1)S(1)} %get-tuple-element.72), channel_id=1, source_target_pairs={{0,8},{1,9},{2,10},{3,11},{4,12},{5,13},{6,14},{7,15},{8,0},{9,1},... | collective-permute-start | bytes 98312 | tf_op jit(solution)/shard_map/ppermute | solution.py:39
  161.6 10.0 %collective-permute-start.35 = (bf16[4,4096]{1,0:T(4,128)(2,1)S(1)}, bf16[4,4096]{1,0:T(4,128)(2,1)S(1)}, u32[]{:S(2)}, u32[]{:S(2)}) collective-permute-start(bf16[4,4096]{1,0:T(4,128)(2,1)S(1)} %get-tuple-element.69), channel_id=1, source_target_pairs={{0,152},{1,153},{2,154},{3,155},{4,156},{5,157},{6,158},{7,159},{8... | collective-permute-start | bytes 98312 | tf_op jit(solution)/shard_map/ppermute | solution.py:39
  163.2 8.4 %collective-permute-start.34 = (bf16[4,4096]{1,0:T(4,128)(2,1)S(1)}, bf16[4,4096]{1,0:T(4,128)(2,1)S(1)}, u32[]{:S(2)}, u32[]{:S(2)}) collective-permute-start(bf16[4,4096]{1,0:T(4,128)(2,1)S(1)} %get-tuple-element.70), channel_id=1, source_target_pairs={{0,144},{1,145},{2,146},{3,147},{4,148},{5,149},{6,150},{7,151},{8... | collective-permute-start | bytes 98312 | tf_op jit(solution)/shard_map/ppermute | solution.py:39
  (13 other events, 156.3 us)

commit v4 on v2

--- a/solution.py
+++ b/solution.py
@@ -240,6 +240,10 @@
         pltpu.with_memory_space_constraint(w, pltpu.HBM)
         for w in (gate_weight[0].T, up_weight[0].T, down_weight[0])
     ]
+    gate_near, up_near, down_near = [
+        pltpu.with_memory_space_constraint(w, pltpu.VMEM)
+        for w in (gate_weight[0].T, up_weight[0].T, down_weight[0])
+    ]
     slot_rows = returned[0]
 
     update_factor = step_rate / token_count
@@ -310,7 +314,7 @@
         [],
         per_row * token_count * 5,
         "terms",
-        [spread, hidden, grad_gate_act, grad_up_act, own_rows, gate_local, up_local, down_local],
+        [spread, hidden, grad_gate_act, grad_up_act, own_rows, gate_near, up_near, down_near],
     )
     from_core = send(other, dc=1)
     gate_part, up_part, gate_sent, up_sent = run(
@@ -328,7 +332,7 @@
         ],
         per_row * token_count * 5,
         "second",
-        nexts + [normed_all, grad_gate_act, grad_up_act, gate_local, up_local],
+        nexts + [normed_all, grad_gate_act, grad_up_act, gate_near, up_near],
     )
     mate_gate = send(gate_sent, ds=half_ring)
     mate_up = send(up_sent, ds=half_ring)
@@ -347,7 +351,7 @@
         [pltpu.VMEM((pair_tokens, units), BF16), pltpu.VMEM((pair_tokens, token_count), BF16)],
         per_row * token_count * 3,
         "third",
-        [gate_part, up_part, mate_gate, mate_up, hidden, cotangent, down_local],
+        [gate_part, up_part, mate_gate, mate_up, hidden, cotangent, down_near],
     )
     pair = add_up([mine, send(other, dc=1)]).astype(BF16)
     both = cut(after(both, pair), NZ)

time: 173 us -> 168 us (0.971)
  Pallas kernels: 25.5 us -> 21.8 us
    pallas_call x4, Pallas kernels: 25.5 us -> 21.8 us  [run(): pl.pallas_call(kernel, grid=(steps,), in_specs=in_specs, out_shape=outs,...]
where the time goes in v4:
time: 168 us; the launch traced here: 167 us
  waiting for transfers between devices  68.1 us (41%)
  starting transfers between devices  62.4 us (37%)
  Pallas kernels  21.8 us (13%)
  other arithmetic  8.09 us (5%)
  local copies, waits for them, and re-layouts  3.6 us (2%)
    ppermute x40, waiting for transfers between devices, send(): return lax.ppermute(value, ('section', 'rep'), pairs)  68.1 us
    ppermute x40, starting transfers between devices, send(): return lax.ppermute(value, ('section', 'rep'), pairs)  62.4 us
    pallas_call x4, Pallas kernels, run(): pl.pallas_call(kernel, grid=(steps,), in_specs=in_specs, out_shape=outs,...  21.8 us
  transfers between devices with their start and end apart: 40, of which 22 were waited for; matrix products, arithmetic and copies ran while one was open for 5% of the time, Pallas kernels for 8%

profile of v4, /device:TPU:8, one launch (start us, length us, event | category | flops | bytes accessed | tf_op | source)
XLA Modules:
  0.0 166.6 jit_solution(970436610579707252)
XLA Ops:
  0.6 9.5 %collective-permute-start = (bf16[8,4096]{1,0:T(8,128)(2,1)}, bf16[8,4096]{1,0:T(8,128)(2,1)S(1)}, u32[]{:S(2)}, u32[]{:S(2)}) collective-permute-start(bf16[8,4096]{1,0:T(8,128)(2,1)} %bitcast.49), channel_id=1, source_target_pairs={{0,224},{1,225},{2,226},{3,227},{4,228},{5,229},{6,230},{7,231},{8... | collective-permute-start | bytes 196616 | tf_op jit(solution)/shard_map/ppermute | solution.py:39
  13.9 6.8 %collective-permute-done.4 = bf16[4,4096]{1,0:T(4,128)(2,1)S(1)} collective-permute-done((bf16[4,4096]{1,0:T(4,128)(2,1)S(1)}, bf16[4,4096]{1,0:T(4,128)(2,1)S(1)}, u32[]{:S(2)}, u32[]{:S(2)}) %collective-permute-start.4) | collective-permute-done | bytes 32800 | tf_op jit(solution)/shard_map/ppermute | solution.py:39
  22.1 3.1 %collective-permute-done.5 = bf16[8,4096]{1,0:T(8,128)(2,1)S(1)} collective-permute-done((bf16[8,4096]{1,0:T(8,128)(2,1)S(1)}, bf16[8,4096]{1,0:T(8,128)(2,1)S(1)}, u32[]{:S(2)}, u32[]{:S(2)}) %collective-permute-start.5) | collective-permute-done | bytes 65568 | tf_op jit(solution)/shard_map/ppermute | solution.py:39
  28.4 1.8 %collective-permute-start.3 = (bf16[12,4096]{1,0:T(8,128)(2,1)S(1)}, bf16[12,4096]{1,0:T(8,128)(2,1)S(1)}, u32[]{:S(2)}, u32[]{:S(2)}) collective-permute-start(bf16[12,4096]{1,0:T(8,128)(2,1)S(1)} %pad_maximum_fusion), channel_id=1, source_target_pairs={{0,24},{1,25},{2,26},{3,27},{4,28},{5,29},{6,30},{7,31},{8,16},{9,... | collective-permute-start | bytes 294920 | tf_op jit(solution)/shard_map/ppermute | solution.py:39
  30.2 2.6 %collective-permute-start.7 = (bf16[16,4096]{1,0:T(8,128)(2,1)S(1)}, bf16[16,4096]{1,0:T(8,128)(2,1)S(1)}, u32[]{:S(2)}, u32[]{:S(2)}) collective-permute-start(bf16[16,4096]{1,0:T(8,128)(2,1)S(1)} %get-tuple-element.75), channel_id=1, source_target_pairs={{0,4},{1,5},{2,6},{3,7},{4,0},{5,1},{6,2},{7,3},{8,12},{9,13},{10,... | collective-permute-start | bytes 393224 | tf_op jit(solution)/shard_map/ppermute | solution.py:39
  33.0 1.7 %collective-permute-start.8 = (bf16[16,4096]{1,0:T(8,128)(2,1)S(1)}, bf16[16,4096]{1,0:T(8,128)(2,1)S(1)}, u32[]{:S(2)}, u32[]{:S(2)}) collective-permute-start(bf16[16,4096]{1,0:T(8,128)(2,1)S(1)} %get-tuple-element.75), channel_id=1, source_target_pairs={{0,2},{1,3},{2,4},{3,5},{4,6},{5,7},{6,0},{7,1},{8,10},{9,11},{10,... | collective-permute-start | bytes 393224 | tf_op jit(solution)/shard_map/ppermute | solution.py:39
  34.7 2.2 %collective-permute-done.2 = bf16[12,4096]{1,0:T(8,128)(2,1)S(1)} collective-permute-done((bf16[12,4096]{1,0:T(8,128)(2,1)S(1)}, bf16[12,4096]{1,0:T(8,128)(2,1)S(1)}, u32[]{:S(2)}, u32[]{:S(2)}) %collective-permute-start.2) | collective-permute-done | bytes 98336 | tf_op jit(solution)/shard_map/ppermute | solution.py:39
  37.7 1.6 collective-permute-done.8
  39.3 7.7 %collective-permute-start.12 = (bf16[48,4096]{1,0:T(8,128)(2,1)S(1)}, bf16[48,4096]{1,0:T(8,128)(2,1)S(1)}, u32[]{:S(2)}, u32[]{:S(2)}) collective-permute-start(bf16[48,4096]{1,0:T(8,128)(2,1)S(1)} %concatenate.45.refs_1_), channel_id=1, source_target_pairs={{0,6},{1,7},{2,0},{3,1},{4,2},{5,3},{6,4},{7,5},{8,14},{9,15},{10,... | collective-permute-start | bytes 1179656 | tf_op jit(solution)/shard_map/ppermute | solution.py:39
  47.0 1.6 collective-permute-start.14
  50.0 2.3 %collective-permute-done.12.refs_2_ = bf16[48,4096]{1,0:T(8,128)(2,1)S(1)} collective-permute-done((bf16[48,4096]{1,0:T(8,128)(2,1)S(1)}, bf16[48,4096]{1,0:T(8,128)(2,1)S(1)}, u32[]{:S(2)}, u32[]{:S(2)}) %collective-permute-start.12) | collective-permute-done | bytes 393248 | tf_op jit(solution)/shard_map/ppermute | solution.py:39
  52.3 4.2 %collective-permute-done.13.refs_3_ = bf16[48,4096]{1,0:T(8,128)(2,1)} collective-permute-done((bf16[48,4096]{1,0:T(8,128)(2,1)S(1)}, bf16[48,4096]{1,0:T(8,128)(2,1)}, u32[]{:S(2)}, u32[]{:S(2)}) %collective-permute-start.13) | collective-permute-done | bytes 393248 | tf_op jit(solution)/shard_map/ppermute | solution.py:39
  58.5 7.7 %collective-permute-done.9.refs_1_ = bf16[64,4096]{1,0:T(8,128)(2,1)S(1)} collective-permute-done((bf16[64,4096]{1,0:T(8,128)(2,1)S(1)}, bf16[64,4096]{1,0:T(8,128)(2,1)S(1)}, u32[]{:S(2)}, u32[]{:S(2)}) %collective-permute-start.9) | collective-permute-done | bytes 524320 | tf_op jit(solution)/shard_map/ppermute | solution.py:39
  69.0 9.5 %first.1 = (bf16[128,4096]{1,0:T(8,128)(2,1)S(1)}, bf16[128,4096]{1,0:T(8,128)(2,1)S(1)}, bf16[128,448]{1,0:T(8,128)(2,1)S(1)}, bf16[128,448]{1,0:T(8,128)(2,1)S(1)}, bf16[128,448]{1,0:T(8,128)(2,1)S(1)}) custom-call(bf16[256,384]{1,0:T(8,128)(2,1)S(1)} %copy.14.refs_0_, bf16[48,4096]{1,0:T(8,128)(2,1)S(1)} %concatenate.45.refs_1_, ...), custom_call_target="tpu_custom_call" | custom-call | flops 1879048192 | bytes 14352384 | tf_op jit(solution)/shard_map/first/pallas_call | solution.py:218
  78.6 4.4 %terms.1 = (bf16[192,4096]{1,0:T(8,128)(2,1)S(1)}, bf16[192,4096]{1,0:T(8,128)(2,1)S(1)}) custom-call(bf16[384,256]{1,0:T(8,128)(2,1)S(1)} %bitcast.44, bf16[128,448]{1,0:T(8,128)(2,1)S(1)} %get-tuple-element.43.hidden, bf16[128,448]{1,0:T(8,128)(2,1)S(1)} %get-tuple-element.38.refs_5_.dgate, bf16[128,448]{1,0:T(8,128)(2,1)S(1)} %get-tuple-element.39.refs_6_.dup, ...), custom_call_target="tpu_custom_call" | custom-call | flops 2348810240 | bytes 11681792 | tf_op jit(solution)/shard_map/terms/pallas_call | solution.py:218
  83.6 4.5 %second.1 = (f32[256,448]{1,0:T(8,128)S(1)}, f32[256,448]{1,0:T(8,128)S(1)}, bf16[256,448]{1,0:T(8,128)(2,1)S(1)}, bf16[256,448]{1,0:T(8,128)(2,1)S(1)}) custom-call(bf16[64,4096]{1,0:T(8,128)(2,1)S(1)} %constant_dynamic-update-slice_fusion.2.refs_0_, bf16[64,4096]{1,0:T(8,128)(2,1)S(1)} %collective-permute-done.9.refs_1_, ...), custom_call_target="tpu_custom_call" | custom-call | flops 2348810240 | bytes 10715136 | tf_op jit(solution)/shard_map/second/pallas_call | solution.py:218
  88.9 3.1 %collective-permute-start.21 = (bf16[48,4096]{1,0:T(8,128)(2,1)S(1)}, bf16[48,4096]{1,0:T(8,128)(2,1)S(1)}, u32[]{:S(2)}, u32[]{:S(2)}) collective-permute-start(bf16[48,4096]{1,0:T(8,128)(2,1)S(1)} %get-tuple-element.59), channel_id=1, source_target_pairs={{0,4},{1,5},{2,6},{3,7},{4,0},{5,1},{6,2},{7,3},{8,12},{9,13},{10,... | collective-permute-start | bytes 1179656 | tf_op jit(solution)/shard_map/ppermute | solution.py:39
  92.9 2.3 %collective-permute-start.23 = (bf16[256,448]{1,0:T(8,128)(2,1)S(1)}, bf16[256,448]{1,0:T(8,128)(2,1)S(1)}, u32[]{:S(2)}, u32[]{:S(2)}) collective-permute-start(bf16[256,448]{1,0:T(8,128)(2,1)S(1)} %get-tuple-element.46), channel_id=1, source_target_pairs={{0,128},{1,129},{2,130},{3,131},{4,132},{5,133},{6,134},{7,135},{8... | collective-permute-start | bytes 688136 | tf_op jit(solution)/shard_map/ppermute | solution.py:39
  95.2 3.6 %collective-permute-start.24 = (bf16[256,448]{1,0:T(8,128)(2,1)S(1)}, bf16[256,448]{1,0:T(8,128)(2,1)S(1)}, u32[]{:S(2)}, u32[]{:S(2)}) collective-permute-start(bf16[256,448]{1,0:T(8,128)(2,1)S(1)} %get-tuple-element.47), channel_id=1, source_target_pairs={{0,128},{1,129},{2,130},{3,131},{4,132},{5,133},{6,134},{7,135},{8... | collective-permute-start | bytes 688136 | tf_op jit(solution)/shard_map/ppermute | solution.py:39
  99.9 9.5 %collective-permute-done.21 = bf16[48,4096]{1,0:T(8,128)(2,1)S(1)} collective-permute-done((bf16[48,4096]{1,0:T(8,128)(2,1)S(1)}, bf16[48,4096]{1,0:T(8,128)(2,1)S(1)}, u32[]{:S(2)}, u32[]{:S(2)}) %collective-permute-start.21) | collective-permute-done | bytes 393248 | tf_op jit(solution)/shard_map/ppermute | solution.py:39
  110.4 4.1 %collective-permute-done.23.mate_gate = bf16[256,448]{1,0:T(8,128)(2,1)S(1)} collective-permute-done((bf16[256,448]{1,0:T(8,128)(2,1)S(1)}, bf16[256,448]{1,0:T(8,128)(2,1)S(1)}, u32[]{:S(2)}, u32[]{:S(2)}) %collective-permute-start.23) | collective-permute-done | bytes 229408 | tf_op jit(solution)/shard_map/ppermute | solution.py:39
  114.5 5.5 %collective-permute-done.24.mate_up = bf16[256,448]{1,0:T(8,128)(2,1)S(1)} collective-permute-done((bf16[256,448]{1,0:T(8,128)(2,1)S(1)}, bf16[256,448]{1,0:T(8,128)(2,1)S(1)}, u32[]{:S(2)}, u32[]{:S(2)}) %collective-permute-start.24) | collective-permute-done | bytes 229408 | tf_op jit(solution)/shard_map/ppermute | solution.py:39
  120.0 3.4 %third.1 = (bf16[128,4096]{1,0:T(8,128)(2,1)S(1)}, bf16[128,4096]{1,0:T(8,128)(2,1)S(1)}) custom-call(f32[256,448]{1,0:T(8,128)S(1)} %get-tuple-element.50.gate, f32[256,448]{1,0:T(8,128)S(1)} %get-tuple-element.51.up, bf16[256,448]{1,0:T(8,128)(2,1)S(1)} %collective-permute-done.23.mate_gate, bf16[256,448]{1,0:T(8,128)(2,1)S(1)} %collective-permute-done.24.mate_up, ...), custom_call_target="tpu_custom_call" | custom-call | flops 1409286144 | bytes 6209536 | tf_op jit(solution)/shard_map/third/pallas_call | solution.py:218
  123.4 2.6 %collective-permute-done.25 = bf16[128,4096]{1,0:T(8,128)(2,1)S(1)} collective-permute-done((bf16[128,4096]{1,0:T(8,128)(2,1)S(1)}, bf16[128,4096]{1,0:T(8,128)(2,1)S(1)}, u32[]{:S(2)}, u32[]{:S(2)}) %collective-permute-start.25) | collective-permute-done | bytes 1048608 | tf_op jit(solution)/shard_map/ppermute | solution.py:39
  127.1 3.8 %collective-permute-start.26 = (bf16[12,4096]{1,0:T(8,128)(2,1)S(1)}, bf16[12,4096]{1,0:T(8,128)(2,1)S(1)}, u32[]{:S(2)}, u32[]{:S(2)}) collective-permute-start(bf16[12,4096]{1,0:T(8,128)(2,1)S(1)} %get-tuple-element.63), channel_id=1, source_target_pairs={{0,8},{1,9},{2,10},{3,11},{4,12},{5,13},{6,14},{7,15},{8,0},{9,1},... | collective-permute-start | bytes 294920 | tf_op jit(solution)/shard_map/ppermute | solution.py:39
  135.9 3.1 %collective-permute-done.27 = bf16[12,4096]{1,0:T(8,128)(2,1)S(1)} collective-permute-done((bf16[12,4096]{1,0:T(8,128)(2,1)S(1)}, bf16[12,4096]{1,0:T(8,128)(2,1)S(1)}, u32[]{:S(2)}, u32[]{:S(2)}) %collective-permute-start.27) | collective-permute-done | bytes 98336 | tf_op jit(solution)/shard_map/ppermute | solution.py:39
  139.6 5.1 %collective-permute-done.31 = bf16[32,4096]{1,0:T(8,128)(2,1)S(1)} collective-permute-done((bf16[32,4096]{1,0:T(8,128)(2,1)S(1)}, bf16[32,4096]{1,0:T(8,128)(2,1)S(1)}, u32[]{:S(2)}, u32[]{:S(2)}) %collective-permute-start.31) | collective-permute-done | bytes 262176 | tf_op jit(solution)/shard_map/ppermute | solution.py:39
  148.1 2.6 %collective-permute-start.37 = (bf16[4,4096]{1,0:T(4,128)(2,1)S(1)}, bf16[4,4096]{1,0:T(4,128)(2,1)S(1)}, u32[]{:S(2)}, u32[]{:S(2)}) collective-permute-start(bf16[4,4096]{1,0:T(4,128)(2,1)S(1)} %get-tuple-element.72), channel_id=1, source_target_pairs={{0,8},{1,9},{2,10},{3,11},{4,12},{5,13},{6,14},{7,15},{8,0},{9,1},... | collective-permute-start | bytes 98312 | tf_op jit(solution)/shard_map/ppermute | solution.py:39
  151.6 2.9 %collective-permute-start.35 = (bf16[4,4096]{1,0:T(4,128)(2,1)S(1)}, bf16[4,4096]{1,0:T(4,128)(2,1)S(1)}, u32[]{:S(2)}, u32[]{:S(2)}) collective-permute-start(bf16[4,4096]{1,0:T(4,128)(2,1)S(1)} %get-tuple-element.70), channel_id=1, source_target_pairs={{0,144},{1,145},{2,146},{3,147},{4,148},{5,149},{6,150},{7,151},{8... | collective-permute-start | bytes 98312 | tf_op jit(solution)/shard_map/ppermute | solution.py:39
  154.4 3.0 %collective-permute-start.34 = (bf16[4,4096]{1,0:T(4,128)(2,1)S(1)}, bf16[4,4096]{1,0:T(4,128)(2,1)S(1)}, u32[]{:S(2)}, u32[]{:S(2)}) collective-permute-start(bf16[4,4096]{1,0:T(4,128)(2,1)S(1)} %get-tuple-element.71), channel_id=1, source_target_pairs={{0,136},{1,137},{2,138},{3,139},{4,140},{5,141},{6,142},{7,143},{8... | collective-permute-start | bytes 98312 | tf_op jit(solution)/shard_map/ppermute | solution.py:39
  157.5 2.6 %collective-permute-start.33 = (bf16[4,4096]{1,0:T(4,128)(2,1)S(1)}, bf16[4,4096]{1,0:T(4,128)(2,1)S(1)}, u32[]{:S(2)}, u32[]{:S(2)}) collective-permute-start(bf16[4,4096]{1,0:T(4,128)(2,1)S(1)} %get-tuple-element.68), channel_id=1, source_target_pairs={{0,128},{1,129},{2,130},{3,131},{4,132},{5,133},{6,134},{7,135},{8... | collective-permute-start | bytes 98312 | tf_op jit(solution)/shard_map/ppermute | solution.py:39
  161.7 3.6 %collective-permute-done.33 = bf16[4,4096]{1,0:T(4,128)(2,1)S(1)} collective-permute-done((bf16[4,4096]{1,0:T(4,128)(2,1)S(1)}, bf16[4,4096]{1,0:T(4,128)(2,1)S(1)}, u32[]{:S(2)}, u32[]{:S(2)}) %collective-permute-start.33) | collective-permute-done | bytes 32800 | tf_op jit(solution)/shard_map/ppermute | solution.py:39
  (116 shorter events, 33.5 us)
Async XLA Ops:
  0.6 20.2 %collective-permute-start = (bf16[8,4096]{1,0:T(8,128)(2,1)}, bf16[8,4096]{1,0:T(8,128)(2,1)S(1)}, u32[]{:S(2)}, u32[]{:S(2)}) collective-permute-start(bf16[8,4096]{1,0:T(8,128)(2,1)} %bitcast.49), channel_id=1, source_target_pairs={{0,224},{1,225},{2,226},{3,227},{4,228},{5,229},{6,230},{7,231},{8... | collective-permute-start | bytes 196616 | tf_op jit(solution)/shard_map/ppermute | solution.py:39
  12.8 7.9 %collective-permute-start.4 = (bf16[4,4096]{1,0:T(4,128)(2,1)S(1)}, bf16[4,4096]{1,0:T(4,128)(2,1)S(1)}, u32[]{:S(2)}, u32[]{:S(2)}) collective-permute-start(bf16[4,4096]{1,0:T(4,128)(2,1)S(1)} %get-tuple-element.81), channel_id=1, source_target_pairs={{0,128},{1,129},{2,130},{3,131},{4,132},{5,133},{6,134},{7,135},{8... | collective-permute-start | bytes 98312 | tf_op jit(solution)/shard_map/ppermute | solution.py:39
  25.2 12.5 %collective-permute-start.6 = (bf16[16,4096]{1,0:T(8,128)(2,1)S(1)}, bf16[16,4096]{1,0:T(8,128)(2,1)S(1)}, u32[]{:S(2)}, u32[]{:S(2)}) collective-permute-start(bf16[16,4096]{1,0:T(8,128)(2,1)S(1)} %get-tuple-element.75), channel_id=1, source_target_pairs={{0,6},{1,7},{2,0},{3,1},{4,2},{5,3},{6,4},{7,5},{8,14},{9,15},{10,... | collective-permute-start | bytes 393224 | tf_op jit(solution)/shard_map/ppermute | solution.py:39
  27.0 10.0 %collective-permute-start.2 = (bf16[12,4096]{1,0:T(8,128)(2,1)S(1)}, bf16[12,4096]{1,0:T(8,128)(2,1)S(1)}, u32[]{:S(2)}, u32[]{:S(2)}) collective-permute-start(bf16[12,4096]{1,0:T(8,128)(2,1)S(1)} %pad_maximum_fusion), channel_id=1, source_target_pairs={{0,16},{1,17},{2,18},{3,19},{4,20},{5,21},{6,22},{7,23},{8,24},{9,... | collective-permute-start | bytes 294920 | tf_op jit(solution)/shard_map/ppermute | solution.py:39
  28.4 8.5 %collective-permute-start.3 = (bf16[12,4096]{1,0:T(8,128)(2,1)S(1)}, bf16[12,4096]{1,0:T(8,128)(2,1)S(1)}, u32[]{:S(2)}, u32[]{:S(2)}) collective-permute-start(bf16[12,4096]{1,0:T(8,128)(2,1)S(1)} %pad_maximum_fusion), channel_id=1, source_target_pairs={{0,24},{1,25},{2,26},{3,27},{4,28},{5,29},{6,30},{7,31},{8,16},{9,... | collective-permute-start | bytes 294920 | tf_op jit(solution)/shard_map/ppermute | solution.py:39
  39.3 13.0 %collective-permute-start.12 = (bf16[48,4096]{1,0:T(8,128)(2,1)S(1)}, bf16[48,4096]{1,0:T(8,128)(2,1)S(1)}, u32[]{:S(2)}, u32[]{:S(2)}) collective-permute-start(bf16[48,4096]{1,0:T(8,128)(2,1)S(1)} %concatenate.45.refs_1_), channel_id=1, source_target_pairs={{0,6},{1,7},{2,0},{3,1},{4,2},{5,3},{6,4},{7,5},{8,14},{9,15},{10,... | collective-permute-start | bytes 1179656 | tf_op jit(solution)/shard_map/ppermute | solution.py:39
  47.0 9.5 %collective-permute-start.13 = (bf16[48,4096]{1,0:T(8,128)(2,1)S(1)}, bf16[48,4096]{1,0:T(8,128)(2,1)}, u32[]{:S(2)}, u32[]{:S(2)}) collective-permute-start(bf16[48,4096]{1,0:T(8,128)(2,1)S(1)} %concatenate.45.refs_1_), channel_id=1, source_target_pairs={{0,4},{1,5},{2,6},{3,7},{4,0},{5,1},{6,2},{7,3},{8,12},{9,13},{10,... | collective-permute-start | bytes 1179656 | tf_op jit(solution)/shard_map/ppermute | solution.py:39
  47.0 10.2 %collective-permute-start.14 = (bf16[48,4096]{1,0:T(8,128)(2,1)S(1)}, bf16[48,4096]{1,0:T(8,128)(2,1)}, u32[]{:S(2)}, u32[]{:S(2)}) collective-permute-start(bf16[48,4096]{1,0:T(8,128)(2,1)S(1)} %concatenate.45.refs_1_), channel_id=1, source_target_pairs={{0,2},{1,3},{2,4},{3,5},{4,6},{5,7},{6,0},{7,1},{8,10},{9,11},{10,... | collective-permute-start | bytes 1179656 | tf_op jit(solution)/shard_map/ppermute | solution.py:39
  48.6 17.6 %collective-permute-start.9 = (bf16[64,4096]{1,0:T(8,128)(2,1)S(1)}, bf16[64,4096]{1,0:T(8,128)(2,1)S(1)}, u32[]{:S(2)}, u32[]{:S(2)}) collective-permute-start(bf16[64,4096]{1,0:T(8,128)(2,1)S(1)} %constant_dynamic-update-slice_fusion.2.refs_0_), channel_id=1, source_target_pairs={{0,16},{1,17},{2,18},{3,19},{4,20},{5,21},{6,22},{7,23},{8,24},{9,... | collective-permute-start | bytes 1572872 | tf_op jit(solution)/shard_map/ppermute | solution.py:39
  48.6 8.7 %collective-permute-start.15 = (bf16[48,4096]{1,0:T(8,128)(2,1)S(1)}, bf16[48,4096]{1,0:T(8,128)(2,1)S(1)}, u32[]{:S(2)}, u32[]{:S(2)}) collective-permute-start(bf16[48,4096]{1,0:T(8,128)(2,1)S(1)} %concatenate.45.refs_1_), channel_id=1, source_target_pairs={{0,1},{1,0},{2,3},{3,2},{4,5},{5,4},{6,7},{7,6},{8,9},{9,8},{10,11... | collective-permute-start | bytes 1179656 | tf_op jit(solution)/shard_map/ppermute | solution.py:39
  52.3 15.7 %collective-permute-start.16 = (bf16[48,4096]{1,0:T(8,128)(2,1)S(1)}, bf16[48,4096]{1,0:T(8,128)(2,1)}, u32[]{:S(2)}, u32[]{:S(2)}) collective-permute-start(bf16[48,4096]{1,0:T(8,128)(2,1)S(1)} %collective-permute-done.12.refs_2_), channel_id=1, source_target_pairs={{0,1},{1,0},{2,3},{3,2},{4,5},{5,4},{6,7},{7,6},{8,9},{9,8},{10,11... | collective-permute-start | bytes 1179656 | tf_op jit(solution)/shard_map/ppermute | solution.py:39
  56.5 11.5 %collective-permute-start.17 = (bf16[48,4096]{1,0:T(8,128)(2,1)}, bf16[48,4096]{1,0:T(8,128)(2,1)}, u32[]{:S(2)}, u32[]{:S(2)}) collective-permute-start(bf16[48,4096]{1,0:T(8,128)(2,1)} %collective-permute-done.13.refs_3_), channel_id=1, source_target_pairs={{0,1},{1,0},{2,3},{3,2},{4,5},{5,4},{6,7},{7,6},{8,9},{9,8},{10,11... | collective-permute-start | bytes 1179656 | tf_op jit(solution)/shard_map/ppermute | solution.py:39
  57.2 10.8 %collective-permute-start.18 = (bf16[48,4096]{1,0:T(8,128)(2,1)}, bf16[48,4096]{1,0:T(8,128)(2,1)}, u32[]{:S(2)}, u32[]{:S(2)}) collective-permute-start(bf16[48,4096]{1,0:T(8,128)(2,1)} %collective-permute-done.14.refs_4_), channel_id=1, source_target_pairs={{0,1},{1,0},{2,3},{3,2},{4,5},{5,4},{6,7},{7,6},{8,9},{9,8},{10,11... | collective-permute-start | bytes 1179656 | tf_op jit(solution)/shard_map/ppermute | solution.py:39
  58.0 20.5 %collective-permute-start.10 = (bf16[64,4096]{1,0:T(8,128)(2,1)S(1)}, bf16[64,4096]{1,0:T(8,128)(2,1)S(1)}, u32[]{:S(2)}, u32[]{:S(2)}) collective-permute-start(bf16[64,4096]{1,0:T(8,128)(2,1)S(1)} %constant_dynamic-update-slice_fusion.2.refs_0_), channel_id=1, source_target_pairs={{0,1},{1,0},{2,3},{3,2},{4,5},{5,4},{6,7},{7,6},{8,9},{9,8},{10,11... | collective-permute-start | bytes 1572872 | tf_op jit(solution)/shard_map/ppermute | solution.py:39
  66.2 12.4 %collective-permute-start.11 = (bf16[64,4096]{1,0:T(8,128)(2,1)S(1)}, bf16[64,4096]{1,0:T(8,128)(2,1)S(1)}, u32[]{:S(2)}, u32[]{:S(2)}) collective-permute-start(bf16[64,4096]{1,0:T(8,128)(2,1)S(1)} %collective-permute-done.9.refs_1_), channel_id=1, source_target_pairs={{0,1},{1,0},{2,3},{3,2},{4,5},{5,4},{6,7},{7,6},{8,9},{9,8},{10,11... | collective-permute-start | bytes 1572872 | tf_op jit(solution)/shard_map/ppermute | solution.py:39
  88.8 11.1 %collective-permute-start.22 = (bf16[48,4096]{1,0:T(8,128)(2,1)S(1)}, bf16[48,4096]{1,0:T(8,128)(2,1)S(1)}, u32[]{:S(2)}, u32[]{:S(2)}) collective-permute-start(bf16[48,4096]{1,0:T(8,128)(2,1)S(1)} %get-tuple-element.58), channel_id=1, source_target_pairs={{0,6},{1,7},{2,0},{3,1},{4,2},{5,3},{6,4},{7,5},{8,14},{9,15},{10,... | collective-permute-start | bytes 1179656 | tf_op jit(solution)/shard_map/ppermute | solution.py:39
  88.9 20.6 %collective-permute-start.21 = (bf16[48,4096]{1,0:T(8,128)(2,1)S(1)}, bf16[48,4096]{1,0:T(8,128)(2,1)S(1)}, u32[]{:S(2)}, u32[]{:S(2)}) collective-permute-start(bf16[48,4096]{1,0:T(8,128)(2,1)S(1)} %get-tuple-element.59), channel_id=1, source_target_pairs={{0,4},{1,5},{2,6},{3,7},{4,0},{5,1},{6,2},{7,3},{8,12},{9,13},{10,... | collective-permute-start | bytes 1179656 | tf_op jit(solution)/shard_map/ppermute | solution.py:39
  92.0 18.2 %collective-permute-start.20 = (bf16[48,4096]{1,0:T(8,128)(2,1)S(1)}, bf16[48,4096]{1,0:T(8,128)(2,1)S(1)}, u32[]{:S(2)}, u32[]{:S(2)}) collective-permute-start(bf16[48,4096]{1,0:T(8,128)(2,1)S(1)} %get-tuple-element.57), channel_id=1, source_target_pairs={{0,2},{1,3},{2,4},{3,5},{4,6},{5,7},{6,0},{7,1},{8,10},{9,11},{10,... | collective-permute-start | bytes 1179656 | tf_op jit(solution)/shard_map/ppermute | solution.py:39
  92.9 21.6 %collective-permute-start.23 = (bf16[256,448]{1,0:T(8,128)(2,1)S(1)}, bf16[256,448]{1,0:T(8,128)(2,1)S(1)}, u32[]{:S(2)}, u32[]{:S(2)}) collective-permute-start(bf16[256,448]{1,0:T(8,128)(2,1)S(1)} %get-tuple-element.46), channel_id=1, source_target_pairs={{0,128},{1,129},{2,130},{3,131},{4,132},{5,133},{6,134},{7,135},{8... | collective-permute-start | bytes 688136 | tf_op jit(solution)/shard_map/ppermute | solution.py:39
  95.2 24.8 %collective-permute-start.24 = (bf16[256,448]{1,0:T(8,128)(2,1)S(1)}, bf16[256,448]{1,0:T(8,128)(2,1)S(1)}, u32[]{:S(2)}, u32[]{:S(2)}) collective-permute-start(bf16[256,448]{1,0:T(8,128)(2,1)S(1)} %get-tuple-element.47), channel_id=1, source_target_pairs={{0,128},{1,129},{2,130},{3,131},{4,132},{5,133},{6,134},{7,135},{8... | collective-permute-start | bytes 688136 | tf_op jit(solution)/shard_map/ppermute | solution.py:39
  126.4 8.4 %collective-permute-start.28 = (bf16[12,4096]{1,0:T(8,128)(2,1)S(1)}, bf16[12,4096]{1,0:T(8,128)(2,1)S(1)}, u32[]{:S(2)}, u32[]{:S(2)}) collective-permute-start(bf16[12,4096]{1,0:T(8,128)(2,1)S(1)} %get-tuple-element.64), channel_id=1, source_target_pairs={{0,24},{1,25},{2,26},{3,27},{4,28},{5,29},{6,30},{7,31},{8,16},{9,... | collective-permute-start | bytes 294920 | tf_op jit(solution)/shard_map/ppermute | solution.py:39
  127.1 11.8 %collective-permute-start.27 = (bf16[12,4096]{1,0:T(8,128)(2,1)S(1)}, bf16[12,4096]{1,0:T(8,128)(2,1)S(1)}, u32[]{:S(2)}, u32[]{:S(2)}) collective-permute-start(bf16[12,4096]{1,0:T(8,128)(2,1)S(1)} %get-tuple-element.65), channel_id=1, source_target_pairs={{0,16},{1,17},{2,18},{3,19},{4,20},{5,21},{6,22},{7,23},{8,24},{9,... | collective-permute-start | bytes 294920 | tf_op jit(solution)/shard_map/ppermute | solution.py:39
  127.1 11.8 %collective-permute-start.26 = (bf16[12,4096]{1,0:T(8,128)(2,1)S(1)}, bf16[12,4096]{1,0:T(8,128)(2,1)S(1)}, u32[]{:S(2)}, u32[]{:S(2)}) collective-permute-start(bf16[12,4096]{1,0:T(8,128)(2,1)S(1)} %get-tuple-element.63), channel_id=1, source_target_pairs={{0,8},{1,9},{2,10},{3,11},{4,12},{5,13},{6,14},{7,15},{8,0},{9,1},... | collective-permute-start | bytes 294920 | tf_op jit(solution)/shard_map/ppermute | solution.py:39
  131.0 8.6 %collective-permute-start.32 = (bf16[32,4096]{1,0:T(8,128)(2,1)S(1)}, bf16[32,4096]{1,0:T(8,128)(2,1)S(1)}, u32[]{:S(2)}, u32[]{:S(2)}) collective-permute-start(bf16[32,4096]{1,0:T(8,128)(2,1)S(1)} %get-tuple-element.61), channel_id=1, source_target_pairs={{0,6},{1,7},{2,0},{3,1},{4,2},{5,3},{6,4},{7,5},{8,14},{9,15},{10,... | collective-permute-start | bytes 786440 | tf_op jit(solution)/shard_map/ppermute | solution.py:39
  132.2 12.4 %collective-permute-start.31 = (bf16[32,4096]{1,0:T(8,128)(2,1)S(1)}, bf16[32,4096]{1,0:T(8,128)(2,1)S(1)}, u32[]{:S(2)}, u32[]{:S(2)}) collective-permute-start(bf16[32,4096]{1,0:T(8,128)(2,1)S(1)} %get-tuple-element.62), channel_id=1, source_target_pairs={{0,4},{1,5},{2,6},{3,7},{4,0},{5,1},{6,2},{7,3},{8,12},{9,13},{10,... | collective-permute-start | bytes 786440 | tf_op jit(solution)/shard_map/ppermute | solution.py:39
  134.8 11.2 %collective-permute-start.30 = (bf16[32,4096]{1,0:T(8,128)(2,1)S(1)}, bf16[32,4096]{1,0:T(8,128)(2,1)S(1)}, u32[]{:S(2)}, u32[]{:S(2)}) collective-permute-start(bf16[32,4096]{1,0:T(8,128)(2,1)S(1)} %get-tuple-element.60), channel_id=1, source_target_pairs={{0,2},{1,3},{2,4},{3,5},{4,6},{5,7},{6,0},{7,1},{8,10},{9,11},{10,... | collective-permute-start | bytes 786440 | tf_op jit(solution)/shard_map/ppermute | solution.py:39
  139.2 12.4 %collective-permute-start.29 = (bf16[8,4096]{1,0:T(8,128)(2,1)S(1)}, bf16[8,4096]{1,0:T(8,128)(2,1)S(1)}, u32[]{:S(2)}, u32[]{:S(2)}) collective-permute-start(bf16[8,4096]{1,0:T(8,128)(2,1)S(1)} %slice.172), channel_id=1, source_target_pairs={{0,32},{1,33},{2,34},{3,35},{4,36},{5,37},{6,38},{7,39},{8,40},{9,... | collective-permute-start | bytes 196616 | tf_op jit(solution)/shard_map/ppermute | solution.py:39
  146.2 8.2 %collective-permute-start.39 = (bf16[4,4096]{1,0:T(4,128)(2,1)S(1)}, bf16[4,4096]{1,0:T(4,128)(2,1)S(1)}, u32[]{:S(2)}, u32[]{:S(2)}) collective-permute-start(bf16[4,4096]{1,0:T(4,128)(2,1)S(1)} %get-tuple-element.73), channel_id=1, source_target_pairs={{0,24},{1,25},{2,26},{3,27},{4,28},{5,29},{6,30},{7,31},{8,16},{9,... | collective-permute-start | bytes 98312 | tf_op jit(solution)/shard_map/ppermute | solution.py:39
  146.9 10.5 %collective-permute-start.38 = (bf16[4,4096]{1,0:T(4,128)(2,1)S(1)}, bf16[4,4096]{1,0:T(4,128)(2,1)S(1)}, u32[]{:S(2)}, u32[]{:S(2)}) collective-permute-start(bf16[4,4096]{1,0:T(4,128)(2,1)S(1)} %get-tuple-element.74), channel_id=1, source_target_pairs={{0,16},{1,17},{2,18},{3,19},{4,20},{5,21},{6,22},{7,23},{8,24},{9,... | collective-permute-start | bytes 98312 | tf_op jit(solution)/shard_map/ppermute | solution.py:39
  148.1 12.7 %collective-permute-start.37 = (bf16[4,4096]{1,0:T(4,128)(2,1)S(1)}, bf16[4,4096]{1,0:T(4,128)(2,1)S(1)}, u32[]{:S(2)}, u32[]{:S(2)}) collective-permute-start(bf16[4,4096]{1,0:T(4,128)(2,1)S(1)} %get-tuple-element.72), channel_id=1, source_target_pairs={{0,8},{1,9},{2,10},{3,11},{4,12},{5,13},{6,14},{7,15},{8,0},{9,1},... | collective-permute-start | bytes 98312 | tf_op jit(solution)/shard_map/ppermute | solution.py:39
  150.8 10.0 %collective-permute-start.36 = (bf16[4,4096]{1,0:T(4,128)(2,1)S(1)}, bf16[4,4096]{1,0:T(4,128)(2,1)S(1)}, u32[]{:S(2)}, u32[]{:S(2)}) collective-permute-start(bf16[4,4096]{1,0:T(4,128)(2,1)S(1)} %get-tuple-element.69), channel_id=1, source_target_pairs={{0,152},{1,153},{2,154},{3,155},{4,156},{5,157},{6,158},{7,159},{8... | collective-permute-start | bytes 98312 | tf_op jit(solution)/shard_map/ppermute | solution.py:39
  151.6 9.2 %collective-permute-start.35 = (bf16[4,4096]{1,0:T(4,128)(2,1)S(1)}, bf16[4,4096]{1,0:T(4,128)(2,1)S(1)}, u32[]{:S(2)}, u32[]{:S(2)}) collective-permute-start(bf16[4,4096]{1,0:T(4,128)(2,1)S(1)} %get-tuple-element.70), channel_id=1, source_target_pairs={{0,144},{1,145},{2,146},{3,147},{4,148},{5,149},{6,150},{7,151},{8... | collective-permute-start | bytes 98312 | tf_op jit(solution)/shard_map/ppermute | solution.py:39
  (17 other events, 186.4 us)
